TPU v7x, 32 devices: a whole 2x2x4 slice. The times are simulated.
32 devices in a mesh: dp: 16 (over z, x, core), tensor: 2 (over y).
Axes of the slice: x: 2, y: 2, z: 4, core: 2. Of those that a mesh axis runs over, the one named last changes fastest.
Arguments:
- tokens: bfloat16 [18944, 768], P('dp'), may hold values from -6 to 6
- w_qkv: bfloat16 [3, 768, 768], P(None, None, 'tensor'), may hold values from -0.21875 to 0.21875
- bias_qv: float32 [2, 768], P(None, 'tensor'), may hold values from -2 to 2
- w_out: bfloat16 [768, 768], P('tensor'), may hold values from -2.5 to 2.5
- bias_out: float32 [768], replicated, may hold values from -2 to 2
- gain_one: float32 [768], replicated, may hold values from 0.25 to 1.75
- shift_one: float32 [768], replicated, may hold values from -2 to 2
- w_up: bfloat16 [768, 3072], P(None, 'tensor'), may hold values from -0.21875 to 0.21875
- bias_up: float32 [3072], P('tensor'), may hold values from -2 to 2
- w_down: bfloat16 [3072, 768], P('tensor'), may hold values from -0.15625 to 0.15625
- bias_down: float32 [768], replicated, may hold values from -2 to 2
- gain_two: float32 [768], replicated, may hold values from 0.25 to 1.75
- shift_two: float32 [768], replicated, may hold values from -2 to 2
- grad_out: bfloat16 [18944, 768], P('dp'), may hold values from -6 to 6
- parent: int32 [128], P('dp'), may hold values from -1 to 126, as said below
- mem_slots: int32 [128, 10], P('dp'), may hold values from 0 to 147, as said below
Outputs:
- output: bfloat16 [18944, 768], P('dp')
- grad_tokens: bfloat16 [18944, 768], P('dp')
- grad_w_qkv: float32 [3, 768, 768], P(None, None, 'tensor')
- grad_bias_qv: float32 [2, 768], P(None, 'tensor')
- grad_w_out: float32 [768, 768], P('tensor')
- grad_bias_out: float32 [768], replicated
- grad_gain_one: float32 [768], replicated
- grad_shift_one: float32 [768], replicated
- grad_w_up: float32 [768, 3072], P(None, 'tensor')
- grad_bias_up: float32 [3072], P('tensor')
- grad_w_down: float32 [3072, 768], P('tensor')
- grad_bias_down: float32 [768], replicated
- grad_gain_two: float32 [768], replicated
- grad_shift_two: float32 [768], replicated
Inputs may be any that keep to these rules, and one draw needn't show every extreme that they name: `parent`: segments 8 * t to 8 * t + 7 form tree t; its first segment has -1, every other segment an earlier segment of the same tree, and its last segment the segment just before it. `mem_slots`: the 10 offsets of one segment are distinct.
All inputs are finite; a program needn't handle non-finite values.
Results may differ from a plain program's by a relative error of at most 0.014.
Values sent between devices are 32-bit elements; how exact they have to be, the bound alone decides.
A program may use at most 320 MiB of HBM per device.

v0:
```python
import jax
import jax.numpy as jnp
from jax import lax
from jax.sharding import PartitionSpec as P

HD = 64
SEG = 148


EPSILON = 1e-12
MASKED = -1e30


def normalize(values, gain, shift):
    average = jnp.mean(values, axis=-1, keepdims=True)
    centered = values - average
    variance = jnp.mean(centered * centered, axis=-1, keepdims=True)
    return centered * lax.rsqrt(variance + EPSILON) * gain + shift


def gelu_exact(values):
    return jax.nn.gelu(values, approximate=False)


def allowed_mask(local_parent, slot_ids):
    seg_count = local_parent.shape[0]
    seg_index = jnp.arange(seg_count, dtype=jnp.int32)
    ancestor = jnp.zeros((seg_count, seg_count), dtype=jnp.bool_)
    current = local_parent
    for hop in range(seg_count):
        matches = current[:, None] == seg_index[None, :]
        ancestor = jnp.logical_or(ancestor, matches)
        following = jnp.sum(jnp.where(matches, local_parent[None, :], 0), axis=1)
        current = jnp.where(jnp.any(matches, axis=1), following, -1)
    offsets = jnp.arange(SEG, dtype=jnp.int32)
    memory = jnp.any(slot_ids[:, :, None] == offsets[None, None, :], axis=1).reshape(
        seg_count * SEG
    )
    row_seg = jnp.arange(seg_count * SEG, dtype=jnp.int32) // SEG
    same_seg = row_seg[:, None] == row_seg[None, :]
    reach_all = jnp.repeat(jnp.repeat(ancestor, SEG, axis=0), SEG, axis=1)
    return jnp.logical_or(same_seg, jnp.logical_and(reach_all, memory[None, :]))


def head_scores(queries, key_rows, allowed, head_count):
    row_count = queries.shape[0]
    head_shape = (row_count, head_count, HD)
    scores = jnp.einsum(
        "qhd,khd->hqk",
        queries.reshape(head_shape),
        key_rows.reshape(head_shape),
        preferred_element_type=jnp.float32,
    ) * HD ** (-0.5)
    return jnp.where(allowed[None], scores, MASKED)


def attend(queries, key_rows, value_rows, allowed, head_count):
    row_count = queries.shape[0]
    scores = head_scores(queries, key_rows, allowed, head_count)
    row_max = jnp.max(scores, axis=-1, keepdims=True)
    raised = jnp.exp(scores - row_max)
    row_total = jnp.sum(raised, axis=-1, keepdims=True)
    chances = (raised / row_total).astype(jnp.bfloat16)
    mixed_heads = jnp.einsum(
        "hqk,khd->qhd",
        chances,
        value_rows.reshape(row_count, head_count, HD),
        preferred_element_type=jnp.float32,
    )
    return (
        mixed_heads.reshape(row_count, head_count * HD).astype(jnp.bfloat16),
        row_max + jnp.log(row_total),
    )


def attend_back(queries, key_rows, value_rows, log_total, d_mixed, allowed, head_count):
    row_count = queries.shape[0]
    head_shape = (row_count, head_count, HD)
    scale = HD ** (-0.5)
    scores = head_scores(queries, key_rows, allowed, head_count)
    chances = jnp.exp(scores - log_total)
    chances_low = chances.astype(jnp.bfloat16)
    mixed_grad = d_mixed.reshape(head_shape)
    d_chances = jnp.einsum(
        "qhd,khd->hqk",
        mixed_grad,
        value_rows.reshape(head_shape),
        preferred_element_type=jnp.float32,
    )
    row_inner = jnp.sum(chances * d_chances, axis=-1, keepdims=True)
    d_scores = (chances * (d_chances - row_inner)).astype(jnp.bfloat16)
    d_queries = (
        jnp.einsum(
            "hqk,khd->qhd",
            d_scores,
            key_rows.reshape(head_shape),
            preferred_element_type=jnp.float32,
        )
        * scale
    )
    d_keys = (
        jnp.einsum(
            "hqk,qhd->khd",
            d_scores,
            queries.reshape(head_shape),
            preferred_element_type=jnp.float32,
        )
        * scale
    )
    d_values = jnp.einsum(
        "hqk,qhd->khd", chances_low, mixed_grad, preferred_element_type=jnp.float32
    )
    flat_shape = (row_count, head_count * HD)
    return (
        d_queries.reshape(flat_shape).astype(jnp.bfloat16),
        d_keys.reshape(flat_shape).astype(jnp.bfloat16),
        d_values.reshape(flat_shape).astype(jnp.bfloat16),
    )


def forward_pass(tokens, weights, allowed, again):
    (
        w_qkv,
        bias_qv,
        w_out,
        bias_out,
        gain_one,
        shift_one,
        w_up,
        bias_up,
        w_down,
        bias_down,
        gain_two,
        shift_two,
    ) = weights
    head_count = w_out.shape[0] // HD
    projected = jnp.einsum("td,cde->cte", tokens, w_qkv, preferred_element_type=jnp.float32)
    queries = (projected[0] + bias_qv[0]).astype(jnp.bfloat16)
    key_rows = projected[1].astype(jnp.bfloat16)
    value_rows = (projected[2] + bias_qv[1]).astype(jnp.bfloat16)
    mixed_heads, log_total = attend(queries, key_rows, value_rows, allowed, head_count)
    partial_attn = jnp.dot(mixed_heads, w_out, preferred_element_type=jnp.float32)
    if again:
        attended = lax.psum(partial_attn, "tensor")
    else:
        attended = lax.psum(partial_attn, "tensor")
    resid_one = tokens.astype(jnp.float32) + (attended + bias_out)
    hidden = normalize(resid_one, gain_one, shift_one)
    hidden_low = hidden.astype(jnp.bfloat16)
    inner_pre = jnp.dot(hidden_low, w_up, preferred_element_type=jnp.float32) + bias_up
    acted = gelu_exact(inner_pre).astype(jnp.bfloat16)
    partial_ffn = jnp.dot(acted, w_down, preferred_element_type=jnp.float32)
    if again:
        ffn_summed = lax.psum(partial_ffn, "tensor")
    else:
        ffn_summed = lax.psum(partial_ffn, "tensor")
    resid_two = hidden + (ffn_summed + bias_down)
    output = normalize(resid_two, gain_two, shift_two)
    saved = (
        queries,
        key_rows,
        value_rows,
        log_total,
        mixed_heads,
        resid_one,
        hidden_low,
        inner_pre,
        acted,
        resid_two,
    )
    return (output, saved)


def shards(
    tokens,
    w_qkv,
    bias_qv,
    w_out,
    bias_out,
    gain_one,
    shift_one,
    w_up,
    bias_up,
    w_down,
    bias_down,
    gain_two,
    shift_two,
    grad_out,
    parent,
    mem_slots,
):
    seg_count = parent.shape[0]
    local_parent = parent - lax.axis_index("dp") * seg_count
    allowed = allowed_mask(local_parent, mem_slots)
    weights = (
        w_qkv,
        bias_qv,
        w_out,
        bias_out,
        gain_one,
        shift_one,
        w_up,
        bias_up,
        w_down,
        bias_down,
        gain_two,
        shift_two,
    )
    output, saved = forward_pass(tokens, weights, allowed, False)
    unused_out, saved = forward_pass(tokens, weights, allowed, True)
    (
        queries,
        key_rows,
        value_rows,
        log_total,
        mixed_heads,
        resid_one,
        hidden_low,
        inner_pre,
        acted,
        resid_two,
    ) = saved
    head_count = w_out.shape[0] // HD
    cotangent = grad_out.astype(jnp.float32)
    ignored, pull_two = jax.vjp(normalize, resid_two, gain_two, shift_two)
    d_two, d_gain_two, d_shift_two = pull_two(cotangent)
    d_ffn = d_two.astype(jnp.bfloat16)
    d_w_down = jnp.einsum("tf,td->fd", acted, d_ffn, preferred_element_type=jnp.float32)
    d_bias_down = jnp.sum(d_ffn.astype(jnp.float32), axis=0)
    d_acted = jnp.einsum("td,fd->tf", d_ffn, w_down, preferred_element_type=jnp.float32)
    ignored, pull_gelu = jax.vjp(gelu_exact, inner_pre)
    d_inner = pull_gelu(d_acted)[0].astype(jnp.bfloat16)
    d_w_up = jnp.einsum("td,tf->df", hidden_low, d_inner, preferred_element_type=jnp.float32)
    d_bias_up = jnp.sum(d_inner.astype(jnp.float32), axis=0)
    hidden_part = jnp.einsum("tf,df->td", d_inner, w_up, preferred_element_type=jnp.float32)
    d_hidden = lax.psum(hidden_part, "tensor") + d_two
    ignored, pull_one = jax.vjp(normalize, resid_one, gain_one, shift_one)
    d_one, d_gain_one, d_shift_one = pull_one(d_hidden)
    d_attn = d_one.astype(jnp.bfloat16)
    d_w_out = jnp.einsum("te,td->ed", mixed_heads, d_attn, preferred_element_type=jnp.float32)
    d_bias_out = jnp.sum(d_attn.astype(jnp.float32), axis=0)
    d_mixed = jnp.einsum("td,ed->te", d_attn, w_out, preferred_element_type=jnp.float32).astype(
        jnp.bfloat16
    )
    d_queries, d_keys, d_values = attend_back(
        queries, key_rows, value_rows, log_total, d_mixed, allowed, head_count
    )
    d_stacked = jnp.stack([d_queries, d_keys, d_values])
    d_w_qkv = jnp.einsum("td,cte->cde", tokens, d_stacked, preferred_element_type=jnp.float32)
    d_bias_flat = jnp.concatenate(
        [
            jnp.sum(d_queries.astype(jnp.float32), axis=0),
            jnp.sum(d_values.astype(jnp.float32), axis=0),
        ]
    )
    input_part = jnp.einsum("cte,cde->td", d_stacked, w_qkv, preferred_element_type=jnp.float32)
    grad_tokens = (lax.psum(input_part, "tensor") + d_one).astype(jnp.bfloat16)
    shared = (
        lax.psum_scatter(d_w_qkv, "dp", scatter_dimension=1, tiled=True),
        lax.psum_scatter(d_bias_flat, "dp", scatter_dimension=0, tiled=True),
        lax.psum_scatter(d_w_out, "dp", scatter_dimension=1, tiled=True),
        lax.psum_scatter(d_bias_out, "dp", scatter_dimension=0, tiled=True),
        lax.psum_scatter(d_gain_one, "dp", scatter_dimension=0, tiled=True),
        lax.psum_scatter(d_shift_one, "dp", scatter_dimension=0, tiled=True),
        lax.psum_scatter(d_w_up, "dp", scatter_dimension=0, tiled=True),
        lax.psum_scatter(d_bias_up, "dp", scatter_dimension=0, tiled=True),
        lax.psum_scatter(d_w_down, "dp", scatter_dimension=1, tiled=True),
        lax.psum_scatter(d_bias_down, "dp", scatter_dimension=0, tiled=True),
        lax.psum_scatter(d_gain_two, "dp", scatter_dimension=0, tiled=True),
        lax.psum_scatter(d_shift_two, "dp", scatter_dimension=0, tiled=True),
    )
    all_grads = tuple(
        (
            lax.all_gather(shared[0], "dp", axis=1, tiled=True),
            lax.all_gather(shared[1], "dp", axis=0, tiled=True),
            lax.all_gather(shared[2], "dp", axis=1, tiled=True),
            lax.all_gather(shared[3], "dp", axis=0, tiled=True),
            lax.all_gather(shared[4], "dp", axis=0, tiled=True),
            lax.all_gather(shared[5], "dp", axis=0, tiled=True),
            lax.all_gather(shared[6], "dp", axis=0, tiled=True),
            lax.all_gather(shared[7], "dp", axis=0, tiled=True),
            lax.all_gather(shared[8], "dp", axis=1, tiled=True),
            lax.all_gather(shared[9], "dp", axis=0, tiled=True),
            lax.all_gather(shared[10], "dp", axis=0, tiled=True),
            lax.all_gather(shared[11], "dp", axis=0, tiled=True),
        )
    )
    grad_bias_qv = all_grads[1].reshape(2, all_grads[1].shape[0] // 2)
    return (
        output.astype(jnp.bfloat16),
        grad_tokens,
        all_grads[0],
        grad_bias_qv,
        all_grads[2],
        all_grads[3],
        all_grads[4],
        all_grads[5],
        all_grads[6],
        all_grads[7],
        all_grads[8],
        all_grads[9],
        all_grads[10],
        all_grads[11],
    )


def solution(mesh):
    placed = (
        P("dp", None),
        P(None, None, "tensor"),
        P(None, "tensor"),
        P("tensor", None),
        P(),
        P(),
        P(),
        P(None, "tensor"),
        P("tensor"),
        P("tensor", None),
        P(),
        P(),
        P(),
        P("dp", None),
        P("dp"),
        P("dp", None),
    )
    return jax.shard_map(
        shards,
        mesh=mesh,
        in_specs=placed,
        out_specs=(
            P("dp", None),
            P("dp", None),
            P(None, None, "tensor"),
            P(None, "tensor"),
            P("tensor", None),
            P(),
            P(),
            P(),
            P(None, "tensor"),
            P("tensor"),
            P("tensor", None),
            P(),
            P(),
            P(),
        ),
        check_vma=False,
    )
```

profile of v0, /device:TPU:0, one launch (start us, length us, event | category | flops | bytes accessed | tf_op | source)
XLA Modules:
  0.0 1150.2 jit_solution(700404143986913243)
XLA Ops:
  8.9 4.6 convolution_bitcast_fusion
  13.4 1.0 slice.32
  14.5 2.1 fusion.57
  17.2 1.5 broadcast_in_dim.82
  18.7 4.4 reshape.300
  23.2 1.6 copy.78
  24.7 3.2 copy.75
  27.9 2.8 copy.77
  30.8 2.9 and_or_fusion
  33.7 15.2 %fusion.59 = (f32[6,1184]{1,0:T(8,128)S(1)}, f32[6,1184,1184]{1,2,0:T(8,128)}) fusion(bf16[1184,6,64]{0,2,1:T(8,128)(2,1)S(1)} %bitcast.62, f32[1184,6,64]{0,2,1:T(8,128)S(1)} %bitcast.59, f32[6,64]{1,0:T(8,128)S(1)} %add.177, pred[1184,1184]{0,1:T(8,128)(4,1)S(1)} %and_or_fusion), kind=kOutput, calls=%fused_computation.153 | convolution fusion | flops 1102760960 | bytes 37804288 | tf_op jit(solution)/shard_map/qhd,khd->hqk/dot_general | solution.py:48
  48.9 14.5 %fusion.1 = f32[6,1184]{1,0:T(8,128)S(1)} fusion(f32[6,1184,1184]{1,2,0:T(8,128)} %get-tuple-element.117, f32[6,1184]{1,0:T(8,128)S(1)} %get-tuple-element.116), kind=kLoop, calls=%fused_computation.7 | loop fusion | flops 16815168 | bytes 33701376 | tf_op jit(solution)/shard_map/reduce_sum | solution.py:62
  63.4 15.1 %fusion.23 = bf16[6,64,1184]{2,1,0:T(8,128)(2,1)S(1)} fusion(f32[6,1184,1184]{1,2,0:T(8,128)} %get-tuple-element.117, f32[6,1184]{1,0:T(8,128)S(1)} %fusion.1, f32[6,1184]{1,0:T(8,128)S(1)} %get-tuple-element.116, f32[1184,6,64]{0,2,1:T(8,128)} %bitcast.64, f32[6,64]{1,0:T(8,128)S(1)} %add.174), kind=kOutput, calls=%fused_computation.64 | convolution fusion | flops 1103222784 | bytes 36430848 | tf_op jit(solution)/shard_map/hqk,khd->qhd/dot_general | solution.py:64
  78.5 4.0 fusion.60
  82.6 99.3 %all-reduce.25.cloned.1.call-done = f32[1184,768]{1,0:T(8,128)} async-done(((f32[1184,768]{1,0:T(8,128)}), f32[1184,768]{1,0:T(8,128)}) %all-reduce.25.cloned.1.call-update) | async-done | bytes 3637264 | tf_op jit(solution)/shard_map/psum | solution.py:146
  181.9 3.1 fusion.56
  185.9 20.6 %multiply_convert_fusion.1 = (bf16[1184,1536]{1,0:T(8,128)(2,1)S(1)}, f32[1184,1536]{1,0:T(8,128)}, f32[1184,1536]{1,0:T(8,128)}) fusion(f32[1536]{0:T(1024)S(1)} %copy-done.28, bf16[768,1536]{1,0:T(8,128)(2,1)S(1)} %copy-done, f32[1184,768]{1,0:T(8,128)S(1)} %get-tuple-element.110, f32[768]{0:T(1024)S(1)} %copy-done.21, f32[768]{0:T(1024)S(1)} %copy-done.15, ...), kind=kOutput, calls=%fused_computation.17 | convolution fusion | flops 2917982208 | bytes 24204544 | tf_op jit(solution)/shard_map/dot_general | solution.py:150
  206.5 1.8 copy-done.30
  208.2 4.8 fusion.61
  213.1 96.6 %all-reduce.27.cloned.1.call-done = f32[1184,768]{1,0:T(8,128)} async-done(((f32[1184,768]{1,0:T(8,128)}), f32[1184,768]{1,0:T(8,128)}) %all-reduce.27.cloned.1.call-update) | async-done | bytes 3637264 | tf_op jit(solution)/shard_map/psum | solution.py:156
  309.7 4.4 fusion.54
  314.8 0.9 copy-done.8
  315.6 2.0 fusion.16
  317.6 3.1 fusion.53
  320.8 1.9 copy-done.4
  323.9 5.1 convert_reduce_fusion
  329.0 1.8 copy-done.29
  330.8 4.8 fusion.62
  335.7 96.6 %all-reduce.29.cloned.1.call-done = f32[1184,768]{1,0:T(8,128)} async-done(((f32[1184,768]{1,0:T(8,128)}), f32[1184,768]{1,0:T(8,128)}) %all-reduce.29.cloned.1.call-update) | async-done | bytes 3637264 | tf_op jit(solution)/shard_map/psum | solution.py:236
  432.3 5.8 multiply_reduce_fusion.1
  438.2 1.7 fusion.52
  439.9 1.8 copy-done.3
  442.1 1.2 copy-done.11
  443.3 2.2 fusion.63
  445.5 3.7 convolution_convert_fusion
  449.2 1.6 copy.80
  450.8 15.4 %convert_reduce_fusion.4 = (f32[6,64]{1,0:T(8,128)S(1)}, bf16[6,64,1184]{2,1,0:T(8,128)(2,1)}) fusion(bf16[1184,6,64]{0,2,1:T(8,128)(2,1)S(1)} %bitcast.60, f32[6,1184,1184]{1,2,0:T(8,128)} %get-tuple-element.117, f32[6,1184]{1,0:T(8,128)S(1)} %log_add_fusion), kind=kOutput, calls=%fused_computation.67 | convolution fusion | flops 1094811264 | bytes 35493120 | tf_op jit(solution)/shard_map/hqk,qhd->khd/dot_general | solution.py:110
  466.1 28.5 %multiply_reduce_fusion = (f32[6,1184]{1,0:T(8,128)S(1)}, f32[6,1184,1184]{1,2,0:T(8,128)}) fusion(f32[6,1184,1184]{1,2,0:T(8,128)} %get-tuple-element.117, f32[6,1184]{1,0:T(8,128)S(1)} %log_add_fusion, bf16[1184,6,64]{0,2,1:T(8,128)(2,1)S(1)} %bitcast.61, f32[1184,6,64]{0,2,1:T(8,128)} %bitcast.65, f32[6,64]{1,0:T(8,128)S(1)} %add.174), kind=kOutput, calls=%fused_computation.3 | convolution fusion | flops 1102760960 | bytes 70075392 | tf_op jit(solution)/shard_map/qhd,khd->hqk/dot_general | solution.py:84
  494.7 2.4 copy.86
  497.1 30.6 %multiply_convert_fusion = bf16[6,1184,1184]{1,2,0:T(8,128)(2,1)} fusion(f32[6,1184,1184]{1,2,0:T(8,128)} %get-tuple-element.120, f32[6,1184,1184]{1,2,0:T(8,128)} %get-tuple-element.117, f32[6,1184]{1,0:T(8,128)S(1)} %get-tuple-element.119, f32[6,1184]{1,0:T(8,128)S(1)} %log_add_fusion), kind=kLoop, calls=%fused_computation.2 | loop fusion | flops 33644544 | bytes 84168192 | tf_op jit(solution)/shard_map/convert_element_type | solution.py:91
  527.7 10.5 convert_reduce_fusion.5
  538.2 2.2 copy.84
  540.4 10.4 fusion.19
  550.8 1.3 copy.85
  552.1 6.7 convolution_bitcast_fusion.2
  558.8 6.2 copy.87
  565.1 8.0 fusion.64
  573.4 9.0 fusion.49
  582.4 1.1 copy-done.12
  583.6 6.5 convolution_bitcast_fusion.1
  592.1 90.2 %all-reduce.33.cloned.1.call-done = f32[3,768,384]{2,0,1:T(4,128)} async-done(((f32[3,768,384]{2,0,1:T(4,128)}), f32[3,768,384]{2,0,1:T(4,128)}) %all-reduce.33.cloned.1.call-update) | async-done | bytes 3538960
  682.3 1.0 constant_dynamic-slice_fusion
  684.1 77.2 %reduce-scatter.8.cloned.1.call-done = f32[1536,48]{0,1:T(8,128)} async-done(((f32[1536,768]{0,1:T(8,128)}), f32[1536,48]{0,1:T(8,128)}) %reduce-scatter.8.cloned.1.call-update) | async-done | bytes 294928 | tf_op jit(solution)/shard_map/reduce_scatter | solution.py:267
  761.4 79.4 %reduce-scatter.6.cloned.1.call-done = f32[48,1536]{1,0:T(8,128)} async-done(((f32[768,1536]{1,0:T(8,128)}), f32[48,1536]{1,0:T(8,128)}) %reduce-scatter.6.cloned.1.call-update) | async-done | bytes 294928 | tf_op jit(solution)/shard_map/reduce_scatter | solution.py:265
  843.0 58.1 %all-reduce.18 = (f32[768]{0:T(1024)S(1)}, f32[768]{0:T(1024)S(1)}, f32[768]{0:T(1024)S(1)}, f32[768]{0:T(1024)S(1)}, f32[1536]{0:T(1024)S(1)}, /*index=5*/f32[7...) all-reduce(f32[768]{0:T(1024)S(1)} %pad_maximum_fusion.3, ...), channel_id=3, replica_groups=mesh['dp'=16,'tensor'=2] {'dp'}, use_global_device_ids=true, to_apply=%region_33.34.clone | all-reduce | flops 6912 | bytes 55296
  902.3 58.4 %all-reduce.17 = (f32[768]{0:T(1024)S(1)}, f32[768]{0:T(1024)}, f32[768]{0:T(1024)}, f32[768]{0:T(1024)}, f32[1536]{0:T(1024)}, /*index=5*/f32[768]{0:T(1024)}, f32[768]{0:T(1024)}, f32[768]{0:T(1024)}) all-reduce(f32[768]{0:T(1024)S(1)} %dynamic-slice_dynamic-update-slice_fusion.7, ...), channel_id=1, replica_groups=mesh['dp'=16,'tensor'=2] {'dp'}, use_global_device_ids=true, to_apply=%add | all-reduce | flops 6912 | bytes 55296
  961.3 4.7 add_convert_fusion.1
  966.0 13.3 %all-gather.7.cloned.1.call-done = f32[384,768]{0,1:T(8,128)} async-done(((f32[384,48]{0,1:T(8,128)}), f32[384,768]{0,1:T(8,128)}) %all-gather.7.cloned.1.call-update) | async-done | bytes 1179664 | tf_op jit(solution)/shard_map/all_gather | solution.py:276
  979.4 2.7 copy.89
  982.0 46.3 %all-gather.5.cloned.1.call-done = f32[3,768,384]{2,1,0:T(8,128)} async-done(((f32[3,48,384]{2,1,0:T(8,128)}), f32[3,768,384]{2,1,0:T(8,128)}) %all-gather.5.cloned.1.call-update) | async-done | bytes 3538960 | tf_op jit(solution)/shard_map/all_gather | solution.py:274
  1028.3 54.5 %all-gather.11.cloned.1.call-done = f32[1536,768]{0,1:T(8,128)} async-done(((f32[1536,48]{0,1:T(8,128)}), f32[1536,768]{0,1:T(8,128)}) %all-gather.11.cloned.1.call-update) | async-done | bytes 4718608 | tf_op jit(solution)/shard_map/all_gather | solution.py:282
  1082.8 6.0 copy.90
  1088.9 47.9 %all-gather.9.cloned.1.call-done = f32[768,1536]{1,0:T(8,128)} async-done(((f32[48,1536]{1,0:T(8,128)}), f32[768,1536]{1,0:T(8,128)}) %all-gather.9.cloned.1.call-update) | async-done | bytes 4718608 | tf_op jit(solution)/shard_map/all_gather | solution.py:280
  1136.8 4.2 copy.110
  1141.0 2.2 copy.111
  (158 shorter events, 10.3 us)
Async XLA Ops:
  7.2 178.5 %copy-start = (bf16[768,1536]{1,0:T(8,128)(2,1)S(1)}, bf16[768,1536]{1,0:T(8,128)(2,1)}, u32[]{:S(2)}) copy-start(bf16[768,1536]{1,0:T(8,128)(2,1)} %param.23) | copy-start | bytes 7077892
  7.2 174.7 %all-reduce.25.cloned.1.call-start = ((), (), s32[]{:S(2)}) async-start(), calls=%async_computation.3 | async-start | bytes 7274496 | tf_op jit(solution)/shard_map/psum | solution.py:146
  14.5 2.1 copy-start.24
  14.5 2.3 copy-start.23
  16.7 17.0 %copy-start.13 = (f32[6,64]{1,0:T(8,128)}, f32[6,64]{1,0:T(8,128)S(1)}, u32[]{:S(2)}) copy-start(f32[6,64]{1,0:T(8,128)S(1)} %add.177) | copy-start | bytes 4612
  24.7 9.0 copy-start.6
  30.8 3.0 copy-start.5
  82.6 99.4 %copy-start.19 = (f32[768]{0:T(1024)S(1)}, f32[768]{0:T(1024)}, u32[]{:S(2)}) copy-start(f32[768]{0:T(1024)} %param.20) | copy-start | bytes 9220
  82.6 227.1 %all-reduce.27.cloned.1.call-start = ((), (), s32[]{:S(2)}) async-start(), calls=%async_computation.4 | async-start | bytes 7274496 | tf_op jit(solution)/shard_map/psum | solution.py:156
  185.1 21.4 %copy-start.1 = (f32[1184,768]{1,0:T(8,128)}, f32[1184,768]{1,0:T(8,128)S(1)}, u32[]{:S(2)}) copy-start(f32[1184,768]{1,0:T(8,128)S(1)} %get-tuple-element.110) | copy-start | bytes 10911748
  185.1 0.7 copy-start.15
  185.1 0.7 copy-start.21
  185.1 0.8 copy-start.28
  185.9 22.3 %copy-start.26 = (bf16[1536,768]{1,0:T(8,128)(2,1)S(1)}, bf16[1536,768]{1,0:T(8,128)(2,1)}, u32[]{:S(2)}) copy-start(bf16[1536,768]{1,0:T(8,128)(2,1)} %param.25) | copy-start | bytes 7077892
  206.4 1.8 copy-start.30
  213.0 96.7 %copy-start.20 = (f32[768]{0:T(1024)S(1)}, f32[768]{0:T(1024)}, u32[]{:S(2)}) copy-start(f32[768]{0:T(1024)} %param.26) | copy-start | bytes 9220
  213.1 219.3 %all-reduce.29.cloned.1.call-start = ((), (), s32[]{:S(2)}) async-start(), calls=%async_computation.5 | async-start | bytes 7274496 | tf_op jit(solution)/shard_map/psum | solution.py:236
  309.7 13.3 %slice-start.2 = ((s8[7274496]{0:T(1024)(128)(4,1)}), s8[4194304]{0:T(1024)(128)(4,1)S(1)}, s32[]{:S(2)}) async-start(s8[7274496]{0:T(1024)(128)(4,1)} %bitcast.73), calls=%async_computation.17 | async-start | bytes 8388608
  314.1 1.5 copy-start.8
  314.1 1.5 copy-start.16
  314.7 2.9 copy-start.22
  315.6 7.4 slice-start.3
  317.6 5.4 slice-start
  317.6 5.4 slice-start.1
  320.8 1.9 copy-start.4
  320.8 3.1 copy-start.27
  323.0 6.0 copy-start.10
  329.0 1.8 copy-start.29
  335.7 254.5 %reduce-scatter.4.cloned.1.call-start = ((), (), s32[]{:S(2)}) async-start(), calls=%async_computation.8 | async-start | bytes 1253376 | tf_op jit(solution)/shard_map/reduce_scatter | solution.py:261
  432.3 5.9 copy-start.2
  439.9 1.8 copy-start.3
  442.1 1.2 copy-start.11
  494.7 187.6 %all-reduce.33.cloned.1.call-start = ((), (), s32[]{:S(2)}) async-start(), calls=%async_computation.14 | async-start | bytes 9437184
  497.1 30.6 %copy-start.7 = (bf16[1,1184,384]{1,2,0:T(8,128)(2,1)S(1)}, bf16[1,1184,384]{1,2,0:T(8,128)(2,1)}, u32[]{:S(2)}) copy-start(bf16[1,1184,384]{1,2,0:T(8,128)(2,1)} %copy-done.6) | copy-start | bytes 2727940
  527.7 12.7 %copy-start.14 = (f32[6,64]{1,0:T(8,128)S(1)}, f32[6,64]{1,0:T(8,128)}, u32[]{:S(2)}) copy-start(f32[6,64]{1,0:T(8,128)} %copy-done.13) | copy-start | bytes 4612
  565.0 196.3 %reduce-scatter.8.cloned.1.call-start = ((), (), s32[]{:S(2)}) async-start(), calls=%async_computation.12 | async-start | bytes 5013504 | tf_op jit(solution)/shard_map/reduce_scatter | solution.py:267
  573.1 267.7 %reduce-scatter.6.cloned.1.call-start = ((), (), s32[]{:S(2)}) async-start(), calls=%async_computation.10 | async-start | bytes 5013504 | tf_op jit(solution)/shard_map/reduce_scatter | solution.py:265
  582.4 1.2 copy-start.12
  582.4 378.9 %all-reduce.31.cloned.1.call-start = ((), (), s32[]{:S(2)}) async-start(), calls=%async_computation.6 | async-start | bytes 7274496 | tf_op jit(solution)/shard_map/psum | solution.py:257
  590.0 0.8 copy-start.25
  590.0 252.9 %copy-start.17 = (f32[768]{0:T(1024)S(1)}, f32[768]{0:T(1024)}, u32[]{:S(2)}) copy-start(f32[768]{0:T(1024)} %get-tuple-element.72) | copy-start | bytes 9220
  590.0 252.9 %copy-start.18 = (f32[768]{0:T(1024)S(1)}, f32[768]{0:T(1024)}, u32[]{:S(2)}) copy-start(f32[768]{0:T(1024)} %get-tuple-element.75) | copy-start | bytes 9220
  590.1 389.3 %all-gather.7.cloned.1.call-start = ((), (), s32[]{:S(2)}) async-start(), calls=%async_computation.9 | async-start | bytes 1253376 | tf_op jit(solution)/shard_map/all_gather | solution.py:276
  590.8 437.5 %all-gather.5.cloned.1.call-start = ((), (), s32[]{:S(2)}) async-start(), calls=%async_computation.7 | async-start | bytes 3760128 | tf_op jit(solution)/shard_map/all_gather | solution.py:274
  684.0 398.8 %all-gather.11.cloned.1.call-start = ((), (), s32[]{:S(2)}) async-start(), calls=%async_computation.13 | async-start | bytes 5013504 | tf_op jit(solution)/shard_map/all_gather | solution.py:282
  761.3 375.4 %all-gather.9.cloned.1.call-start = ((), (), s32[]{:S(2)}) async-start(), calls=%async_computation.11 | async-start | bytes 5013504 | tf_op jit(solution)/shard_map/all_gather | solution.py:280
  1136.8 4.2 copy-start.9
Sparse Core Ops, SparseCore 0:
  82.7 99.1 all-reduce.24
  213.2 96.4 all-reduce.26
  335.8 96.4 all-reduce.28
  494.8 57.9 reduce-scatter.3
  565.2 117.0 all-reduce.32
  686.0 75.2 reduce-scatter.7
  766.2 74.5 reduce-scatter.5
  843.1 95.5 all-reduce.30
  941.0 38.2 all-gather.6
  982.1 46.1 all-gather.4
  1030.6 52.2 all-gather.10
  1085.0 51.7 all-gather.8
where the time goes:
time: 1150 us
  waiting for transfers between devices  702 us (61%)
  matrix products  175 us (15%)
  blocking collectives  116 us (10%)
  other arithmetic  76.5 us (7%)
  local copies, waits for them, and re-layouts  61.8 us (5%)
  between operations  17.5 us (2%)
    unnamed x2, blocking collectives  116 us
    psum x1, waiting for transfers between devices, forward_pass(): attended = lax.psum(partial_attn, 'tensor')  99.3 us
    psum x1, waiting for transfers between devices, forward_pass(): ffn_summed = lax.psum(partial_ffn, 'tensor')  96.6 us
    psum x1, waiting for transfers between devices, shards(): d_hidden = lax.psum(hidden_part, 'tensor') + d_two  96.6 us
    unnamed x13, waiting for transfers between devices  91 us
    reduce_scatter x1, waiting for transfers between devices, shards(): lax.psum_scatter(d_w_up, 'dp', scatter_dimension=0, tiled=True)  79.4 us
    reduce_scatter x1, waiting for transfers between devices, shards(): lax.psum_scatter(d_w_down, 'dp', scatter_dimension=1, tiled=True)  77.2 us
    all_gather x1, waiting for transfers between devices, shards(): lax.all_gather(shared[8], 'dp', axis=1, tiled=True)  54.5 us
  transfers between devices with their start and end apart: 12, of which 10 were waited for; matrix products, arithmetic and copies ran while one was open for 10% of the time, Pallas kernels for 0%

commit v1 on v0

v1 whole, which is shorter than its diff:
```python
import functools


import jax
import jax.numpy as jnp
from jax import lax
from jax.experimental import pallas as pl
from jax.experimental.pallas import tpu as pltpu
from jax.sharding import PartitionSpec as P


MESH = pl.DeviceIdType.MESH
BR, BC = 128, 384
SPREAD = 2
SLOTS = 16


class Place:
    def __init__(self):
        me = lax.axis_index("dp")
        self.core = lax.rem(me, 2)
        self.x = lax.rem(me // 2, 2)
        self.z = me // 4
        self.sib = me + 1 - 2 * self.core
        self.xn = me + 2 - 4 * self.x
        self.zp = me + 4 - 8 * lax.rem(self.z, 2)
        self.zm = me + 4 * (3 - 2 * self.z)
        self.end = (self.z == 0) | (self.z == 3)
        self.mid = (self.z == 1) | (self.z == 2)


def sum_barrier(pos):
    barrier = pltpu.get_barrier_semaphore()

    def greet(dev):
        pl.semaphore_signal(barrier, inc=1, device_id={"dp": dev}, device_id_type=MESH)

    greet(pos.sib)
    greet(pos.xn)
    greet(pos.zp)

    @pl.when(pos.mid)
    def _():
        greet(pos.zm)

    pl.semaphore_wait(barrier, jnp.where(pos.mid, 4, 3))


def make_tick(pos, grads, from_core, from_one, from_two, from_three, sent, got, credit, count, finish):
    half = BR // 2
    quarter = BR // 4

    def copy(stage, block, source, target, device):
        slot = lax.rem(block, SLOTS)
        return pltpu.make_async_remote_copy(
            src_ref=source,
            dst_ref=target,
            send_sem=sent.at[stage, slot],
            recv_sem=got.at[stage, slot],
            device_id={"dp": device},
            device_id_type=MESH,
        )

    def rows(block, start, size):
        return grads.at[block, pl.ds(pl.multiple_of(start, quarter), size)]

    def add(block, start, size, landed):
        where = pl.ds(pl.multiple_of(start, quarter), size)
        grads[block, where] = grads[block, where] + landed[...]

    def free(index, device):
        pl.semaphore_signal(credit.at[index], inc=1, device_id={"dp": device}, device_id_type=MESH)

    def claim(index):
        pl.semaphore_wait(credit.at[index], 1)

    x_first = pos.core == 0
    z_first = pos.core == 1
    mine = pos.core * half
    xrow = pos.x * quarter
    xrow_other = (1 - pos.x) * quarter
    far = lax.rem(pos.z, 2) == 0
    keep = half + jnp.where(far, quarter, 0)
    give = half + jnp.where(far, 0, quarter)

    def core_out(block):
        return copy(0, block, rows(block, (1 - pos.core) * half, half), from_core.at[lax.rem(block, SLOTS)], pos.sib)

    def x_one(block):
        return copy(1, block, rows(block, xrow_other, quarter), from_one.at[lax.rem(block, SLOTS), pl.ds(0, quarter)], pos.xn)

    def z_one(block):
        return copy(1, block, rows(block, half, half), from_one.at[lax.rem(block, SLOTS)], pos.zp)

    def x_two(block):
        return copy(2, block, rows(block, xrow, quarter), from_two.at[lax.rem(block, SLOTS)], pos.zp)

    def z_two(block):
        return copy(2, block, rows(block, give, quarter), from_two.at[lax.rem(block, SLOTS)], pos.zm)

    def x_three(block):
        return copy(3, block, rows(block, xrow, quarter), from_three.at[lax.rem(block, SLOTS)], pos.zm)

    def z_three(block):
        return copy(3, block, rows(block, keep, quarter), from_three.at[lax.rem(block, SLOTS)], pos.xn)

    def x_four(block):
        return copy(4, block, rows(block, xrow, quarter), rows(block, xrow, quarter), pos.zp)

    def z_four(block):
        return copy(4, block, rows(block, keep, quarter), rows(block, keep, quarter), pos.zm)

    def z_four_in(block):
        return copy(4, block, rows(block, give, quarter), rows(block, give, quarter), pos.zm)

    def x_five(block):
        return copy(5, block, rows(block, xrow, quarter), rows(block, xrow, quarter), pos.xn)

    def x_five_in(block):
        return copy(5, block, rows(block, xrow_other, quarter), rows(block, xrow_other, quarter), pos.xn)

    def z_five(block):
        return copy(5, block, rows(block, half, half), rows(block, half, half), pos.zp)

    def core_six(block):
        return copy(6, block, rows(block, mine, half), rows(block, mine, half), pos.sib)

    def core_six_in(block):
        return copy(6, block, rows(block, (1 - pos.core) * half, half), rows(block, (1 - pos.core) * half, half), pos.sib)

    def stage_zero(block):
        core_out(block).start()

    def stage_one(block):
        core_out(block).wait()
        free(2, pos.sib)
        add(block, mine, half, from_core.at[lax.rem(block, SLOTS)])

        @pl.when(x_first)
        def _():
            x_one(block).start()

        @pl.when(z_first & pos.end)
        def _():
            z_one(block).start()

    def stage_two(block):
        @pl.when(x_first)
        def _():
            x_one(block).wait()
            free(1, pos.xn)
            add(block, xrow, quarter, from_one.at[lax.rem(block, SLOTS), pl.ds(0, quarter)])

            @pl.when(pos.end)
            def _():
                x_two(block).start()

        @pl.when(z_first & pos.end)
        def _():
            z_one(block).wait_send()
            free(1, pos.zp)

        @pl.when(z_first & pos.mid)
        def _():
            z_one(block).wait_recv()
            add(block, half, half, from_one.at[lax.rem(block, SLOTS)])
            z_two(block).start()

    def stage_three(block):
        @pl.when(x_first & pos.end)
        def _():
            x_two(block).wait_send()
            free(0, pos.zp)

        @pl.when(x_first & pos.mid)
        def _():
            x_two(block).wait_recv()
            add(block, xrow, quarter, from_two.at[lax.rem(block, SLOTS)])
            x_three(block).start()

        @pl.when(z_first & pos.mid)
        def _():
            z_two(block).wait()
            free(0, pos.zm)
            add(block, keep, quarter, from_two.at[lax.rem(block, SLOTS)])
            z_three(block).start()

    def stage_four(block):
        @pl.when(x_first & pos.mid)
        def _():
            x_three(block).wait()
            add(block, xrow, quarter, from_three.at[lax.rem(block, SLOTS)])
            claim(0)
            x_four(block).start()

        @pl.when(z_first & pos.mid)
        def _():
            z_three(block).wait()
            add(block, keep, quarter, from_three.at[lax.rem(block, SLOTS)])
            claim(0)
            z_four(block).start()

    def stage_five(block):
        @pl.when(x_first)
        def _():
            @pl.when(pos.end)
            def _():
                x_four(block).wait_recv()

            @pl.when(pos.mid)
            def _():
                x_four(block).wait_send()

            claim(1)
            x_five(block).start()

        @pl.when(z_first & pos.mid)
        def _():
            z_four(block).wait_send()
            z_four_in(block).wait_recv()
            claim(1)
            z_five(block).start()

    def stage_six(block):
        @pl.when(x_first)
        def _():
            x_five(block).wait_send()
            x_five_in(block).wait_recv()

        @pl.when(z_first & pos.end)
        def _():
            z_five(block).wait_recv()

        @pl.when(z_first & pos.mid)
        def _():
            z_five(block).wait_send()

        claim(2)
        core_six(block).start()

    def stage_seven(block):
        core_six(block).wait_send()
        core_six_in(block).wait_recv()
        finish(block)

    stages = (stage_zero, stage_one, stage_two, stage_three, stage_four, stage_five, stage_six, stage_seven)

    def tick(step):
        for index in reversed(range(8)):
            block = step - SPREAD * index

            @pl.when((block >= 0) & (block < count))
            def _(index=index, block=block):
                stages[index](block)

    return tick


def sum_scratch():
    return [
        pltpu.VMEM((SLOTS, BR // 2, BC), jnp.float32),
        pltpu.VMEM((SLOTS, BR // 2, BC), jnp.float32),
        pltpu.VMEM((SLOTS, BR // 4, BC), jnp.float32),
        pltpu.VMEM((SLOTS, BR // 4, BC), jnp.float32),
        pltpu.SemaphoreType.DMA((7, SLOTS)),
        pltpu.SemaphoreType.DMA((7, SLOTS)),
        pltpu.SemaphoreType.REGULAR((3,)),
    ]


def sum_kernel(count, grads_in, out, grads, a, b, c, d, sent, got, credit, out_sem, in_sem):
    pos = Place()
    load = pltpu.make_async_copy(grads_in, grads, in_sem)
    load.start()
    sum_barrier(pos)
    load.wait()

    def put(block):
        return pltpu.make_async_copy(grads.at[block], out.at[block], out_sem.at[lax.rem(block, 4)])

    def finish(block):
        @pl.when(block >= 4)
        def _():
            put(block - 4).wait()

        put(block).start()

    tick = make_tick(pos, grads, a, b, c, d, sent, got, credit, count, finish)

    @pl.loop(0, count + 7 * SPREAD)
    def _(step):
        tick(step)

    for block in range(count - 4, count):
        put(block).wait()


def sum_blocks(blocks):
    count = blocks.shape[0]
    return pl.pallas_call(
        functools.partial(sum_kernel, count),
        out_shape=jax.ShapeDtypeStruct(blocks.shape, jnp.float32),
        in_specs=[pl.BlockSpec(memory_space=pl.ANY)],
        out_specs=pl.BlockSpec(memory_space=pl.ANY),
        scratch_shapes=[pltpu.VMEM(blocks.shape, jnp.float32)]
        + sum_scratch()
        + [pltpu.SemaphoreType.DMA((4,)), pltpu.SemaphoreType.DMA],
        compiler_params=pltpu.CompilerParams(collective_id=1, has_side_effects=True, vmem_limit_bytes=60 * 2**20),
        name="sum_blocks",
    )(blocks)


CR, CC = 64, 384
CHUNKS = 24
BF = jnp.bfloat16


def gather_barrier(pos, other):
    barrier = pltpu.get_barrier_semaphore()
    for where in ({"tensor": other}, {"dp": pos.xn}, {"dp": pos.zp}, {"dp": pos.sib}):
        pl.semaphore_signal(barrier, inc=1, device_id=where, device_id_type=MESH)
    pl.semaphore_wait(barrier, 4)


def chunk_parts(piece, chunk, kind):
    if kind == 0:
        return [(piece * 384 + chunk * 64, 64, 0, 0)]
    if kind == 1:
        return [(piece * 64 + (chunk - 6) * 32, 32, 384 * q, 32 * q) for q in range(2)]
    if kind == 2:
        return [(piece * 128 + (chunk - 8) * 16, 16, 384 * q, 16 * q) for q in range(4)]
    return [(piece * 256 + (chunk - 16) * 32, 32, 384 * q, 32 * q) for q in range(2)]


BOUNDS = ((0, 6), (6, 8), (8, 16), (16, 24))
UNIT = (64, 32, 16, 32)


def make_gather(pos, own, theirs, staged, landed, sent, got):
    other = 1 - lax.axis_index("tensor")
    odd = lax.rem(pos.z, 2)
    ky = jnp.where(pos.x == 0, odd, 2)
    kx = jnp.where(pos.x == 0, 2, odd)
    kz = 1 - odd
    piece_y = 2 * ky + pos.core
    piece_x = 2 * kx + pos.core
    piece_z = 2 * kz + pos.core
    sib_y = 2 * ky + 1 - pos.core
    sib_x = 2 * kx + 1 - pos.core
    sib_z = 2 * kz + 1 - pos.core

    def copy(lane, chunk, source, piece, where):
        return pltpu.make_async_remote_copy(
            src_ref=source,
            dst_ref=landed.at[piece, chunk],
            send_sem=sent.at[lane, chunk],
            recv_sem=got.at[lane, chunk],
            device_id=where,
            device_id_type=MESH,
        )

    def over_y(chunk):
        return copy(0, chunk, staged.at[chunk], piece_y, {"tensor": other})

    def over_x(chunk, piece):
        return copy(1, chunk, landed.at[piece, chunk], piece, {"dp": pos.xn})

    def over_z(chunk, piece):
        return copy(2, chunk, landed.at[piece, chunk], piece, {"dp": pos.zp})

    def over_core(lane, chunk, piece):
        return copy(lane, chunk, landed.at[piece, chunk], piece, {"dp": pos.sib})

    def stage_own():
        for kind in range(4):
            lo, hi = BOUNDS[kind]

            @pl.loop(lo, hi)
            def _(chunk, kind=kind):
                for row, rows, column, at in chunk_parts(piece_y, chunk, kind):
                    staged[chunk, pl.ds(at, rows)] = own[kind][
                        pl.ds(pl.multiple_of(row, UNIT[kind]), rows), pl.ds(column, CC)
                    ].astype(jnp.float32)

    def send_own():
        @pl.loop(0, CHUNKS)
        def _(chunk):
            over_y(chunk).start()

    def unpack(chunk):
        for kind in range(4):
            lo, hi = BOUNDS[kind]

            @pl.when((chunk >= lo) & (chunk < hi))
            def _(kind=kind):
                @pl.loop(0, 6)
                def _(piece):
                    for row, rows, column, at in chunk_parts(piece, chunk, kind):
                        theirs[kind][pl.ds(pl.multiple_of(row, UNIT[kind]), rows), pl.ds(column, CC)] = landed[
                            piece, chunk, pl.ds(at, rows)
                        ].astype(BF)

    def guarded(chunk, body):
        @pl.when((chunk >= 0) & (chunk < CHUNKS))
        def _():
            body(chunk)

    def first(chunk):
        over_y(chunk).wait_recv()
        over_x(chunk, piece_y).start()

        @pl.when(pos.x == 0)
        def _():
            over_z(chunk, piece_y).start()

        over_core(3, chunk, piece_y).start()

    def second(chunk):
        over_x(chunk, piece_x).wait_recv()

        @pl.when(pos.x == 1)
        def _():
            over_z(chunk, piece_x).start()

        over_core(4, chunk, piece_x).start()

    def third(chunk):
        over_z(chunk, piece_z).wait_recv()
        over_core(5, chunk, piece_z).start()

    def fourth(chunk):
        over_core(3, chunk, sib_y).wait_recv()
        over_core(4, chunk, sib_x).wait_recv()
        over_core(5, chunk, sib_z).wait_recv()
        over_y(chunk).wait_send()
        over_x(chunk, piece_y).wait_send()
        over_z(chunk, piece_y).wait_send()
        over_core(3, chunk, piece_y).wait_send()
        over_core(4, chunk, piece_x).wait_send()
        over_core(5, chunk, piece_z).wait_send()
        unpack(chunk)

    def tick(step):
        guarded(step - 6, fourth)
        guarded(step - 4, third)
        guarded(step - 2, second)
        guarded(step, first)

    return stage_own, send_own, tick


GATHER_TICKS = CHUNKS + 6


def gather_scratch():
    return [
        pltpu.VMEM((CHUNKS, CR, CC), jnp.float32),
        pltpu.VMEM((6, CHUNKS, CR, CC), jnp.float32),
        pltpu.SemaphoreType.DMA((6, CHUNKS)),
        pltpu.SemaphoreType.DMA((6, CHUNKS)),
    ]


def swap_small(small, small_out, sems):
    return pltpu.make_async_remote_copy(
        src_ref=small,
        dst_ref=small_out,
        send_sem=sems.at[0],
        recv_sem=sems.at[1],
        device_id={"tensor": 1 - lax.axis_index("tensor")},
        device_id_type=MESH,
    )


def gather_kernel(a, b, c, d, small, oa, ob, oc, od, small_out, staged, landed, sent, got, sems):
    pos = Place()
    stage_own, send_own, tick = make_gather(pos, (a, b, c, d), (oa, ob, oc, od), staged, landed, sent, got)
    stage_own()
    gather_barrier(pos, 1 - lax.axis_index("tensor"))
    swap = swap_small(small, small_out, sems)
    swap.start()
    send_own()

    @pl.loop(0, GATHER_TICKS)
    def _(step):
        tick(step)

    swap.wait()


def gather(ws):
    v = pl.BlockSpec(memory_space=pltpu.VMEM)
    return pl.pallas_call(
        gather_kernel,
        out_shape=[jax.ShapeDtypeStruct(w.shape, w.dtype) for w in ws],
        in_specs=[v] * 5,
        out_specs=[v] * 5,
        scratch_shapes=gather_scratch() + [pltpu.SemaphoreType.DMA((2,))],
        compiler_params=pltpu.CompilerParams(collective_id=0, has_side_effects=True, vmem_limit_bytes=60 * 2**20),
        name="gather_weights",
    )(*ws)


HD = 64
SEG = 148
MEMW = 10
F32 = jnp.float32
EPSILON = 1e-12
MASKED = -1e30
WIN = 160
MEMP = 96
SEGS = 8
PAIR = 2 * HD

CONTRACT_LAST = (((1,), (1,)), ((), ()))
CONTRACT_FIRST = (((0,), (0,)), ((), ()))


def mm(a, b):
    return jnp.dot(a, b, preferred_element_type=F32)


def mm_t(a, b):
    return lax.dot_general(a, b, CONTRACT_LAST, preferred_element_type=F32)


def t_mm(a, b):
    return lax.dot_general(a, b, CONTRACT_FIRST, preferred_element_type=F32)


def build_masks(parent, base, colbias):
    lane = lax.broadcasted_iota(jnp.int32, (1, WIN + MEMP), 1)
    in_mem = [
        ((lane >= WIN + MEMW * t) & (lane < WIN + MEMW * (t + 1))).astype(F32) for t in range(SEGS)
    ]
    reach = [jnp.zeros((1, WIN + MEMP), F32)]
    for s in range(1, SEGS):
        row = jnp.zeros((1, WIN + MEMP), F32)
        for t in range(s):
            hit = jnp.where(parent[s] - base == t, 1.0, 0.0)
            row = row + hit * jnp.maximum(reach[t], in_mem[t])
        reach.append(row)
    for s in range(SEGS):
        off = 4 * (s % 4)
        inside = ((lane >= off) & (lane < off + SEG)).astype(F32)
        colbias[s : s + 1, :] = jnp.where(jnp.maximum(inside, reach[s]) > 0.0, 0.0, MASKED)


def build_select(slot_rows, select):
    place = lax.broadcasted_iota(jnp.int32, select.shape, 1)
    select[...] = (slot_rows[...] == place).astype(F32).astype(BF)


def window(s):
    return pl.multiple_of(144 * s + 16 * (s // 4), 16), 4 * lax.rem(s, 4)


def lane_halves():
    lane = lax.broadcasted_iota(jnp.int32, (1, PAIR), 1)
    left = (lane < HD).astype(F32)
    return left.astype(BF), (1.0 - left).astype(BF), lane < HD


def valid_rows(off):
    row = lax.broadcasted_iota(jnp.int32, (WIN, 1), 0)
    return row, (row >= off) & (row < off + SEG)


def softmax_parts(qs, kk, bias):
    scores = mm_t(qs, kk) * HD ** (-0.5) + bias
    top = jnp.max(scores, axis=-1, keepdims=True)
    raised = jnp.exp(scores - top)
    return raised, 1.0 / jnp.sum(raised, axis=-1, keepdims=True)


def attend_pair(q, k, v, kmem, vmem, colbias, mixed, s, columns):
    left, right, is_left = lane_halves()
    at, off = window(s)
    rows = pl.ds(at, WIN)
    qw = q[rows, columns]
    qs = jnp.concatenate([qw * left, qw * right], axis=0)
    kk = jnp.concatenate([k[rows, columns], kmem[:, columns]], axis=0)
    vv = jnp.concatenate([v[rows, columns], vmem[:, columns]], axis=0)
    raised, scale = softmax_parts(qs, kk, colbias[pl.ds(s, 1), :])
    both = mm((raised * scale).astype(BF), vv)
    out = jnp.where(is_left, both[:WIN], both[WIN:])
    row, valid = valid_rows(off)
    old = mixed[rows, columns].astype(F32)
    mixed[rows, columns] = jnp.where(row >= off, out, old).astype(BF)


def attend_back_pair(q, k, v, kmem, vmem, colbias, dmix, dq, dk, dv, dkmem, dvmem, s, columns, acc):
    left, right, is_left = lane_halves()
    at, off = window(s)
    rows = pl.ds(at, WIN)
    qw = q[rows, columns]
    qs = jnp.concatenate([qw * left, qw * right], axis=0)
    kk = jnp.concatenate([k[rows, columns], kmem[:, columns]], axis=0)
    vv = jnp.concatenate([v[rows, columns], vmem[:, columns]], axis=0)
    dw = dmix[rows, columns]
    ds_in = jnp.concatenate([dw * left, dw * right], axis=0)
    raised, scale = softmax_parts(qs, kk, colbias[pl.ds(s, 1), :])
    row, valid = valid_rows(off)
    keep = jnp.where(valid, 1.0, 0.0)
    chances = raised * (scale * jnp.concatenate([keep, keep], axis=0))
    dp = mm_t(ds_in, vv)
    inner = jnp.sum(chances * dp, axis=-1, keepdims=True)
    ds = (chances * (dp - inner)).astype(BF)
    pb = chances.astype(BF)
    dqs = mm(ds, kk)
    new = jnp.where(is_left, dqs[:WIN], dqs[WIN:]) * HD ** (-0.5)
    old = dq[rows, columns].astype(F32)
    dq[rows, columns] = jnp.where(row >= off, new, old).astype(BF)
    dks = t_mm(ds, qs)
    dvs = t_mm(pb, ds_in)
    dk[rows, acc] = dk[rows, acc] + dks[:WIN]
    dv[rows, acc] = dv[rows, acc] + dvs[:WIN]
    dkmem[:, acc] = dkmem[:, acc] + dks[WIN:]
    dvmem[:, acc] = dvmem[:, acc] + dvs[WIN:]


def spread(select, part):
    high = part.astype(BF)
    low = (part - high.astype(F32)).astype(BF)
    return t_mm(select, high) + t_mm(select, low)


def forward_attention_kernel(parent, slot_rows, q, k, v, mixed, colbias, select, kmem, vmem):
    base = lax.axis_index("dp") * SEGS
    build_masks(parent, base, colbias)
    build_select(slot_rows, select)
    kmem[...] = mm(select[...], k[...]).astype(BF)
    vmem[...] = mm(select[...], v[...]).astype(BF)
    pairs = q.shape[1] // PAIR

    @pl.loop(0, SEGS)
    def _(s):
        for pair in range(pairs):
            attend_pair(q, k, v, kmem, vmem, colbias, mixed, s, pl.ds(pair * PAIR, PAIR))


def backward_attention_kernel(
    parent, slot_rows, q, k, v, dmix, dq, dk, dv, colbias, select, kmem, vmem, dka, dva, dkm, dvm
):
    base = lax.axis_index("dp") * SEGS
    build_masks(parent, base, colbias)
    build_select(slot_rows, select)
    kmem[...] = mm(select[...], k[...]).astype(BF)
    vmem[...] = mm(select[...], v[...]).astype(BF)
    pairs = q.shape[1] // PAIR
    for ref in (dka, dva, dkm, dvm):
        ref[...] = jnp.zeros(ref.shape, F32)

    @pl.loop(0, SEGS)
    def _(s):
        for pair in range(pairs):
            columns = pl.ds(pair * PAIR, PAIR)
            attend_back_pair(
                q, k, v, kmem, vmem, colbias, dmix, dq, dka, dva, dkm, dvm, s, columns, columns
            )

    for pair in range(pairs):
        columns = pl.ds(pair * PAIR, PAIR)
        dk[:, columns] = ((dka[:, columns] + spread(select[...], dkm[:, columns])) * HD ** (-0.5)).astype(BF)
        dv[:, columns] = (dva[:, columns] + spread(select[...], dvm[:, columns])).astype(BF)


def attention_call(kernel, outs, parent, slot_rows, arrays, scratch, name):
    rows, width = arrays[0].shape
    vm = pl.BlockSpec(memory_space=pltpu.VMEM)
    return pl.pallas_call(
        kernel,
        out_shape=[jax.ShapeDtypeStruct((rows, width), BF)] * outs,
        in_specs=[pl.BlockSpec(memory_space=pltpu.SMEM), vm] + [vm] * len(arrays),
        out_specs=[vm] * outs,
        scratch_shapes=[
            pltpu.VMEM((SEGS, WIN + MEMP), F32),
            pltpu.VMEM((MEMP, rows), BF),
            pltpu.VMEM((MEMP, width), BF),
            pltpu.VMEM((MEMP, width), BF),
        ]
        + scratch,
        compiler_params=pltpu.CompilerParams(vmem_limit_bytes=60 * 2**20),
        name=name,
    )(parent, slot_rows, *arrays)


def forward_attention(parent, slot_rows, q, k, v):
    return attention_call(forward_attention_kernel, 1, parent, slot_rows, (q, k, v), [], "attend")[0]


def backward_attention(parent, slot_rows, q, k, v, dmix):
    rows, width = q.shape
    scratch = [pltpu.VMEM((rows, width), F32)] * 2 + [pltpu.VMEM((MEMP, width), F32)] * 2
    return attention_call(
        backward_attention_kernel, 3, parent, slot_rows, (q, k, v, dmix), scratch, "attend_back"
    )


def halves_swap(own, small):
    unit = (lax.axis_index("dp") >= 0).astype(F32)

    def other(array):
        arrived = lax.ppermute(array.astype(F32), "tensor", [(0, 1), (1, 0)])
        return (arrived * unit).astype(array.dtype)

    return tuple(other(array) for array in own) + (other(small),)


def norm_stats(values):
    centered = values - jnp.mean(values, axis=-1, keepdims=True)
    inverse = lax.rsqrt(jnp.mean(centered * centered, axis=-1, keepdims=True) + EPSILON)
    return centered * inverse, inverse


def norm_back(grad, normed, inverse, gain):
    scaled = grad * gain
    return inverse * (
        scaled
        - jnp.mean(scaled, axis=-1, keepdims=True)
        - normed * jnp.mean(scaled * normed, axis=-1, keepdims=True)
    )


def gelu_parts(inner):
    phi = 0.5 * (1.0 + lax.erf(inner * (0.5**0.5)))
    density = jnp.exp(-0.5 * inner * inner) * (2.0 * jnp.pi) ** -0.5
    return (inner * phi).astype(BF), phi + inner * density


def split_blocks(array, rows, columns):
    height, width = array.shape
    return (
        array.reshape(height // rows, rows, width // columns, columns)
        .transpose(0, 2, 1, 3)
        .reshape(-1, rows, columns)
    )


def join_blocks(blocks, height, width):
    count, rows, columns = blocks.shape
    return (
        blocks.reshape(height // rows, width // columns, rows, columns)
        .transpose(0, 2, 1, 3)
        .reshape(height, width)
    )


def shards(
    fast,
    tokens,
    w_qkv,
    bias_qv,
    w_out,
    bias_out,
    gain_one,
    shift_one,
    w_up,
    bias_up,
    w_down,
    bias_down,
    gain_two,
    shift_two,
    grad_out,
    parent,
    mem_slots,
):
    depth, width = w_qkv.shape[1:]
    hidden_units = w_up.shape[1]
    own = (w_qkv.reshape(3 * depth, width), w_out, w_up, w_down)
    small = jnp.concatenate(
        [bias_qv, bias_up.reshape(-1, width), jnp.zeros((8 - 2 - hidden_units // width, width), F32)]
    )
    if fast:
        theirs = gather((*own, small))
    else:
        theirs = halves_swap(own, small)
    *theirs, small_theirs = theirs
    w_qkv_both = [own[0].reshape(w_qkv.shape), theirs[0].reshape(w_qkv.shape)]
    w_out_both, w_up_both, w_down_both = ([own[i], theirs[i]] for i in (1, 2, 3))
    bias_qv_both = [bias_qv, small_theirs[:2]]
    bias_up_both = [bias_up, small_theirs[2 : 2 + hidden_units // width].reshape(-1)]

    offsets = jnp.arange(SEGS, dtype=jnp.int32)[:, None] * SEG
    slot_rows = (mem_slots + offsets).reshape(-1, 1)
    slot_rows = jnp.concatenate([slot_rows, jnp.full((MEMP - slot_rows.shape[0], 1), -1, jnp.int32)])

    def project(index, bias):
        parts = []
        for half in range(2):
            part = mm(tokens, w_qkv_both[half][index])
            if bias is not None:
                part = part + bias_qv_both[half][bias]
            parts.append(part.astype(BF))
        return jnp.concatenate(parts, axis=1)

    queries, keys, values = project(0, 0), project(1, None), project(2, 1)
    mixed = forward_attention(parent, slot_rows, queries, keys, values)
    attended = mm(mixed[:, :width], w_out_both[0]) + mm(mixed[:, width:], w_out_both[1])
    resid_one = tokens.astype(F32) + (attended + bias_out)
    normed_one, inverse_one = norm_stats(resid_one)
    hidden = normed_one * gain_one + shift_one
    hidden_low = hidden.astype(BF)
    acted, slope, summed = [], [], []
    for half in range(2):
        inner = mm(hidden_low, w_up_both[half]) + bias_up_both[half]
        act, steep = gelu_parts(inner)
        acted.append(act)
        slope.append(steep)
        summed.append(mm(act, w_down_both[half]))
    resid_two = hidden + ((summed[0] + summed[1]) + bias_down)
    normed_two, inverse_two = norm_stats(resid_two)
    output = (normed_two * gain_two + shift_two).astype(BF)

    cotangent = grad_out.astype(F32)
    d_two = norm_back(cotangent, normed_two, inverse_two, gain_two)
    d_gain_two = jnp.sum(cotangent * normed_two, axis=0)
    d_shift_two = jnp.sum(cotangent, axis=0)
    d_ffn = d_two.astype(BF)
    d_w_down = t_mm(acted[0], d_ffn)
    d_bias_down = jnp.sum(d_ffn.astype(F32), axis=0)
    d_inner = [(mm_t(d_ffn, w_down_both[half]) * slope[half]).astype(BF) for half in range(2)]
    d_w_up = t_mm(hidden_low, d_inner[0])
    d_bias_up = jnp.sum(d_inner[0].astype(F32), axis=0)
    d_hidden = d_two + (mm_t(d_inner[0], w_up_both[0]) + mm_t(d_inner[1], w_up_both[1]))
    d_one = norm_back(d_hidden, normed_one, inverse_one, gain_one)
    d_gain_one = jnp.sum(d_hidden * normed_one, axis=0)
    d_shift_one = jnp.sum(d_hidden, axis=0)
    d_attn = d_one.astype(BF)
    d_w_out = t_mm(mixed[:, :width], d_attn)
    d_bias_out = jnp.sum(d_attn.astype(F32), axis=0)
    d_mixed = jnp.concatenate([mm_t(d_attn, w_out_both[half]).astype(BF) for half in range(2)], axis=1)
    d_qkv = backward_attention(parent, slot_rows, queries, keys, values, d_mixed)
    d_w_qkv = [t_mm(tokens, part[:, :width]) for part in d_qkv]
    d_bias_qv = [jnp.sum(d_qkv[i][:, :width].astype(F32), axis=0) for i in (0, 2)]
    parts = []
    for half in range(2):
        columns = slice(half * width, (half + 1) * width)
        parts.append(sum(mm_t(d_qkv[i][:, columns], w_qkv_both[half][i]) for i in range(3)))
    grad_tokens = ((parts[0] + parts[1]) + d_one).astype(BF)

    vectors = [*d_bias_qv, d_bias_up, d_bias_out, d_gain_one, d_shift_one, d_bias_down, d_gain_two, d_shift_two]
    if fast:
        flat = jnp.concatenate([v.reshape(-1, width) for v in vectors])
        flat = jnp.concatenate([flat, jnp.zeros((BR - flat.shape[0], width), F32)])
        blocks = jnp.concatenate(
            [
                split_blocks(d_w_down, BR, BC),
                split_blocks(d_w_up, BR, BC),
                split_blocks(d_w_out, BR, BC),
                *[split_blocks(part, BR, BC) for part in d_w_qkv],
                flat[None],
            ]
        )
        blocks = sum_blocks(blocks)
        g_w_down = join_blocks(blocks[:24], *w_down.shape)
        g_w_up = join_blocks(blocks[24:48], *w_up.shape)
        g_w_out = join_blocks(blocks[48:54], *w_out.shape)
        g_w_qkv = blocks[54:72].reshape(w_qkv.shape)
        flat = blocks[72]
        sums, row = [], 0
        for v in vectors:
            sums.append(flat[row : row + v.size // width].reshape(-1))
            row += v.size // width
    else:
        g_w_down, g_w_up, g_w_out, g_w_qkv, *sums = lax.psum(
            (d_w_down, d_w_up, d_w_out, jnp.stack(d_w_qkv), *vectors), "dp"
        )
    g_bias_q, g_bias_v, g_bias_up, g_bias_out, g_gain_one, g_shift_one, g_bias_down, g_gain_two, g_shift_two = sums
    return (
        output,
        grad_tokens,
        g_w_qkv,
        jnp.stack([g_bias_q, g_bias_v]),
        g_w_out,
        g_bias_out,
        g_gain_one,
        g_shift_one,
        g_w_up,
        g_bias_up,
        g_w_down,
        g_bias_down,
        g_gain_two,
        g_shift_two,
    )


def solution(mesh):
    fast = mesh.shape["dp"] == 16 and mesh.shape["tensor"] == 2
    rows, whole = P("dp", None), P()
    return jax.shard_map(
        functools.partial(shards, fast),
        mesh=mesh,
        in_specs=(
            rows,
            P(None, None, "tensor"),
            P(None, "tensor"),
            P("tensor", None),
            whole,
            whole,
            whole,
            P(None, "tensor"),
            P("tensor"),
            P("tensor", None),
            whole,
            whole,
            whole,
            rows,
            P("dp"),
            rows,
        ),
        out_specs=(
            rows,
            rows,
            P(None, None, "tensor"),
            P(None, "tensor"),
            P("tensor", None),
            whole,
            whole,
            whole,
            P(None, "tensor"),
            P("tensor"),
            P("tensor", None),
            whole,
            whole,
            whole,
        ),
        check_vma=False,
    )
```

time: 1150 us -> 514 us (0.45)
  waiting for transfers between devices: 702 us -> 0 us
  Pallas kernels: 0 us -> 290 us
  blocking collectives: 116 us -> 0 us
  matrix products: 175 us -> 99.3 us
  other arithmetic: 76.5 us -> 31 us
  local copies, waits for them, and re-layouts: 61.8 us -> 87.8 us
  between operations: 17.5 us -> 1.64 us
    psum x4 -> x0, waiting for transfers between devices: 292 us -> none  [the longest x1 99.3 us: forward_pass(): attended = lax.psum(partial_attn, 'tensor')]
    pallas_call x0 -> x4, Pallas kernels: none -> 290 us  [the longest x1 155 us: sum_blocks(): pl.pallas_call(functools.partial(sum_kernel, count), out_shape=jax.ShapeD...]
    all_gather x4 -> x0, waiting for transfers between devices: 162 us -> none  [the longest x1 54.5 us: shards(): lax.all_gather(shared[8], 'dp', axis=1, tiled=True)]
    reduce_scatter x3 -> x0, waiting for transfers between devices: 157 us -> none  [the longest x1 79.4 us: shards(): lax.psum_scatter(d_w_up, 'dp', scatter_dimension=0, tiled=True)]
    unnamed x2 -> x0, blocking collectives: 116 us -> none
    unnamed x13 -> x0, waiting for transfers between devices: 91 us -> none
    dot_general x18 -> x29, matrix products: 175 us -> 99.3 us  [the longest x11 40.8 us: mm_t(): return lax.dot_general(a, b, CONTRACT_LAST, preferred_element_type=F32)]
    convert_element_type x2 -> x0, other arithmetic: 35.3 us -> none  [the longest x1 30.6 us: attend_back(): d_scores = (chances * (d_chances - row_inner)).astype(jnp.bfloat16)]
  transfers between devices with their start and end apart: 12 -> 0, of which waited for: 10 -> 0; matrix products, arithmetic and copies ran while one was open for 10% -> 0% of each run, Pallas kernels for 0% -> 0%
where the time goes in v1:
time: 514 us; the launch traced here: 510 us
  Pallas kernels  290 us (56%)
  matrix products  99.3 us (19%)
  local copies, waits for them, and re-layouts  87.8 us (17%)
  other arithmetic  31 us (6%)
    pallas_call x1, Pallas kernels, sum_blocks(): pl.pallas_call(functools.partial(sum_kernel, count), out_shape=jax.ShapeD...  155 us
    pallas_call x1, Pallas kernels, gather(): pl.pallas_call(gather_kernel, out_shape=[jax.ShapeDtypeStruct(w.shape, w....  71.3 us
    pallas_call x2, Pallas kernels, attention_call(): pl.pallas_call(kernel, out_shape=[jax.ShapeDtypeStruct((rows, width), BF)...  63.5 us
    dot_general x11, matrix products, mm_t(): return lax.dot_general(a, b, CONTRACT_LAST, preferred_element_type=F32)  40.8 us
    dot_general x12, matrix products, mm(): return jnp.dot(a, b, preferred_element_type=F32)  38 us
    unnamed x109, local copies, waits for them, and re-layouts  31.5 us
    reshape x6, local copies, waits for them, and re-layouts, split_blocks(): array.reshape(height // rows, rows, width // columns, columns)  20.9 us
    dot_general x6, matrix products, t_mm(): return lax.dot_general(a, b, CONTRACT_FIRST, preferred_element_type=F32)  20.4 us

profile of v1, /device:TPU:0, one launch (start us, length us, event | category | flops | bytes accessed | tf_op | source)
XLA Modules:
  0.0 509.9 jit_solution(17782049032889126533)
XLA Ops:
  2.9 1.4 maximum_maximum_fusion.small
  4.3 71.3 %gather_weights.1 = (bf16[2304,384]{1,0:T(8,128)(2,1)}, bf16[384,768]{1,0:T(8,128)(2,1)}, bf16[768,1536]{1,0:T(8,128)(2,1)}, bf16[1536,768]{1,0:T(8,128)(2,1)}, f32[8,384]{1,0:T(8,128)}) custom-call(bf16[2304,384]{1,0:T(8,128)(2,1)} %bitcast.105, bf16[384,768]{1,0:T(8,128)(2,1)} %b.1, bf16[768,1536]{1,0:T(8,128)(2,1)} %c.1, bf16[1536,768]{1,0:T(8,128)(2,1)} %d.1, ...), custom_call_target="tpu_custom_call" | custom-call | tf_op jit(solution)/shard_map/gather_weights/pallas_call | solution.py:493
  76.4 2.3 fusion.32
  78.8 1.1 fusion.26
  80.2 1.1 fusion.30
  81.4 1.1 convolution_convert_fusion.3
  82.5 2.1 pad_maximum_fusion
  84.6 1.1 fusion.31
  85.7 1.1 fusion.27
  86.8 1.4 pad_maximum_fusion.2.v
  88.2 15.6 %attend.1 = bf16[1184,768]{1,0:T(8,128)(2,1)} custom-call(s32[8]{0:T(128)} %parent.3, s32[96,1]{1,0:T(8,128)} %concatenate.24.slot_rows, bf16[1184,768]{1,0:T(8,128)(2,1)} %get-tuple-element.67.q, bf16[1184,768]{1,0:T(8,128)(2,1)} %get-tuple-element.68.k, bf16[1184,768]{1,0:T(8,128)(2,1)} %pad_maximum_fusion.2.v), custom_call_target="tpu_custom_call" | custom-call | tf_op jit(solution)/shard_map/attend/pallas_call | solution.py:671
  103.8 2.4 fusion.40
  106.3 1.5 fusion.73
  108.4 2.3 copy-done.22
  110.8 6.3 %multiply_convert_fusion.1 = (bf16[1184,1536]{1,0:T(8,128)(2,1)S(1)}, f32[1184,1536]{1,0:T(8,128)}) fusion(f32[1536]{0:T(1024)S(1)} %copy-done.31, bf16[768,1536]{1,0:T(8,128)(2,1)S(1)} %copy-done.22, f32[1184,768]{1,0:T(8,128)S(1)} %get-tuple-element.59, f32[768]{0:T(1024)S(1)} %copy-done.38, f32[768]{0:T(1024)S(1)} %copy-done.35, ...), kind=kOutput, calls=%fused_computation.19 | convolution fusion | flops 2808864768 | bytes 16930048 | tf_op jit(solution)/shard_map/dot_general | solution.py:520
  117.0 4.8 fusion.79
  121.9 6.2 %convolution_add_fusion = f32[1184,1536]{1,0:T(8,128)S(1)} fusion(bf16[768,1536]{1,0:T(8,128)(2,1)} %get-tuple-element.25, f32[1536]{0:T(1024)S(1)} %add.190, f32[1184,768]{1,0:T(8,128)} %copy-done, f32[768]{0:T(1024)S(1)} %copy-done.38, f32[768]{0:T(1024)S(1)} %copy-done.35, f32[1184]{0:T(1024)S(1)} %add_rsqrt_fusion.1, f32[1184]{0:T(1024)S(1)} %broadcast_multiply_fusion.5), kind=kOutput, calls=%fused_computation.4 | convolution fusion | flops 2799771648 | bytes 13292800 | tf_op jit(solution)/shard_map/dot_general | solution.py:520
  128.2 9.0 %fusion.74 = (f32[1184]{0:T(1024)S(1)}, f32[1184,768]{1,0:T(8,128)S(1)}) fusion(f32[768]{0:T(1024)S(1)} %copy-done.37, f32[1184,768]{1,0:T(8,128)} %fusion.79, bf16[1536,768]{1,0:T(8,128)(2,1)S(1)} %copy-done.36, f32[1184,1536]{1,0:T(8,128)S(1)} %convolution_add_fusion, f32[768]{0:T(1024)S(1)} %copy-done.38, f32[768]{0:T(1024)S(1)} %copy-done.35, ...), kind=kOutput, calls=%fused_computation.148 | convolution fusion | flops 2809772800 | bytes 20568960 | tf_op jit(solution)/shard_map/dot_general | solution.py:520
  137.8 2.2 copy-done.11
  140.0 2.1 fusion.23
  142.2 14.8 %convert_reduce_fusion.2 = (f32[768]{0:T(1024)S(1)}, bf16[1184,768]{1,0:T(8,128)(2,1)S(1)}, bf16[1184,768]{1,0:T(8,128)(2,1)}) fusion(f32[1184]{0:T(1024)S(1)} %broadcast_multiply_fusion.2, f32[1184,768]{1,0:T(8,128)S(1)} %get-tuple-element.63, f32[1184]{0:T(1024)S(1)} %broadcast_multiply_fusion.4, f32[1184]{0:T(1024)S(1)} %broadcast_multiply_fusion.3, ...), kind=kLoop, calls=%fused_computation.45 | loop fusion | flops 12729600 | bytes 9121280 | tf_op jit(solution)/shard_map/reduce_sum | solution.py:821
  157.0 5.5 %convert_reduce_fusion = (f32[1536]{0:T(1024)S(1)}, bf16[1184,1536]{1,0:T(8,128)(2,1)S(1)}) fusion(f32[1184,1536]{1,0:T(8,128)S(1)} %bitcast.116, bf16[1184,768]{1,0:T(8,128)(2,1)S(1)} %get-tuple-element.43, bf16[1536,768]{1,0:T(8,128)(2,1)S(1)} %copy-done.21), kind=kOutput, calls=%fused_computation.16 | convolution fusion | flops 2815228416 | bytes 15095808 | tf_op jit(solution)/shard_map/dot_general | solution.py:524
  162.5 1.9 copy-done.39
  164.4 4.9 fusion.80
  169.3 18.6 %multiply_reduce_fusion = (f32[768]{0:T(1024)S(1)}, f32[1184]{0:T(1024)S(1)}, f32[1184]{0:T(1024)S(1)}, f32[768]{0:T(1024)S(1)}, f32[1184,768]{1,0:T(8,128)}) fusion(f32[1184,768]{1,0:T(8,128)} %copy-done, f32[1184]{0:T(1024)S(1)} %add_rsqrt_fusion.1, f32[1184]{0:T(1024)S(1)} %broadcast_multiply_fusion.5, f32[768]{0:T(1024)S(1)} %copy-done.35, ...), kind=kOutput, calls=%fused_computation.46 | convolution fusion | flops 5622272000 | bytes 30229504 | tf_op jit(solution)/shard_map/dot_general | solution.py:524
  187.9 5.0 convert_reduce_fusion.3
  192.9 1.1 convolution_convert_fusion.1
  194.2 1.1 convolution_convert_fusion.2
  195.3 1.4 pad_maximum_fusion.3.dmix
  196.7 47.9 %attend_back.1 = (bf16[1184,768]{1,0:T(8,128)(2,1)}, bf16[1184,768]{1,0:T(8,128)(2,1)}, bf16[1184,768]{1,0:T(8,128)(2,1)}) custom-call(s32[8]{0:T(128)} %parent.3, s32[96,1]{1,0:T(8,128)} %concatenate.24.slot_rows, bf16[1184,768]{1,0:T(8,128)(2,1)} %get-tuple-element.67.q, bf16[1184,768]{1,0:T(8,128)(2,1)} %get-tuple-element.68.k, ...), custom_call_target="tpu_custom_call" | custom-call | tf_op jit(solution)/shard_map/attend_back/pallas_call | solution.py:671
  244.6 2.6 fusion.36
  247.3 1.2 convolution_add_fusion.3
  248.8 1.2 convolution_add_fusion.2
  250.8 1.1 fusion.47
  251.9 1.1 convolution_add_fusion.5
  254.0 2.4 fusion.24
  257.2 5.0 fusion.81
  262.1 6.7 %reshape.203 = f32[12,128,2,384]{3,2,1,0:T(2,128)} reshape(f32[1536,768]{1,0:T(8,128)} %fusion.81) | data formatting | bytes 9437184 | tf_op jit(solution)/shard_map/reshape | solution.py:734
  268.9 3.0 copy.31
  271.8 2.9 constant_dynamic-update-slice_fusion.5
  275.4 1.3 copy-done.40
  276.7 5.2 %fusion.75 = f32[768,1536]{1,0:T(8,128)} fusion(bf16[1184,1536]{1,0:T(8,128)(2,1)S(1)} %copy-done.40, f32[1184,768]{1,0:T(8,128)S(1)} %copy-done.2, f32[768]{0:T(1024)S(1)} %copy-done.38, f32[768]{0:T(1024)S(1)} %copy-done.35, f32[1184]{0:T(1024)S(1)} %add_rsqrt_fusion.1, f32[1184]{0:T(1024)S(1)} %broadcast_multiply_fusion.5), kind=kOutput, calls=%fused_computation.149 | convolution fusion | flops 2797953024 | bytes 12008704 | tf_op jit(solution)/shard_map/dot_general | solution.py:528
  281.9 6.3 %reshape.205 = f32[6,128,4,384]{3,2,1,0:T(4,128)} reshape(f32[768,1536]{1,0:T(8,128)} %fusion.75) | data formatting | bytes 9437184 | tf_op jit(solution)/shard_map/reshape | solution.py:734
  288.2 3.0 copy.32
  291.2 2.8 constant_dynamic-update-slice_fusion.4
  294.7 2.0 fusion.38
  296.7 1.9 reshape.207
  298.7 1.1 constant_dynamic-update-slice_fusion.3
  300.5 2.0 convolution_bitcast_fusion.2
  302.5 1.6 copy.34
  304.1 1.1 constant_dynamic-update-slice_fusion.2
  305.2 3.2 convolution_bitcast_fusion.1
  308.4 1.6 copy.35
  310.0 1.1 constant_dynamic-update-slice_fusion.1
  311.2 3.2 convolution_bitcast_fusion
  314.3 1.8 copy.36
  319.4 155.3 %sum_blocks.1 = f32[73,128,384]{2,1,0:T(8,128)} custom-call(f32[73,128,384]{2,1,0:T(8,128)} %bitcast_dynamic-update-slice_fusion.grads_in), custom_call_target="tpu_custom_call" | custom-call | tf_op jit(solution)/shard_map/sum_blocks/pallas_call | solution.py:300
  474.7 4.2 slice.156
  484.9 6.9 %fusion.72 = (f32[24,128,384]{2,1,0:T(8,128)}, f32[24,128,384]{2,1,0:T(8,128)S(1)}) fusion(f32[73,128,384]{2,1,0:T(8,128)} %sum_blocks.1), kind=kLoop, calls=%fused_computation.146 | loop fusion | bytes 18874368 | tf_op jit(solution)/shard_map/slice | solution.py:856
  491.8 3.0 copy.38
  494.9 2.8 copy.41
  497.7 1.1 slice-done.3
  499.4 6.0 %copy.39 = f32[12,128,2,384]{3,2,1,0:T(2,128)S(1)} copy(f32[12,128,2,384]{3,1,2,0:T(8,128)} %bitcast.103) | data formatting | bytes 9437184 | tf_op jit(solution)/shard_map/transpose | solution.py:744
  505.4 2.5 copy.42
  (149 shorter events, 21.7 us)
Async XLA Ops:
  1.4 75.0 %copy-start.4 = (bf16[1184,768]{1,0:T(8,128)(2,1)S(1)}, bf16[1184,768]{1,0:T(8,128)(2,1)}, u32[]{:S(2)}) copy-start(bf16[1184,768]{1,0:T(8,128)(2,1)} %param.16) | copy-start | bytes 5455876
  76.4 2.3 copy-start.30
  76.4 2.4 copy-start.16
  78.8 1.5 copy-start.26
  88.2 15.6 %copy-start.19 = (bf16[384,768]{1,0:T(8,128)(2,1)S(1)}, bf16[384,768]{1,0:T(8,128)(2,1)}, u32[]{:S(2)}) copy-start(bf16[384,768]{1,0:T(8,128)(2,1)} %b.1) | copy-start | bytes 1769476
  103.8 2.5 copy-start.8
  103.8 2.5 copy-start.28
  103.8 2.5 copy-start.33
  107.8 9.3 %copy-start = (f32[1184,768]{1,0:T(8,128)}, f32[1184,768]{1,0:T(8,128)S(1)}, u32[]{:S(2)}) copy-start(f32[1184,768]{1,0:T(8,128)S(1)} %get-tuple-element.59) | copy-start | bytes 10911748
  107.8 3.0 copy-start.22
  107.8 3.0 copy-start.31
  107.8 3.0 copy-start.35
  107.8 3.0 copy-start.38
  110.8 6.3 %copy-start.20 = (bf16[1536,768]{1,0:T(8,128)(2,1)S(1)}, bf16[1536,768]{1,0:T(8,128)(2,1)}, u32[]{:S(2)}) copy-start(bf16[1536,768]{1,0:T(8,128)(2,1)} %d.1) | copy-start | bytes 7077892
  117.0 4.9 copy-start.42
  117.0 4.9 copy-start.32
  121.9 6.2 %copy-start.1 = (f32[1184,768]{1,0:T(8,128)S(1)}, f32[1184,768]{1,0:T(8,128)}, u32[]{:S(2)}) copy-start(f32[1184,768]{1,0:T(8,128)} %copy-done) | copy-start | bytes 10911748
  121.9 6.2 %copy-start.36 = (bf16[1536,768]{1,0:T(8,128)(2,1)S(1)}, bf16[1536,768]{1,0:T(8,128)(2,1)}, u32[]{:S(2)}) copy-start(bf16[1536,768]{1,0:T(8,128)(2,1)} %get-tuple-element.26) | copy-start | bytes 7077892
  121.9 6.2 %copy-start.37 = (f32[768]{0:T(1024)S(1)}, f32[768]{0:T(1024)}, u32[]{:S(2)}) copy-start(f32[768]{0:T(1024)} %param.26) | copy-start | bytes 9220
  121.9 35.0 %slice-start.5 = ((s8[7274496]{0:T(1024)(128)(4,1)}), s8[4194304]{0:T(1024)(128)(4,1)S(1)}, s32[]{:S(2)}) async-start(s8[7274496]{0:T(1024)(128)(4,1)} %bitcast.115), calls=%async_computation.5 | async-start | bytes 8388608
  128.1 9.0 %copy-start.41 = (f32[1184,1536]{1,0:T(8,128)}, f32[1184,1536]{1,0:T(8,128)S(1)}, u32[]{:S(2)}) copy-start(f32[1184,1536]{1,0:T(8,128)S(1)} %convolution_add_fusion) | copy-start | bytes 21823492
  128.1 28.8 %slice-start.6 = ((s8[7274496]{0:T(1024)(128)(4,1)}), s8[3080192]{0:T(1024)(128)(4,1)S(1)}, s32[]{:S(2)}) async-start(s8[7274496]{0:T(1024)(128)(4,1)} %bitcast.115), calls=%async_computation.6 | async-start | bytes 6160384
  137.2 5.0 copy-start.3
  137.2 2.8 copy-start.11
  137.2 2.8 copy-start.29
  137.8 4.4 copy-start.34
  142.2 14.8 %copy-start.21 = (bf16[1536,768]{1,0:T(8,128)(2,1)S(1)}, bf16[1536,768]{1,0:T(8,128)(2,1)}, u32[]{:S(2)}) copy-start(bf16[1536,768]{1,0:T(8,128)(2,1)} %d.1) | copy-start | bytes 7077892
  157.0 5.5 %copy-start.24 = (bf16[1184,768]{1,0:T(8,128)(2,1)}, bf16[1184,768]{1,0:T(8,128)(2,1)S(1)}, u32[]{:S(2)}) copy-start(bf16[1184,768]{1,0:T(8,128)(2,1)S(1)} %get-tuple-element.43) | copy-start | bytes 5455876
  157.0 7.4 %copy-start.23 = (bf16[768,1536]{1,0:T(8,128)(2,1)S(1)}, bf16[768,1536]{1,0:T(8,128)(2,1)}, u32[]{:S(2)}) copy-start(bf16[768,1536]{1,0:T(8,128)(2,1)} %c.1) | copy-start | bytes 7077892
  162.5 1.9 copy-start.39
  192.9 1.3 copy-start.14
  244.6 2.6 copy-start.18
  244.6 2.6 copy-start.27
  247.3 1.5 copy-start.12
  248.8 1.5 copy-start.5
  248.8 2.0 copy-start.17
  251.9 2.0 copy-start.10
  253.9 2.4 copy-start.25
  253.9 3.2 copy-start.43
  271.8 3.5 copy-start.2
  271.8 4.8 copy-start.40
  291.2 2.8 copy-start.9
  291.2 3.5 copy-start.15
  298.6 1.9 copy-start.6
  314.3 2.9 copy-start.7
  316.1 1.9 copy-start.13
  474.7 5.6 %slice-start.4 = ((f32[73,128,384]{2,1,0:T(8,128)}), f32[6,128,384]{2,1,0:T(8,128)S(1)}, s32[]{:S(2)}) async-start(f32[73,128,384]{2,1,0:T(8,128)} %sum_blocks.1), calls=%async_computation.4 | async-start | bytes 2359296 | tf_op jit(solution)/shard_map/slice | solution.py:858
  484.9 12.7 %slice-start = ((s8[14352384]{0:T(1024)(128)(4,1)}), s8[1769472]{0:T(1024)(128)(4,1)S(1)}, s32[]{:S(2)}) async-start(s8[14352384]{0:T(1024)(128)(4,1)} %bitcast.96), calls=%async_computation | async-start | bytes 3538944
  484.9 12.7 %slice-start.1 = ((s8[14352384]{0:T(1024)(128)(4,1)}), s8[4194304]{0:T(1024)(128)(4,1)S(1)}, s32[]{:S(2)}) async-start(s8[14352384]{0:T(1024)(128)(4,1)} %bitcast.96), calls=%async_computation.1 | async-start | bytes 8388608
  491.8 5.8 %slice-start.2 = ((s8[14352384]{0:T(1024)(128)(4,1)}), s8[4194304]{0:T(1024)(128)(4,1)S(1)}, s32[]{:S(2)}) async-start(s8[14352384]{0:T(1024)(128)(4,1)} %bitcast.96), calls=%async_computation.2 | async-start | bytes 8388608
  494.9 3.9 slice-start.3

commit v2 on v1

--- a/solution.py
+++ b/solution.py
@@ -10,7 +10,7 @@
 
 
 MESH = pl.DeviceIdType.MESH
-BR, BC = 128, 384
+BR, BC = 384, 128
 SPREAD = 2
 SLOTS = 16
 
@@ -266,48 +266,6 @@
         pltpu.SemaphoreType.DMA((7, SLOTS)),
         pltpu.SemaphoreType.REGULAR((3,)),
     ]
-
-
-def sum_kernel(count, grads_in, out, grads, a, b, c, d, sent, got, credit, out_sem, in_sem):
-    pos = Place()
-    load = pltpu.make_async_copy(grads_in, grads, in_sem)
-    load.start()
-    sum_barrier(pos)
-    load.wait()
-
-    def put(block):
-        return pltpu.make_async_copy(grads.at[block], out.at[block], out_sem.at[lax.rem(block, 4)])
-
-    def finish(block):
-        @pl.when(block >= 4)
-        def _():
-            put(block - 4).wait()
-
-        put(block).start()
-
-    tick = make_tick(pos, grads, a, b, c, d, sent, got, credit, count, finish)
-
-    @pl.loop(0, count + 7 * SPREAD)
-    def _(step):
-        tick(step)
-
-    for block in range(count - 4, count):
-        put(block).wait()
-
-
-def sum_blocks(blocks):
-    count = blocks.shape[0]
-    return pl.pallas_call(
-        functools.partial(sum_kernel, count),
-        out_shape=jax.ShapeDtypeStruct(blocks.shape, jnp.float32),
-        in_specs=[pl.BlockSpec(memory_space=pl.ANY)],
-        out_specs=pl.BlockSpec(memory_space=pl.ANY),
-        scratch_shapes=[pltpu.VMEM(blocks.shape, jnp.float32)]
-        + sum_scratch()
-        + [pltpu.SemaphoreType.DMA((4,)), pltpu.SemaphoreType.DMA],
-        compiler_params=pltpu.CompilerParams(collective_id=1, has_side_effects=True, vmem_limit_bytes=60 * 2**20),
-        name="sum_blocks",
-    )(blocks)
 
 
 CR, CC = 64, 384
@@ -695,6 +653,422 @@
     return attention_call(
         backward_attention_kernel, 3, parent, slot_rows, (q, k, v, dmix), scratch, "attend_back"
     )
+
+
+DOWN, UP, OUT, QKV, VEC = 0, 24, 48, 54, 72
+COUNT = 73
+CHUNK = 256
+VEC_ROWS = 54
+
+
+def backward_kernel(
+    fast,
+    parent,
+    slot_rows,
+    inverse,
+    gain,
+    vec_in,
+    tokens_h,
+    hidden_h,
+    d_ffn_h,
+    d_two_h,
+    normed_h,
+    acted_h,
+    slope_own_h,
+    slope_their_h,
+    q_h,
+    k_h,
+    v_h,
+    mixed_h,
+    w_up_own,
+    w_up_their,
+    w_down_own,
+    w_down_their,
+    w_out_own,
+    w_out_their,
+    w_qkv_own,
+    w_qkv_their,
+    g_qkv,
+    g_out,
+    g_up,
+    g_down,
+    g_vec,
+    g_tokens,
+    grads,
+    d_low,
+    hidden,
+    d_res,
+    normed,
+    acc_own,
+    acc_their,
+    a_buf,
+    slope_buf,
+    up_buf,
+    down_buf,
+    d_inner,
+    sums,
+    tokens,
+    mixed,
+    w_out,
+    w_qkv,
+    qkv,
+    d_qkv,
+    d_mixed,
+    colbias,
+    select,
+    kmem,
+    vmem,
+    dkm,
+    dvm,
+    load_sem,
+    chunk_sem,
+    put_sem,
+    *wires,
+):
+    rows, depth = tokens.shape
+    width = mixed.shape[1]
+
+    def fetch(index, source, target):
+        return pltpu.make_async_copy(source, target, load_sem.at[index])
+
+    load_d = fetch(0, d_ffn_h, d_low)
+    load_hidden = fetch(1, hidden_h, hidden)
+    load_two = fetch(2, d_two_h, d_res)
+    load_normed = fetch(3, normed_h, normed)
+    load_mixed = fetch(4, mixed_h.at[:, pl.ds(0, width)], mixed)
+    load_out = [fetch(5 + i, w, w_out.at[i]) for i, w in enumerate((w_out_own, w_out_their))]
+    load_w = [fetch(7 + i, w, w_qkv.at[i]) for i, w in enumerate((w_qkv_own, w_qkv_their))]
+    load_tokens = fetch(9, tokens_h, tokens)
+    load_qkv = [
+        [fetch(10 + 3 * half + i, a.at[:, pl.ds(half * width, width)], qkv.at[i]) for i, a in enumerate((q_h, k_h, v_h))]
+        for half in range(2)
+    ]
+    put_tokens = fetch(16, d_low, g_tokens)
+
+    def load_acted(c):
+        return pltpu.make_async_copy(acted_h.at[:, pl.ds(pl.multiple_of(c * BR, BR), BR)], a_buf.at[lax.rem(c, 2)], chunk_sem.at[0, lax.rem(c, 2)])
+
+    def load_chunk(half, c):
+        slot = lax.rem(c, 2)
+        span = pl.ds(pl.multiple_of(c * CHUNK, CHUNK), CHUNK)
+        slope_h, up_h, down_h = ((slope_own_h, w_up_own, w_down_own), (slope_their_h, w_up_their, w_down_their))[half]
+        return (
+            pltpu.make_async_copy(slope_h.at[:, span], slope_buf.at[slot], chunk_sem.at[1, slot]),
+            pltpu.make_async_copy(up_h.at[:, span], up_buf.at[slot], chunk_sem.at[2, slot]),
+            pltpu.make_async_copy(down_h.at[span, :], down_buf.at[slot], chunk_sem.at[3, slot]),
+        )
+
+    def start(copies):
+        for copy in copies:
+            copy.start()
+
+    def wait(copies):
+        for copy in copies:
+            copy.wait()
+
+    load_d.start()
+    load_acted(0).start()
+    start(load_chunk(0, 0))
+    load_hidden.start()
+    load_two.start()
+    load_normed.start()
+    load_mixed.start()
+    start(load_out)
+    start(load_w)
+    load_tokens.start()
+    start(load_qkv[0])
+
+    def put(block, target):
+        return pltpu.make_async_copy(grads.at[block], target, put_sem.at[lax.rem(block, 8)])
+
+    def wait_put(block):
+        put(block, g_vec).wait()
+
+    def finish(block):
+        @pl.when(block >= 8)
+        def _():
+            wait_put(block - 8)
+
+        def at(row, column):
+            return pl.ds(pl.multiple_of(row, BR), BR), pl.ds(pl.multiple_of(column, BC), BC)
+
+        @pl.when(block < UP)
+        def _():
+            put(block, g_down.at[at(BR * (block // 6), BC * lax.rem(block, 6))]).start()
+
+        @pl.when((block >= UP) & (block < OUT))
+        def _():
+            i = block - UP
+            put(block, g_up.at[at(BR * lax.rem(i // 2, 2), CHUNK * (i // 4) + BC * lax.rem(i, 2))]).start()
+
+        @pl.when((block >= OUT) & (block < QKV))
+        def _():
+            put(block, g_out.at[at(0, BC * (block - OUT))]).start()
+
+        @pl.when((block >= QKV) & (block < VEC))
+        def _():
+            i = block - QKV
+            put(block, g_qkv.at[at(BR * (i // 3), BC * lax.rem(i, 3))]).start()
+
+        @pl.when(block == VEC)
+        def _():
+            put(block, g_vec).start()
+
+    if fast:
+        pos = Place()
+        tick = make_tick(pos, grads, *wires, COUNT, finish)
+        last = COUNT + 7 * SPREAD
+    else:
+
+        def tick(step):
+            finish(step)
+
+        last = COUNT
+    done = [0]
+
+    def ticks(index, each, trips):
+        for i in range(each):
+            tick(done[0] + index * each + i)
+        return trips * each
+
+    grads[VEC] = jnp.zeros((BR, BC), F32)
+    grads[VEC, 36:54] = vec_in[...]
+    acc_own[...] = jnp.zeros(acc_own.shape, F32)
+    acc_their[...] = jnp.zeros(acc_their.shape, F32)
+    sums[...] = jnp.zeros(sums.shape, F32)
+    if fast:
+        sum_barrier(pos)
+
+    load_d.wait()
+
+    @pl.loop(0, 4)
+    def _(c):
+        load_acted(c).wait()
+
+        @pl.when(c < 3)
+        def _():
+            load_acted(c + 1).start()
+
+        for part in range(2):
+            piece = t_mm(a_buf[lax.rem(c, 2)], d_low[:, part * width : (part + 1) * width])
+            for j in range(3):
+                grads[DOWN + 6 * c + 3 * part + j] = piece[:, BC * j : BC * (j + 1)]
+        ticks(c, TICKS[0], 4)
+
+    done[0] += 4 * TICKS[0]
+
+    load_hidden.wait()
+    for half in range(2):
+        acc = (acc_own, acc_their)[half]
+
+        @pl.loop(0, 6)
+        def _(c, half=half, acc=acc):
+            slot = lax.rem(c, 2)
+            wait(load_chunk(half, c))
+
+            @pl.when(c < 5)
+            def _():
+                start(load_chunk(half, c + 1))
+
+            if half == 0:
+
+                @pl.when(c == 5)
+                def _():
+                    start(load_chunk(1, 0))
+
+            d_inner[...] = (mm_t(d_low[...], down_buf[slot]) * slope_buf[slot].astype(F32)).astype(BF)
+            if half == 0:
+                piece = t_mm(hidden[...], d_inner[...])
+                for r in range(2):
+                    for j in range(2):
+                        grads[UP + 4 * c + 2 * r + j] = piece[BR * r : BR * (r + 1), BC * j : BC * (j + 1)]
+                total = jnp.sum(d_inner[...].astype(F32), axis=0, keepdims=True)
+                for j in range(2):
+                    grads[VEC, pl.ds(6 + 2 * c + j, 1), :] = total[:, BC * j : BC * (j + 1)]
+            ticks(c, TICKS[1 + half], 6)
+            for part in range(3):
+                columns = slice(CHUNK * part, CHUNK * (part + 1))
+                acc[:, columns] = acc[:, columns] + mm_t(d_inner[...], up_buf[slot, columns, :])
+
+        done[0] += 6 * TICKS[1 + half]
+
+    load_two.wait()
+    load_normed.wait()
+    tile = 32
+    trips = rows // tile
+
+    @pl.loop(0, trips)
+    def _(i):
+        span = pl.ds(pl.multiple_of(i * tile, tile), tile)
+        total = d_res[span, :] + (acc_own[span, :] + acc_their[span, :])
+        unit = normed[span, :]
+        one = norm_back(total, unit, inverse[span, :], gain[...])
+        d_res[span, :] = one
+        low = one.astype(BF)
+        d_low[span, :] = low
+        for index, value in enumerate((low.astype(F32), total * unit, total)):
+            sums[index] = sums[index] + value.reshape(tile // 8, 8, depth).sum(axis=0)
+
+        @pl.when(lax.rem(i, TICK_TILES) == 0)
+        def _():
+            tick(done[0] + i // TICK_TILES)
+
+    done[0] += -(-trips // TICK_TILES)
+    for index in range(3):
+        total = jnp.sum(sums[index], axis=0, keepdims=True)
+        for j in range(6):
+            grads[VEC, 18 + 6 * index + j : 19 + 6 * index + j, :] = total[:, BC * j : BC * (j + 1)]
+
+    load_mixed.wait()
+    wait(load_out)
+
+    @pl.loop(0, 2)
+    def _(half):
+        d_mixed[half] = mm_t(d_low[...], w_out[half]).astype(BF)
+        piece = t_mm(mixed[...], d_low[:, pl.ds(pl.multiple_of(half * width, BC), width)])
+        for j in range(3):
+            grads[OUT + 3 * half + j] = piece[:, BC * j : BC * (j + 1)]
+        ticks(half, TICKS[3], 2)
+
+    done[0] += 2 * TICKS[3]
+
+    build_masks(parent, lax.axis_index("dp") * SEGS, colbias)
+    build_select(slot_rows, select)
+    wait(load_w)
+    load_tokens.wait()
+    pairs = width // PAIR
+    dka, dva = acc_their.at[:, pl.ds(0, width)], acc_their.at[:, pl.ds(width, width)]
+    for half in range(2):
+        wait(load_qkv[half])
+        q, k, v = (qkv.at[i] for i in range(3))
+        kmem[...] = mm(select[...], k[...]).astype(BF)
+        vmem[...] = mm(select[...], v[...]).astype(BF)
+        acc_their[...] = jnp.zeros(acc_their.shape, F32)
+        dkm[...] = jnp.zeros(dkm.shape, F32)
+        dvm[...] = jnp.zeros(dvm.shape, F32)
+
+        @pl.loop(0, SEGS)
+        def _(s, half=half):
+            for pair in range(pairs):
+                columns = pl.ds(pair * PAIR, PAIR)
+                attend_back_pair(
+                    q, k, v, kmem, vmem, colbias, d_mixed.at[half], d_qkv.at[0], dka, dva, dkm, dvm, s, columns, columns
+                )
+                if pair < TICKS[4 + half]:
+                    tick(done[0] + s * TICKS[4 + half] + pair)
+
+        done[0] += SEGS * TICKS[4 + half]
+        if half == 0:
+            start(load_qkv[1])
+        for pair in range(pairs):
+            columns = pl.ds(pair * PAIR, PAIR)
+            d_qkv[1, :, columns] = ((dka[:, columns] + spread(select[...], dkm[:, columns])) * HD ** (-0.5)).astype(BF)
+            d_qkv[2, :, columns] = (dva[:, columns] + spread(select[...], dvm[:, columns])).astype(BF)
+        if half == 0:
+
+            @pl.loop(0, 3)
+            def _(c):
+                piece = t_mm(tokens[...], d_qkv[c])
+                for r in range(2):
+                    for j in range(3):
+                        grads[QKV + 6 * c + 3 * r + j] = piece[BR * r : BR * (r + 1), BC * j : BC * (j + 1)]
+                columns = pl.ds(pl.multiple_of(c * CHUNK, CHUNK), CHUNK)
+                part = mm_t(d_qkv[0], w_qkv[half, pl.ds(pl.multiple_of(c * CHUNK, CHUNK), CHUNK), :])
+                for i in (1, 2):
+                    part = part + mm_t(d_qkv[i], w_qkv[half, pl.ds(pl.multiple_of(i * depth + c * CHUNK, CHUNK), CHUNK), :])
+                acc_own[:, columns] = part
+                ticks(c, TICKS[6], 3)
+
+            done[0] += 3 * TICKS[6]
+            for index, row in ((0, 0), (2, 3)):
+                total = jnp.sum(d_qkv[index].astype(F32), axis=0, keepdims=True)
+                for j in range(3):
+                    grads[VEC, row + j : row + j + 1, :] = total[:, BC * j : BC * (j + 1)]
+        else:
+
+            @pl.loop(0, 3)
+            def _(c):
+                columns = pl.ds(pl.multiple_of(c * CHUNK, CHUNK), CHUNK)
+                part = mm_t(d_qkv[0], w_qkv[half, pl.ds(pl.multiple_of(c * CHUNK, CHUNK), CHUNK), :])
+                for i in (1, 2):
+                    part = part + mm_t(d_qkv[i], w_qkv[half, pl.ds(pl.multiple_of(i * depth + c * CHUNK, CHUNK), CHUNK), :])
+                d_low[:, columns] = ((acc_own[:, columns] + part) + d_res[:, columns]).astype(BF)
+                ticks(c, TICKS[7], 3)
+
+            done[0] += 3 * TICKS[7]
+            put_tokens.start()
+    assert done[0] <= COUNT
+
+    @pl.loop(done[0], last)
+    def _(step):
+        tick(step)
+
+    for block in range(COUNT - 8, COUNT):
+        wait_put(block)
+    put_tokens.wait()
+
+
+TICKS = (1, 2, 1, 1, 2, 2, 2, 1)
+TICK_TILES = 8
+
+
+def backward(fast, parent, slot_rows, inverse, gain, vec_in, arrays):
+    tokens, acted, mixed = arrays[0], arrays[5], arrays[11]
+    rows, depth = tokens.shape
+    units = acted.shape[1]
+    width = mixed.shape[1] // 2
+    vm = pl.BlockSpec(memory_space=pltpu.VMEM)
+    hbm = pl.BlockSpec(memory_space=pl.ANY)
+    sd = jax.ShapeDtypeStruct
+    return pl.pallas_call(
+        functools.partial(backward_kernel, fast),
+        out_shape=[
+            sd((3 * depth, width), F32),
+            sd((width, depth), F32),
+            sd((depth, units), F32),
+            sd((units, depth), F32),
+            sd((BR, BC), F32),
+            sd((rows, depth), BF),
+        ],
+        in_specs=[pl.BlockSpec(memory_space=pltpu.SMEM), vm, vm, vm, vm] + [hbm] * len(arrays),
+        out_specs=[hbm] * 6,
+        scratch_shapes=[
+            pltpu.VMEM((COUNT, BR, BC), F32),
+            pltpu.VMEM((rows, depth), BF),
+            pltpu.VMEM((rows, depth), BF),
+            pltpu.VMEM((rows, depth), F32),
+            pltpu.VMEM((rows, depth), F32),
+            pltpu.VMEM((rows, depth), F32),
+            pltpu.VMEM((rows, depth), F32),
+            pltpu.VMEM((2, rows, BR), BF),
+            pltpu.VMEM((2, rows, CHUNK), BF),
+            pltpu.VMEM((2, depth, CHUNK), BF),
+            pltpu.VMEM((2, CHUNK, depth), BF),
+            pltpu.VMEM((rows, CHUNK), BF),
+            pltpu.VMEM((3, 8, depth), F32),
+            pltpu.VMEM((rows, depth), BF),
+            pltpu.VMEM((rows, width), BF),
+            pltpu.VMEM((2, width, depth), BF),
+            pltpu.VMEM((2, 3 * depth, width), BF),
+            pltpu.VMEM((3, rows, width), BF),
+            pltpu.VMEM((3, rows, width), BF),
+            pltpu.VMEM((2, rows, width), BF),
+            pltpu.VMEM((SEGS, WIN + MEMP), F32),
+            pltpu.VMEM((MEMP, rows), BF),
+            pltpu.VMEM((MEMP, width), BF),
+            pltpu.VMEM((MEMP, width), BF),
+            pltpu.VMEM((MEMP, width), F32),
+            pltpu.VMEM((MEMP, width), F32),
+            pltpu.SemaphoreType.DMA((17,)),
+            pltpu.SemaphoreType.DMA((4, 2)),
+            pltpu.SemaphoreType.DMA((8,)),
+        ]
+        + (sum_scratch() if fast else []),
+        compiler_params=pltpu.CompilerParams(
+            collective_id=1 if fast else None, has_side_effects=fast, vmem_limit_bytes=67043328
+        ),
+        name="backward",
+    )(parent, slot_rows, inverse, gain, vec_in, *arrays)
 
 
 def halves_swap(own, small):
@@ -817,55 +1191,21 @@
     d_gain_two = jnp.sum(cotangent * normed_two, axis=0)
     d_shift_two = jnp.sum(cotangent, axis=0)
     d_ffn = d_two.astype(BF)
-    d_w_down = t_mm(acted[0], d_ffn)
     d_bias_down = jnp.sum(d_ffn.astype(F32), axis=0)
-    d_inner = [(mm_t(d_ffn, w_down_both[half]) * slope[half]).astype(BF) for half in range(2)]
-    d_w_up = t_mm(hidden_low, d_inner[0])
-    d_bias_up = jnp.sum(d_inner[0].astype(F32), axis=0)
-    d_hidden = d_two + (mm_t(d_inner[0], w_up_both[0]) + mm_t(d_inner[1], w_up_both[1]))
-    d_one = norm_back(d_hidden, normed_one, inverse_one, gain_one)
-    d_gain_one = jnp.sum(d_hidden * normed_one, axis=0)
-    d_shift_one = jnp.sum(d_hidden, axis=0)
-    d_attn = d_one.astype(BF)
-    d_w_out = t_mm(mixed[:, :width], d_attn)
-    d_bias_out = jnp.sum(d_attn.astype(F32), axis=0)
-    d_mixed = jnp.concatenate([mm_t(d_attn, w_out_both[half]).astype(BF) for half in range(2)], axis=1)
-    d_qkv = backward_attention(parent, slot_rows, queries, keys, values, d_mixed)
-    d_w_qkv = [t_mm(tokens, part[:, :width]) for part in d_qkv]
-    d_bias_qv = [jnp.sum(d_qkv[i][:, :width].astype(F32), axis=0) for i in (0, 2)]
-    parts = []
-    for half in range(2):
-        columns = slice(half * width, (half + 1) * width)
-        parts.append(sum(mm_t(d_qkv[i][:, columns], w_qkv_both[half][i]) for i in range(3)))
-    grad_tokens = ((parts[0] + parts[1]) + d_one).astype(BF)
-
-    vectors = [*d_bias_qv, d_bias_up, d_bias_out, d_gain_one, d_shift_one, d_bias_down, d_gain_two, d_shift_two]
-    if fast:
-        flat = jnp.concatenate([v.reshape(-1, width) for v in vectors])
-        flat = jnp.concatenate([flat, jnp.zeros((BR - flat.shape[0], width), F32)])
-        blocks = jnp.concatenate(
-            [
-                split_blocks(d_w_down, BR, BC),
-                split_blocks(d_w_up, BR, BC),
-                split_blocks(d_w_out, BR, BC),
-                *[split_blocks(part, BR, BC) for part in d_w_qkv],
-                flat[None],
-            ]
-        )
-        blocks = sum_blocks(blocks)
-        g_w_down = join_blocks(blocks[:24], *w_down.shape)
-        g_w_up = join_blocks(blocks[24:48], *w_up.shape)
-        g_w_out = join_blocks(blocks[48:54], *w_out.shape)
-        g_w_qkv = blocks[54:72].reshape(w_qkv.shape)
-        flat = blocks[72]
-        sums, row = [], 0
-        for v in vectors:
-            sums.append(flat[row : row + v.size // width].reshape(-1))
-            row += v.size // width
-    else:
-        g_w_down, g_w_up, g_w_out, g_w_qkv, *sums = lax.psum(
-            (d_w_down, d_w_up, d_w_out, jnp.stack(d_w_qkv), *vectors), "dp"
-        )
+    vec_in = jnp.concatenate([v.reshape(-1, BC) for v in (d_bias_down, d_gain_two, d_shift_two)])
+    slope = [part.astype(BF) for part in slope]
+    arrays = (tokens, hidden_low, d_ffn, d_two, normed_one, acted[0], *slope, queries, keys, values, mixed)
+    weights = (*w_up_both, *w_down_both, *w_out_both, own[0], theirs[0])
+    g_w_qkv, g_w_out, g_w_up, g_w_down, flat, grad_tokens = backward(
+        fast, parent, slot_rows, inverse_one, gain_one.reshape(1, -1), vec_in, arrays + weights
+    )
+    if not fast:
+        g_w_qkv, g_w_out, g_w_up, g_w_down, flat = lax.psum((g_w_qkv, g_w_out, g_w_up, g_w_down, flat), "dp")
+    g_w_qkv = g_w_qkv.reshape(w_qkv.shape)
+    sums, row = [], 0
+    for size in (width, width, hidden_units) + (depth,) * 6:
+        sums.append(flat[row : row + size // BC].reshape(-1))
+        row += size // BC
     g_bias_q, g_bias_v, g_bias_up, g_bias_out, g_gain_one, g_shift_one, g_bias_down, g_gain_two, g_shift_two = sums
     return (
         output,

time: 514 us -> 348 us (0.68)
  local copies, waits for them, and re-layouts: 87.8 us -> 23.4 us
  matrix products: 99.3 us -> 35.4 us
  Pallas kernels: 290 us -> 270 us
  other arithmetic: 31 us -> 14.8 us
    dot_general x17 -> x0, matrix products: 61.3 us -> none  [the longest x11 40.8 us: mm_t(): return lax.dot_general(a, b, CONTRACT_LAST, preferred_element_type=F32)]
    pallas_call x2 -> x1, Pallas kernels: 63.5 us -> 15.6 us  [attention_call(): pl.pallas_call(kernel, out_shape=[jax.ShapeDtypeStruct((rows, width), BF)...]
    pallas_call x1, Pallas kernels: 155 us -> 182 us  [backward(): pl.pallas_call(functools.partial(backward_kernel, fast), out_shape=[sd((3...]
    reshape x22 -> x2, local copies, waits for them, and re-layouts: 25.2 us -> 2.7 us  [shards(): sums.append(flat[row:row + size // BC].reshape(-1))]
    unnamed x109 -> x66, local copies, waits for them, and re-layouts: 31.5 us -> 14.6 us
    slice x7 -> x0, local copies, waits for them, and re-layouts: 12.7 us -> none  [the longest x1 6.89 us: shards(): g_w_down = join_blocks(blocks[:24], *w_down.shape)]
    reduce_sum x1, other arithmetic: 14.8 us -> 3.85 us  [shards(): d_bias_down = jnp.sum(d_ffn.astype(F32), axis=0)]
    transpose x3 -> x0, local copies, waits for them, and re-layouts: 9.92 us -> none  [join_blocks(): return blocks.reshape(height // rows, width // columns, rows, columns).tr...]
where the time goes in v2:
time: 348 us; the launch traced here: 344 us
  Pallas kernels  270 us (78%)
  matrix products  35.4 us (10%)
  local copies, waits for them, and re-layouts  23.4 us (7%)
  other arithmetic  14.8 us (4%)
    pallas_call x1, Pallas kernels, backward(): pl.pallas_call(functools.partial(backward_kernel, fast), out_shape=[sd((3...  182 us
    pallas_call x1, Pallas kernels, gather(): pl.pallas_call(gather_kernel, out_shape=[jax.ShapeDtypeStruct(w.shape, w....  71.8 us
    dot_general x12, matrix products, mm(): return jnp.dot(a, b, preferred_element_type=F32)  35.4 us
    pallas_call x1, Pallas kernels, attention_call(): pl.pallas_call(kernel, out_shape=[jax.ShapeDtypeStruct((rows, width), BF)...  15.6 us
    unnamed x66, local copies, waits for them, and re-layouts  14.6 us

profile of v2, /device:TPU:0, one launch (start us, length us, event | category | flops | bytes accessed | tf_op | source)
XLA Modules:
  0.0 344.4 jit_solution(10659165208584733714)
XLA Ops:
  0.7 0.1 pad.14.clone
  0.7 1.3 broadcast_in_dim.5.gain
  2.0 0.8 broadcast_add_fusion
  2.8 0.8 slice_reduce_fusion.1
  3.5 0.7 reshape.138
  4.2 1.4 maximum_maximum_fusion.small
  5.6 0.1 reshape.150
  5.7 0.6 concatenate.18.slot_rows
  6.3 3.8 %fusion.23 = bf16[1184,384]{1,0:T(8,128)(2,1)} fusion(bf16[1184,768]{1,0:T(8,128)(2,1)} %tokens_h.1, f32[384]{0:T(512)S(1)} %get-tuple-element.42, bf16[3,768,384]{2,1,0:T(8,128)(2,1)} %param.17), kind=kOutput, calls=%fused_computation.47 | convolution fusion | flops 699260928 | bytes 3319296 | tf_op jit(solution)/shard_map/dot_general | solution.py:478
  10.1 0.0 copy-done.7
  10.1 1.1 fusion.22
  11.2 2.0 convolution_convert_fusion.1
  13.2 71.8 %gather_weights.1 = (bf16[2304,384]{1,0:T(8,128)(2,1)}, bf16[384,768]{1,0:T(8,128)(2,1)}, bf16[768,1536]{1,0:T(8,128)(2,1)}, bf16[1536,768]{1,0:T(8,128)(2,1)}, f32[8,384]{1,0:T(8,128)}) custom-call(bf16[2304,384]{1,0:T(8,128)(2,1)} %bitcast.61, bf16[384,768]{1,0:T(8,128)(2,1)} %w_out_own.1, bf16[768,1536]{1,0:T(8,128)(2,1)} %w_up_own.1, ...), custom_call_target="tpu_custom_call" | custom-call | tf_op jit(solution)/shard_map/gather_weights/pallas_call | solution.py:451
  85.1 0.8 slice_reduce_fusion
  85.9 0.7 slice.84
  86.6 2.3 fusion.27
  89.0 1.5 pad_maximum_fusion.2.v.v_h
  90.5 1.1 fusion.28
  91.6 0.0 copy-start.16
  91.6 1.1 fusion.26
  92.7 0.1 copy-done.16
  92.8 2.2 pad_maximum_fusion
  95.0 15.6 %attend.1.mixed_h = bf16[1184,768]{1,0:T(8,128)(2,1)} custom-call(s32[8]{0:T(128)} %parent.3, s32[96,1]{1,0:T(8,128)} %concatenate.18.slot_rows, bf16[1184,768]{1,0:T(8,128)(2,1)} %get-tuple-element.66.q.q_h, bf16[1184,768]{1,0:T(8,128)(2,1)} %get-tuple-element.67.k.k_h, bf16[1184,768]{1,0:T(8,128)(2,1)} %pad_maximum_fusion.2.v.v_h), custom_call_target="tpu_custom_call" | custom-call | tf_op jit(solution)/shard_map/attend/pallas_call | solution.py:629
  110.5 0.0 copy-done.8
  110.5 0.0 copy-start.21
  110.5 2.4 fusion.30
  113.0 1.4 fusion.42
  114.4 0.0 copy-start.19
  114.5 0.0 copy-start.23
  114.5 0.6 multiply_reduce_fusion.1
  115.1 1.0 rsqrt.16.inverse
  116.1 0.0 copy-done.23
  116.1 0.7 fusion.21
  116.8 0.9 copy-done.2
  117.8 6.5 %fusion.4 = (bf16[1184,1536]{1,0:T(8,128)(2,1)}, bf16[1184,1536]{1,0:T(8,128)(2,1)S(1)}) fusion(f32[1536]{0:T(1024)S(1)} %copy-done.20, bf16[1184,768]{1,0:T(8,128)(2,1)S(1)} %get-tuple-element.47.hidden_h, bf16[768,1536]{1,0:T(8,128)(2,1)S(1)} %copy-done.2), kind=kOutput, calls=%fused_computation.8 | convolution fusion | flops 2815229952 | bytes 11458560 | tf_op jit(solution)/shard_map/dot_general | solution.py:478
  124.4 3.0 fusion.44
  127.4 0.0 copy-done.6
  127.4 0.0 copy-done.9
  127.4 0.0 copy-done.11
  127.4 0.0 copy-start.12
  127.4 0.0 copy-start.24
  127.4 6.2 %fusion.9 = (bf16[1184,1536]{1,0:T(8,128)(2,1)}, f32[1184,1536]{1,0:T(8,128)S(1)}) fusion(f32[1536]{0:T(1024)S(1)} %add.171, bf16[1184,768]{1,0:T(8,128)(2,1)S(1)} %get-tuple-element.47.hidden_h, bf16[768,1536]{1,0:T(8,128)(2,1)S(1)} %copy-done.11), kind=kOutput, calls=%fused_computation.13 | convolution fusion | flops 2811592704 | bytes 15095808 | tf_op jit(solution)/shard_map/dot_general | solution.py:478
  133.7 4.3 %fusion.43 = (f32[1184]{0:T(1024)S(1)}, f32[1184,768]{1,0:T(8,128)S(1)}) fusion(f32[768]{0:T(1024)S(1)} %copy-done.24, f32[1184,768]{1,0:T(8,128)S(1)} %fusion.44, bf16[1536,768]{1,0:T(8,128)(2,1)S(1)} %copy-done.12, f32[1184,1536]{1,0:T(8,128)S(1)} %get-tuple-element.65, f32[768]{0:T(1024)S(1)} %copy-done.23, ...), kind=kOutput, calls=%fused_computation.97 | convolution fusion | flops 2807954176 | bytes 20559488 | tf_op jit(solution)/shard_map/dot_general | solution.py:478
  137.9 0.0 copy-start.4
  137.9 0.0 copy-start.18
  137.9 0.6 multiply_reduce_fusion
  138.5 0.0 copy-start.22
  138.5 0.9 copy-done.4
  139.4 2.1 fusion.19
  141.6 3.8 %convert_reduce_fusion.1 = (f32[768]{0:T(1024)S(1)}, bf16[1184,768]{1,0:T(8,128)(2,1)}, f32[1184,768]{1,0:T(8,128)}, bf16[1184,768]{1,0:T(8,128)(2,1)}) fusion(f32[1184]{0:T(1024)S(1)} %broadcast_multiply_fusion, f32[1184,768]{1,0:T(8,128)S(1)} %get-tuple-element.63, f32[1184]{0:T(1024)S(1)} %broadcast_multiply_fusion.2, ...), kind=kLoop, calls=%fused_computation.34 | loop fusion | flops 12729600 | bytes 12758528 | tf_op jit(solution)/shard_map/reduce_sum | solution.py:1194
  145.4 0.6 pad_maximum_fusion.3.vec_in
  146.0 182.2 %backward.1 = (f32[2304,384]{1,0:T(8,128)}, f32[384,768]{1,0:T(8,128)}, f32[768,1536]{1,0:T(8,128)}, f32[1536,768]{1,0:T(8,128)}, f32[384,128]{1,0:T(8,128)}, /*index=5*/bf16[1184,768]{1,0:T(8,128)(2,1)}) custom-call(s32[8]{0:T(128)} %parent.3, s32[96,1]{1,0:T(8,128)} %concatenate.18.slot_rows, f32[1184,1]{1,0:T(8,128)} %rsqrt.16.inverse, ...), custom_call_target="tpu_custom_call" | custom-call | tf_op jit(solution)/shard_map/backward/pallas_call | solution.py:1023
  328.2 0.8 slice_bitcast_fusion.8
  329.0 0.6 pad_maximum_fusion.4
  329.6 1.3 slice_bitcast_fusion
  330.9 1.4 slice_bitcast_fusion.1
  332.3 3.0 copy.44
  335.3 1.8 copy.45
  337.1 0.3 copy-done.15
  337.4 1.0 copy.46
  338.4 2.4 copy.47
  340.8 0.8 slice-done
  341.7 0.3 slice-done.1
  342.0 2.2 copy.48
  (50 shorter events, 0.1 us)
Async XLA Ops:
  6.3 3.8 %copy-start.5 = (bf16[1184,768]{1,0:T(8,128)(2,1)S(1)}, bf16[1184,768]{1,0:T(8,128)(2,1)}, u32[]{:S(2)}) copy-start(bf16[1184,768]{1,0:T(8,128)(2,1)} %tokens_h.1) | copy-start | bytes 5455876
  6.3 3.8 %copy-start.7 = (bf16[3,768,384]{2,1,0:T(8,128)(2,1)S(1)}, bf16[3,768,384]{2,1,0:T(8,128)(2,1)}, u32[]{:S(2)}) copy-start(bf16[3,768,384]{2,1,0:T(8,128)(2,1)} %param.17) | copy-start | bytes 5308420
  86.6 2.3 copy-start.17
  86.6 3.8 %copy-start.14 = (bf16[2304,384]{1,0:T(8,128)(2,1)S(1)}, bf16[2304,384]{1,0:T(8,128)(2,1)}, u32[]{:S(2)}) copy-start(bf16[2304,384]{1,0:T(8,128)(2,1)} %get-tuple-element.25.w_qkv_their) | copy-start | bytes 5308420
  91.6 1.2 copy-start.16
  94.9 15.6 %copy-start.8 = (bf16[384,768]{1,0:T(8,128)(2,1)S(1)}, bf16[384,768]{1,0:T(8,128)(2,1)}, u32[]{:S(2)}) copy-start(bf16[384,768]{1,0:T(8,128)(2,1)} %w_out_own.1) | copy-start | bytes 1769476
  110.5 2.4 copy-start
  110.5 2.5 copy-start.13
  110.5 2.5 copy-start.21
  114.4 1.7 copy-start.19
  114.5 1.7 copy-start.23
  116.1 1.7 copy-start.2
  116.1 1.7 copy-start.20
  116.8 10.6 %copy-start.6 = (bf16[1184,768]{1,0:T(8,128)(2,1)}, bf16[1184,768]{1,0:T(8,128)(2,1)S(1)}, u32[]{:S(2)}) copy-start(bf16[1184,768]{1,0:T(8,128)(2,1)S(1)} %get-tuple-element.47.hidden_h) | copy-start | bytes 5455876
  116.8 16.8 %copy-start.1 = (f32[1184,768]{1,0:T(8,128)}, f32[1184,768]{1,0:T(8,128)S(1)}, u32[]{:S(2)}) copy-start(f32[1184,768]{1,0:T(8,128)S(1)} %get-tuple-element.48.normed_h) | copy-start | bytes 10911748
  117.8 6.6 %copy-start.3 = (bf16[1536,768]{1,0:T(8,128)(2,1)S(1)}, bf16[1536,768]{1,0:T(8,128)(2,1)}, u32[]{:S(2)}) copy-start(bf16[1536,768]{1,0:T(8,128)(2,1)} %w_down_own.1) | copy-start | bytes 7077892
  124.3 3.1 copy-start.9
  124.4 3.1 copy-start.11
  127.4 6.2 %copy-start.12 = (bf16[1536,768]{1,0:T(8,128)(2,1)S(1)}, bf16[1536,768]{1,0:T(8,128)(2,1)}, u32[]{:S(2)}) copy-start(bf16[1536,768]{1,0:T(8,128)(2,1)} %get-tuple-element.29.w_down_their) | copy-start | bytes 7077892
  127.4 6.2 %copy-start.24 = (f32[768]{0:T(1024)S(1)}, f32[768]{0:T(1024)}, u32[]{:S(2)}) copy-start(f32[768]{0:T(1024)} %param.26) | copy-start | bytes 9220
  137.9 1.5 copy-start.4
  137.9 1.5 copy-start.18
  138.5 3.0 copy-start.22
  328.2 7.1 %copy-start.10 = (f32[2304,384]{1,0:T(8,128)S(1)}, f32[2304,384]{1,0:T(8,128)}, u32[]{:S(2)}) copy-start(f32[2304,384]{1,0:T(8,128)} %get-tuple-element.31) | copy-start | bytes 10616836
  332.3 6.1 %slice-start.2 = ((s8[4718592]{0:T(1024)(128)(4,1)}), s8[4194304]{0:T(1024)(128)(4,1)S(1)}, s32[]{:S(2)}) async-start(s8[4718592]{0:T(1024)(128)(4,1)} %bitcast.65), calls=%async_computation.2 | async-start | bytes 8388608
  335.3 2.1 copy-start.15
  335.3 3.1 slice-start.3
  337.4 4.3 %slice-start = ((s8[4718592]{0:T(1024)(128)(4,1)}), s8[4194304]{0:T(1024)(128)(4,1)S(1)}, s32[]{:S(2)}) async-start(s8[4718592]{0:T(1024)(128)(4,1)} %bitcast.63), calls=%async_computation | async-start | bytes 8388608
  338.4 3.5 %slice-start.1 = ((s8[4718592]{0:T(1024)(128)(4,1)}), s8[524288]{0:T(1024)(128)(4,1)S(1)}, s32[]{:S(2)}) async-start(s8[4718592]{0:T(1024)(128)(4,1)} %bitcast.63), calls=%async_computation.1 | async-start | bytes 1048576

commit v3 on v2

--- a/solution.py
+++ b/solution.py
@@ -270,6 +270,7 @@
 
 CR, CC = 64, 384
 CHUNKS = 24
+RELAY = 1
 BF = jnp.bfloat16
 
 
@@ -399,15 +400,15 @@
         unpack(chunk)
 
     def tick(step):
-        guarded(step - 6, fourth)
-        guarded(step - 4, third)
-        guarded(step - 2, second)
+        guarded(step - 3 * RELAY, fourth)
+        guarded(step - 2 * RELAY, third)
+        guarded(step - RELAY, second)
         guarded(step, first)
 
     return stage_own, send_own, tick
 
 
-GATHER_TICKS = CHUNKS + 6
+GATHER_TICKS = CHUNKS + 3 * RELAY
 
 
 def gather_scratch():
@@ -428,35 +429,6 @@
         device_id={"tensor": 1 - lax.axis_index("tensor")},
         device_id_type=MESH,
     )
-
-
-def gather_kernel(a, b, c, d, small, oa, ob, oc, od, small_out, staged, landed, sent, got, sems):
-    pos = Place()
-    stage_own, send_own, tick = make_gather(pos, (a, b, c, d), (oa, ob, oc, od), staged, landed, sent, got)
-    stage_own()
-    gather_barrier(pos, 1 - lax.axis_index("tensor"))
-    swap = swap_small(small, small_out, sems)
-    swap.start()
-    send_own()
-
-    @pl.loop(0, GATHER_TICKS)
-    def _(step):
-        tick(step)
-
-    swap.wait()
-
-
-def gather(ws):
-    v = pl.BlockSpec(memory_space=pltpu.VMEM)
-    return pl.pallas_call(
-        gather_kernel,
-        out_shape=[jax.ShapeDtypeStruct(w.shape, w.dtype) for w in ws],
-        in_specs=[v] * 5,
-        out_specs=[v] * 5,
-        scratch_shapes=gather_scratch() + [pltpu.SemaphoreType.DMA((2,))],
-        compiler_params=pltpu.CompilerParams(collective_id=0, has_side_effects=True, vmem_limit_bytes=60 * 2**20),
-        name="gather_weights",
-    )(*ws)
 
 
 HD = 64
@@ -655,6 +627,350 @@
     )
 
 
+def norm_stats(values):
+    centered = values - jnp.mean(values, axis=-1, keepdims=True)
+    inverse = lax.rsqrt(jnp.mean(centered * centered, axis=-1, keepdims=True) + EPSILON)
+    return centered * inverse, inverse
+
+
+def norm_back(grad, normed, inverse, gain):
+    scaled = grad * gain
+    return inverse * (
+        scaled
+        - jnp.mean(scaled, axis=-1, keepdims=True)
+        - normed * jnp.mean(scaled * normed, axis=-1, keepdims=True)
+    )
+
+
+def gelu_parts(inner):
+    phi = 0.5 + 0.5 * lax.erf(inner * (0.5**0.5))
+    density = jnp.exp(-0.5 * inner * inner) * (2.0 * jnp.pi) ** -0.5
+    return (inner * phi).astype(BF), (phi + inner * density).astype(BF)
+
+
+TILE = 128
+
+
+def row_tiles(rows, body):
+    full = rows // TILE
+
+    @pl.loop(0, full)
+    def _(i):
+        body(pl.ds(pl.multiple_of(i * TILE, TILE), TILE))
+
+    if rows % TILE:
+        body(pl.ds(full * TILE, rows % TILE))
+
+
+def forward_kernel(
+    fast,
+    parent,
+    slot_rows,
+    small,
+    rows_in,
+    tokens_h,
+    grad_h,
+    own_qkv,
+    own_out,
+    own_up,
+    own_down,
+    *rest,
+):
+    count = 0 if fast else 5
+    given, outs, rest = rest[:count], rest[count : count + 16], rest[count + 16 :]
+    (
+        output_h,
+        their_qkv_h,
+        their_out_h,
+        their_up_h,
+        their_down_h,
+        qkv_h,
+        mixed_h,
+        normed_h,
+        inverse,
+        hidden_h,
+        acted_h,
+        slope_own_h,
+        slope_their_h,
+        d_two_h,
+        d_ffn_h,
+        vec,
+    ) = outs
+    (
+        tokens,
+        their_qkv,
+        their_out,
+        their_up,
+        their_down,
+        small_their,
+        qkv,
+        mixed,
+        normed,
+        hidden,
+        acc_own,
+        acc_their,
+        acted,
+        slopes,
+        colbias,
+        select,
+        kmem,
+        vmem,
+        sums,
+        io_sem,
+        slope_sem,
+        *wires,
+    ) = rest
+    rows, depth = tokens.shape
+    width = mixed.shape[2]
+    theirs = (their_qkv, their_out, their_up, their_down)
+    own = (own_qkv, own_out, own_up, own_down)
+
+    def move(index, source, target):
+        return pltpu.make_async_copy(source, target, io_sem.at[index])
+
+    load_tokens = move(0, tokens_h, tokens)
+    load_grad = move(1, grad_h, tokens)
+    put_qkv = move(2, qkv, qkv_h)
+    put_mixed = move(3, mixed.at[0], mixed_h)
+    put_normed = move(4, normed, normed_h)
+    put_hidden = move(5, hidden, hidden_h)
+    put_acted = move(6, acted, acted_h)
+    put_two = move(7, acc_own, d_two_h)
+    put_ffn = move(8, hidden, d_ffn_h)
+    put_output = move(9, tokens, output_h)
+    put_theirs = [
+        move(10 + i, ref, target)
+        for i, (ref, target) in enumerate(zip(theirs, (their_qkv_h, their_out_h, their_up_h, their_down_h)))
+    ]
+    load_tokens.start()
+    done = [0]
+    if fast:
+        pos = Place()
+        small_sem, *wires = wires
+        stage_own, send_own, tick = make_gather(pos, own, theirs, *wires)
+        stage_own()
+        gather_barrier(pos, 1 - lax.axis_index("tensor"))
+        swap = swap_small(small, small_their, small_sem)
+        swap.start()
+        send_own()
+    else:
+        copies = [move(10 + i, a, b) for i, (a, b) in enumerate(zip(given, theirs + (small_their,)))]
+        for copy in copies:
+            copy.start()
+        for copy in copies:
+            copy.wait()
+
+        def tick(step):
+            pass
+
+    def ticks(index, each, trips):
+        for i in range(each):
+            tick(done[0] + index * each + i)
+
+    def until(count):
+        if done[0] < count:
+
+            @pl.loop(done[0], count)
+            def _(step):
+                tick(step)
+
+            done[0] = count
+
+    build_masks(parent, lax.axis_index("dp") * SEGS, colbias)
+    build_select(slot_rows, select)
+    load_tokens.wait()
+    pairs = width // PAIR
+    for half in range(2):
+        weights = (own_qkv, their_qkv)[half]
+        table = (small, small_their)[half]
+        if half == 1:
+            until(BOUNDS[0][1] + 3 * RELAY)
+            if fast:
+                swap.wait()
+
+        @pl.loop(0, 3)
+        def _(c, half=half, weights=weights, table=table):
+            part = mm(tokens[...], weights[pl.ds(pl.multiple_of(c * depth, depth), depth), :])
+            qkv[half, c] = (part + table[pl.ds(c, 1), :]).astype(BF)
+            ticks(c, GATHER[2 * half], 3)
+
+        done[0] += 3 * GATHER[2 * half]
+        q, k, v = (qkv.at[half, i] for i in range(3))
+        kmem[...] = mm(select[...], k[...]).astype(BF)
+        vmem[...] = mm(select[...], v[...]).astype(BF)
+
+        @pl.loop(0, SEGS)
+        def _(s, half=half, q=q, k=k, v=v):
+            for pair in range(pairs):
+                attend_pair(q, k, v, kmem, vmem, colbias, mixed.at[half], s, pl.ds(pair * PAIR, PAIR))
+                if pair < GATHER[2 * half + 1]:
+                    tick(done[0] + s * GATHER[2 * half + 1] + pair)
+
+        done[0] += SEGS * GATHER[2 * half + 1]
+    put_qkv.start()
+    put_mixed.start()
+    until(BOUNDS[1][1] + 3 * RELAY)
+
+    @pl.loop(0, 3)
+    def _(n):
+        columns = pl.ds(pl.multiple_of(n * CHUNK, CHUNK), CHUNK)
+        acc_own[:, columns] = mm(mixed[0], own_out[:, columns]) + mm(mixed[1], their_out[:, columns])
+        ticks(n, GATHER[4], 3)
+
+    done[0] += 3 * GATHER[4]
+
+    def norm_one(span):
+        resid = tokens[span, :].astype(F32) + (acc_own[span, :] + rows_in[0:1, :])
+        unit, scale = norm_stats(resid)
+        normed[span, :] = unit
+        inverse[span, :] = scale
+        hidden[span, :] = (unit * rows_in[1:2, :] + rows_in[2:3, :]).astype(BF)
+
+    row_tiles(rows, norm_one)
+    load_grad.start()
+    put_normed.start()
+    put_hidden.start()
+
+    for half in range(2):
+        up, down = ((own_up, own_down), (their_up, their_down))[half]
+        table = (small, small_their)[half]
+        slope_h = (slope_own_h, slope_their_h)[half]
+        acc = (acc_own, acc_their)[half]
+
+        def put_slope(c, slope_h=slope_h):
+            span = pl.ds(pl.multiple_of(c * CHUNK, CHUNK), CHUNK)
+            return pltpu.make_async_copy(slopes.at[lax.rem(c, 2)], slope_h.at[:, span], slope_sem.at[lax.rem(c, 2)])
+
+        if half == 1:
+            until(BOUNDS[2][1] + 3 * RELAY)
+            put_acted.wait()
+            put_slope(4).wait()
+            put_slope(5).wait()
+
+        @pl.loop(0, 6)
+        def _(c, half=half, up=up, table=table, put_slope=put_slope):
+            span = pl.ds(pl.multiple_of(c * CHUNK, CHUNK), CHUNK)
+
+            @pl.when(c >= 2)
+            def _():
+                put_slope(c - 2).wait()
+
+            bias = table[pl.ds(3 + c, 1), 0:CHUNK]
+            act, steep = gelu_parts(mm(hidden[...], up[:, span]) + bias)
+            acted[:, span] = act
+            slopes[lax.rem(c, 2)] = steep
+            put_slope(c).start()
+            ticks(c, GATHER[5 + 2 * half], 6)
+
+        done[0] += 6 * GATHER[5 + 2 * half]
+        if half == 0:
+            put_acted.start()
+        else:
+            until(BOUNDS[3][1] + 3 * RELAY)
+            if fast:
+                for copy in put_theirs:
+                    copy.start()
+
+        @pl.loop(0, 3)
+        def _(n, half=half, down=down, acc=acc):
+            columns = pl.ds(pl.multiple_of(n * CHUNK, CHUNK), CHUNK)
+            acc[:, columns] = mm(acted[...], down[:, columns])
+            ticks(n, GATHER[6 + 2 * half], 3)
+
+        done[0] += 3 * GATHER[6 + 2 * half]
+    put_slope(4).wait()
+    put_slope(5).wait()
+
+    load_grad.wait()
+    put_hidden.wait()
+    sums[...] = jnp.zeros(sums.shape, F32)
+
+    def norm_two(span):
+        first = normed[span, :] * rows_in[1:2, :] + rows_in[2:3, :]
+        resid = first + ((acc_own[span, :] + acc_their[span, :]) + rows_in[3:4, :])
+        unit, scale = norm_stats(resid)
+        grad = tokens[span, :].astype(F32)
+        tokens[span, :] = (unit * rows_in[4:5, :] + rows_in[5:6, :]).astype(BF)
+        back = norm_back(grad, unit, scale, rows_in[4:5, :])
+        acc_own[span, :] = back
+        low = back.astype(BF)
+        hidden[span, :] = low
+        for index, value in enumerate((low.astype(F32), grad * unit, grad)):
+            sums[index] = sums[index] + value.reshape(-1, 8, depth).sum(axis=0)
+
+    row_tiles(rows, norm_two)
+    put_two.start()
+    put_ffn.start()
+    put_output.start()
+    for index in range(3):
+        total = jnp.sum(sums[index], axis=0, keepdims=True)
+        for j in range(6):
+            vec[6 * index + j : 6 * index + j + 1, :] = total[:, BC * j : BC * (j + 1)]
+    for copy in (put_qkv, put_mixed, put_normed, put_two, put_ffn, put_output):
+        copy.wait()
+    if fast:
+        for copy in put_theirs:
+            copy.wait()
+
+
+GATHER = (0, 1, 1, 1, 0, 1, 0, 0, 0)
+
+
+def forward(fast, parent, slot_rows, small, rows_in, tokens, grad_out, own, given):
+    rows, depth = tokens.shape
+    width = own[0].shape[1]
+    units = own[2].shape[1]
+    vm = pl.BlockSpec(memory_space=pltpu.VMEM)
+    hbm = pl.BlockSpec(memory_space=pl.ANY)
+    sd = jax.ShapeDtypeStruct
+    out_shape = [
+        sd((rows, depth), BF),
+        *[sd(w.shape, BF) for w in own],
+        sd((2, 3, rows, width), BF),
+        sd((rows, width), BF),
+        sd((rows, depth), F32),
+        sd((rows, 1), F32),
+        sd((rows, depth), BF),
+        sd((rows, units), BF),
+        sd((rows, units), BF),
+        sd((rows, units), BF),
+        sd((rows, depth), F32),
+        sd((rows, depth), BF),
+        sd((18, BC), F32),
+    ]
+    return pl.pallas_call(
+        functools.partial(forward_kernel, fast),
+        out_shape=out_shape,
+        in_specs=[pl.BlockSpec(memory_space=pltpu.SMEM), vm, vm, vm, hbm, hbm] + [vm] * 4 + [hbm] * len(given),
+        out_specs=[hbm] * 8 + [vm] + [hbm] * 6 + [vm],
+        scratch_shapes=[
+            pltpu.VMEM((rows, depth), BF),
+            *[pltpu.VMEM(w.shape, BF) for w in own],
+            pltpu.VMEM(small.shape, F32),
+            pltpu.VMEM((2, 3, rows, width), BF),
+            pltpu.VMEM((2, rows, width), BF),
+            pltpu.VMEM((rows, depth), F32),
+            pltpu.VMEM((rows, depth), BF),
+            pltpu.VMEM((rows, depth), F32),
+            pltpu.VMEM((rows, depth), F32),
+            pltpu.VMEM((rows, units), BF),
+            pltpu.VMEM((2, rows, CHUNK), BF),
+            pltpu.VMEM((SEGS, WIN + MEMP), F32),
+            pltpu.VMEM((MEMP, rows), BF),
+            pltpu.VMEM((MEMP, width), BF),
+            pltpu.VMEM((MEMP, width), BF),
+            pltpu.VMEM((3, 8, depth), F32),
+            pltpu.SemaphoreType.DMA((15,)),
+            pltpu.SemaphoreType.DMA((2,)),
+        ]
+        + ([pltpu.SemaphoreType.DMA((2,))] + gather_scratch() if fast else []),
+        compiler_params=pltpu.CompilerParams(
+            collective_id=0 if fast else None, has_side_effects=fast, vmem_limit_bytes=67043328
+        ),
+        name="forward",
+    )(parent, slot_rows, small, rows_in, tokens, grad_out, *own, *given)
+
+
 DOWN, UP, OUT, QKV, VEC = 0, 24, 48, 54, 72
 COUNT = 73
 CHUNK = 256
@@ -676,9 +992,7 @@
     acted_h,
     slope_own_h,
     slope_their_h,
-    q_h,
-    k_h,
-    v_h,
+    qkv_h,
     mixed_h,
     w_up_own,
     w_up_their,
@@ -735,15 +1049,12 @@
     load_hidden = fetch(1, hidden_h, hidden)
     load_two = fetch(2, d_two_h, d_res)
     load_normed = fetch(3, normed_h, normed)
-    load_mixed = fetch(4, mixed_h.at[:, pl.ds(0, width)], mixed)
+    load_mixed = fetch(4, mixed_h, mixed)
     load_out = [fetch(5 + i, w, w_out.at[i]) for i, w in enumerate((w_out_own, w_out_their))]
     load_w = [fetch(7 + i, w, w_qkv.at[i]) for i, w in enumerate((w_qkv_own, w_qkv_their))]
     load_tokens = fetch(9, tokens_h, tokens)
-    load_qkv = [
-        [fetch(10 + 3 * half + i, a.at[:, pl.ds(half * width, width)], qkv.at[i]) for i, a in enumerate((q_h, k_h, v_h))]
-        for half in range(2)
-    ]
-    put_tokens = fetch(16, d_low, g_tokens)
+    load_qkv = [fetch(10 + half, qkv_h.at[half], qkv) for half in range(2)]
+    put_tokens = fetch(12, d_low, g_tokens)
 
     def load_acted(c):
         return pltpu.make_async_copy(acted_h.at[:, pl.ds(pl.multiple_of(c * BR, BR), BR)], a_buf.at[lax.rem(c, 2)], chunk_sem.at[0, lax.rem(c, 2)])
@@ -776,7 +1087,7 @@
     start(load_out)
     start(load_w)
     load_tokens.start()
-    start(load_qkv[0])
+    load_qkv[0].start()
 
     def put(block, target):
         return pltpu.make_async_copy(grads.at[block], target, put_sem.at[lax.rem(block, 8)])
@@ -939,7 +1250,7 @@
     pairs = width // PAIR
     dka, dva = acc_their.at[:, pl.ds(0, width)], acc_their.at[:, pl.ds(width, width)]
     for half in range(2):
-        wait(load_qkv[half])
+        load_qkv[half].wait()
         q, k, v = (qkv.at[i] for i in range(3))
         kmem[...] = mm(select[...], k[...]).astype(BF)
         vmem[...] = mm(select[...], v[...]).astype(BF)
@@ -959,7 +1270,7 @@
 
         done[0] += SEGS * TICKS[4 + half]
         if half == 0:
-            start(load_qkv[1])
+            load_qkv[1].start()
         for pair in range(pairs):
             columns = pl.ds(pair * PAIR, PAIR)
             d_qkv[1, :, columns] = ((dka[:, columns] + spread(select[...], dkm[:, columns])) * HD ** (-0.5)).astype(BF)
@@ -1013,10 +1324,10 @@
 
 
 def backward(fast, parent, slot_rows, inverse, gain, vec_in, arrays):
-    tokens, acted, mixed = arrays[0], arrays[5], arrays[11]
+    tokens, acted, mixed = arrays[0], arrays[5], arrays[9]
     rows, depth = tokens.shape
     units = acted.shape[1]
-    width = mixed.shape[1] // 2
+    width = mixed.shape[1]
     vm = pl.BlockSpec(memory_space=pltpu.VMEM)
     hbm = pl.BlockSpec(memory_space=pl.ANY)
     sd = jax.ShapeDtypeStruct
@@ -1059,7 +1370,7 @@
             pltpu.VMEM((MEMP, width), BF),
             pltpu.VMEM((MEMP, width), F32),
             pltpu.VMEM((MEMP, width), F32),
-            pltpu.SemaphoreType.DMA((17,)),
+            pltpu.SemaphoreType.DMA((13,)),
             pltpu.SemaphoreType.DMA((4, 2)),
             pltpu.SemaphoreType.DMA((8,)),
         ]
@@ -1079,45 +1390,6 @@
         return (arrived * unit).astype(array.dtype)
 
     return tuple(other(array) for array in own) + (other(small),)
-
-
-def norm_stats(values):
-    centered = values - jnp.mean(values, axis=-1, keepdims=True)
-    inverse = lax.rsqrt(jnp.mean(centered * centered, axis=-1, keepdims=True) + EPSILON)
-    return centered * inverse, inverse
-
-
-def norm_back(grad, normed, inverse, gain):
-    scaled = grad * gain
-    return inverse * (
-        scaled
-        - jnp.mean(scaled, axis=-1, keepdims=True)
-        - normed * jnp.mean(scaled * normed, axis=-1, keepdims=True)
-    )
-
-
-def gelu_parts(inner):
-    phi = 0.5 * (1.0 + lax.erf(inner * (0.5**0.5)))
-    density = jnp.exp(-0.5 * inner * inner) * (2.0 * jnp.pi) ** -0.5
-    return (inner * phi).astype(BF), phi + inner * density
-
-
-def split_blocks(array, rows, columns):
-    height, width = array.shape
-    return (
-        array.reshape(height // rows, rows, width // columns, columns)
-        .transpose(0, 2, 1, 3)
-        .reshape(-1, rows, columns)
-    )
-
-
-def join_blocks(blocks, height, width):
-    count, rows, columns = blocks.shape
-    return (
-        blocks.reshape(height // rows, width // columns, rows, columns)
-        .transpose(0, 2, 1, 3)
-        .reshape(height, width)
-    )
 
 
 def shards(
@@ -1142,62 +1414,36 @@
     depth, width = w_qkv.shape[1:]
     hidden_units = w_up.shape[1]
     own = (w_qkv.reshape(3 * depth, width), w_out, w_up, w_down)
-    small = jnp.concatenate(
-        [bias_qv, bias_up.reshape(-1, width), jnp.zeros((8 - 2 - hidden_units // width, width), F32)]
+    table = jnp.pad(bias_up.reshape(-1, CHUNK), ((0, 0), (0, width - CHUNK)))
+    small = jnp.concatenate([bias_qv[:1], jnp.zeros((1, width), F32), bias_qv[1:], table])
+    small = jnp.pad(small, ((0, 16 - small.shape[0]), (0, 0)))
+    given = () if fast else halves_swap(own, small)
+    slot_rows = mem_slots + jnp.arange(SEGS, dtype=jnp.int32)[:, None] * SEG
+    slot_rows = jnp.pad(slot_rows.reshape(-1, 1), ((0, MEMP - MEMW * SEGS), (0, 0)), constant_values=-1)
+    rows_in = jnp.stack(
+        [bias_out, gain_one, shift_one, bias_down, gain_two, shift_two, jnp.zeros_like(gain_one), jnp.zeros_like(gain_one)]
     )
-    if fast:
-        theirs = gather((*own, small))
-    else:
-        theirs = halves_swap(own, small)
-    *theirs, small_theirs = theirs
-    w_qkv_both = [own[0].reshape(w_qkv.shape), theirs[0].reshape(w_qkv.shape)]
-    w_out_both, w_up_both, w_down_both = ([own[i], theirs[i]] for i in (1, 2, 3))
-    bias_qv_both = [bias_qv, small_theirs[:2]]
-    bias_up_both = [bias_up, small_theirs[2 : 2 + hidden_units // width].reshape(-1)]
-
-    offsets = jnp.arange(SEGS, dtype=jnp.int32)[:, None] * SEG
-    slot_rows = (mem_slots + offsets).reshape(-1, 1)
-    slot_rows = jnp.concatenate([slot_rows, jnp.full((MEMP - slot_rows.shape[0], 1), -1, jnp.int32)])
-
-    def project(index, bias):
-        parts = []
-        for half in range(2):
-            part = mm(tokens, w_qkv_both[half][index])
-            if bias is not None:
-                part = part + bias_qv_both[half][bias]
-            parts.append(part.astype(BF))
-        return jnp.concatenate(parts, axis=1)
-
-    queries, keys, values = project(0, 0), project(1, None), project(2, 1)
-    mixed = forward_attention(parent, slot_rows, queries, keys, values)
-    attended = mm(mixed[:, :width], w_out_both[0]) + mm(mixed[:, width:], w_out_both[1])
-    resid_one = tokens.astype(F32) + (attended + bias_out)
-    normed_one, inverse_one = norm_stats(resid_one)
-    hidden = normed_one * gain_one + shift_one
-    hidden_low = hidden.astype(BF)
-    acted, slope, summed = [], [], []
-    for half in range(2):
-        inner = mm(hidden_low, w_up_both[half]) + bias_up_both[half]
-        act, steep = gelu_parts(inner)
-        acted.append(act)
-        slope.append(steep)
-        summed.append(mm(act, w_down_both[half]))
-    resid_two = hidden + ((summed[0] + summed[1]) + bias_down)
-    normed_two, inverse_two = norm_stats(resid_two)
-    output = (normed_two * gain_two + shift_two).astype(BF)
-
-    cotangent = grad_out.astype(F32)
-    d_two = norm_back(cotangent, normed_two, inverse_two, gain_two)
-    d_gain_two = jnp.sum(cotangent * normed_two, axis=0)
-    d_shift_two = jnp.sum(cotangent, axis=0)
-    d_ffn = d_two.astype(BF)
-    d_bias_down = jnp.sum(d_ffn.astype(F32), axis=0)
-    vec_in = jnp.concatenate([v.reshape(-1, BC) for v in (d_bias_down, d_gain_two, d_shift_two)])
-    slope = [part.astype(BF) for part in slope]
-    arrays = (tokens, hidden_low, d_ffn, d_two, normed_one, acted[0], *slope, queries, keys, values, mixed)
-    weights = (*w_up_both, *w_down_both, *w_out_both, own[0], theirs[0])
+    (
+        output,
+        *theirs,
+        qkv,
+        mixed,
+        normed,
+        inverse,
+        hidden_low,
+        acted,
+        slope_own,
+        slope_their,
+        d_two,
+        d_ffn,
+        vec,
+    ) = forward(fast, parent, slot_rows, small, rows_in, tokens, grad_out, own, given)
+    if not fast:
+        theirs = given[:4]
+    arrays = (tokens, hidden_low, d_ffn, d_two, normed, acted, slope_own, slope_their, qkv, mixed)
+    weights = tuple(w[i] for i in (2, 3, 1, 0) for w in (own, theirs))
     g_w_qkv, g_w_out, g_w_up, g_w_down, flat, grad_tokens = backward(
-        fast, parent, slot_rows, inverse_one, gain_one.reshape(1, -1), vec_in, arrays + weights
+        fast, parent, slot_rows, inverse, gain_one.reshape(1, -1), vec, arrays + weights
     )
     if not fast:
         g_w_qkv, g_w_out, g_w_up, g_w_down, flat = lax.psum((g_w_qkv, g_w_out, g_w_up, g_w_down, flat), "dp")

time: 348 us -> 350 us (level)
  Pallas kernels: 270 us -> 322 us
  matrix products: 35.4 us -> 0 us
  other arithmetic: 14.8 us -> 1.42 us
    pallas_call x2 -> x1, Pallas kernels: 87.4 us -> 141 us  [forward(): pl.pallas_call(functools.partial(forward_kernel, fast), out_shape=out_sha...]
    dot_general x12 -> x0, matrix products: 35.4 us -> none  [mm(): return jnp.dot(a, b, preferred_element_type=F32)]
    reduce_sum x4 -> x0, other arithmetic: 7.12 us -> none  [the longest x1 3.85 us: shards(): d_bias_down = jnp.sum(d_ffn.astype(F32), axis=0)]
    concatenate x4 -> x1, other arithmetic: 5.63 us -> 0.08 us  [shards(): jnp.concatenate([bias_qv[:1], jnp.zeros((1, width), F32), bias_qv[1:], ta...]
    another operation x0 -> x9, local copies, waits for them, and re-layouts: none -> 4.79 us  [the longest x8 4.78 us: shards(): jnp.stack([bias_out, gain_one, shift_one, bias_down, gain_two, shift_two,...]
    unnamed x66 -> x23, local copies, waits for them, and re-layouts: 14.6 us -> 15 us
where the time goes in v3:
time: 350 us
  Pallas kernels  322 us (92%)
  local copies, waits for them, and re-layouts  25.4 us (7%)
    pallas_call x1, Pallas kernels, backward(): pl.pallas_call(functools.partial(backward_kernel, fast), out_shape=[sd((3...  181 us
    pallas_call x1, Pallas kernels, forward(): pl.pallas_call(functools.partial(forward_kernel, fast), out_shape=out_sha...  141 us
    unnamed x23, local copies, waits for them, and re-layouts  15 us

profile of v3, /device:TPU:0, one launch (start us, length us, event | category | flops | bytes accessed | tf_op | source)
XLA Modules:
  0.0 349.5 jit_solution(3765285874701824)
XLA Ops:
  0.6 0.1 pad.18.clone
  0.7 0.7 stack.28.gain
  1.4 0.0 copy-start.3
  1.4 0.7 stack.27
  2.1 0.7 stack.29
  2.8 0.7 stack.30
  3.5 0.7 stack.31
  4.2 0.7 stack.32
  4.9 0.8 fusion
  5.6 0.8 broadcast_add_fusion
  6.4 0.0 copy-done.3
  6.4 0.6 stack.34.rows_in
  7.0 0.7 reshape.68
  7.7 0.1 select_maximum_fusion
  7.8 0.6 pad.14.small
  8.4 0.1 reshape.78
  8.5 0.6 pad.12.slot_rows
  9.1 141.2 %forward.1 = (bf16[1184,768]{1,0:T(8,128)(2,1)}, bf16[2304,384]{1,0:T(8,128)(2,1)}, bf16[384,768]{1,0:T(8,128)(2,1)}, bf16[768,1536]{1,0:T(8,128)(2,1)}, bf16[15...) custom-call(s32[8]{0:T(128)} %parent.3, ...), custom_call_target="tpu_custom_call" | custom-call | tf_op jit(solution)/shard_map/forward/pallas_call | solution.py:941
  150.4 180.8 %backward.1 = (f32[2304,384]{1,0:T(8,128)}, f32[384,768]{1,0:T(8,128)}, f32[768,1536]{1,0:T(8,128)}, f32[1536,768]{1,0:T(8,128)}, f32[384,128]{1,0:T(8,128)}, /*index=5*/bf16[1184,768]{1,0:T(8,128)(2,1)}) custom-call(s32[8]{0:T(128)} %parent.3, s32[96,1]{1,0:T(8,128)} %pad.12.slot_rows, f32[1184,1]{1,0:T(8,128)} %get-tuple-element.37.inverse, ...), custom_call_target="tpu_custom_call" | custom-call | tf_op jit(solution)/shard_map/backward/pallas_call | solution.py:1334
  331.2 0.0 copy-start.1
  331.2 0.8 slice_bitcast_fusion.8
  332.0 0.6 pad_maximum_fusion
  332.6 1.3 slice_bitcast_fusion
  333.9 1.4 slice_bitcast_fusion.1
  335.3 0.0 copy-start
  335.3 3.0 copy.41
  338.3 0.0 copy-done.1
  338.3 0.0 slice-start.2
  338.3 1.2 copy.42
  339.5 0.0 copy-done
  339.5 0.0 copy-start.2
  339.5 0.0 slice-start.3
  339.5 1.8 copy.43
  341.3 1.4 copy-done.2
  342.8 0.0 slice-start
  342.8 1.0 copy.44
  343.8 0.0 slice-done.2
  343.8 0.0 slice-done.3
  343.8 0.0 slice-start.1
  343.8 2.4 copy.45
  346.2 0.8 slice-done
  347.0 0.3 slice-done.1
  347.3 2.2 copy.46
  (5 shorter events, 0.0 us)
Async XLA Ops:
  1.4 5.0 %copy-start.3 = (f32[1,768]{1,0:T(1,128)}, f32[1,768]{1,0:T(1,128)S(1)}, u32[]{:S(2)}) copy-start(f32[1,768]{1,0:T(1,128)S(1)} %stack.28.gain) | copy-start | bytes 9220
  331.2 7.1 %copy-start.1 = (bf16[1184,768]{1,0:T(8,128)(2,1)S(1)}, bf16[1184,768]{1,0:T(8,128)(2,1)}, u32[]{:S(2)}) copy-start(bf16[1184,768]{1,0:T(8,128)(2,1)} %get-tuple-element.85) | copy-start | bytes 5455876
  335.3 4.2 %copy-start = (f32[2304,384]{1,0:T(8,128)S(1)}, f32[2304,384]{1,0:T(8,128)}, u32[]{:S(2)}) copy-start(f32[2304,384]{1,0:T(8,128)} %get-tuple-element.53) | copy-start | bytes 10616836
  338.3 5.5 %slice-start.2 = ((s8[4718592]{0:T(1024)(128)(4,1)}), s8[4194304]{0:T(1024)(128)(4,1)S(1)}, s32[]{:S(2)}) async-start(s8[4718592]{0:T(1024)(128)(4,1)} %bitcast.31), calls=%async_computation.2 | async-start | bytes 8388608
  339.5 3.2 copy-start.2
  339.5 4.3 %slice-start.3 = ((s8[4718592]{0:T(1024)(128)(4,1)}), s8[524288]{0:T(1024)(128)(4,1)S(1)}, s32[]{:S(2)}) async-start(s8[4718592]{0:T(1024)(128)(4,1)} %bitcast.31), calls=%async_computation.3 | async-start | bytes 1048576
  342.8 4.3 %slice-start = ((s8[4718592]{0:T(1024)(128)(4,1)}), s8[4194304]{0:T(1024)(128)(4,1)S(1)}, s32[]{:S(2)}) async-start(s8[4718592]{0:T(1024)(128)(4,1)} %bitcast.29), calls=%async_computation | async-start | bytes 8388608
  343.8 3.5 %slice-start.1 = ((s8[4718592]{0:T(1024)(128)(4,1)}), s8[524288]{0:T(1024)(128)(4,1)S(1)}, s32[]{:S(2)}) async-start(s8[4718592]{0:T(1024)(128)(4,1)} %bitcast.29), calls=%async_computation.1 | async-start | bytes 1048576

commit v4 on v3

--- a/solution.py
+++ b/solution.py
@@ -11,7 +11,7 @@
 
 MESH = pl.DeviceIdType.MESH
 BR, BC = 384, 128
-SPREAD = 2
+SPREAD = 3
 SLOTS = 16
 
 
@@ -270,7 +270,7 @@
 
 CR, CC = 64, 384
 CHUNKS = 24
-RELAY = 1
+RELAY = 2
 BF = jnp.bfloat16
 
 

time: 350 us -> 289 us (0.83)
  Pallas kernels: 322 us -> 260 us
    pallas_call x1, Pallas kernels: 141 us -> 95.2 us  [forward(): pl.pallas_call(functools.partial(forward_kernel, fast), out_shape=out_sha...]
    pallas_call x1, Pallas kernels: 181 us -> 165 us  [backward(): pl.pallas_call(functools.partial(backward_kernel, fast), out_shape=[sd((3...]
where the time goes in v4:
time: 289 us; the launch traced here: 288 us
  Pallas kernels  260 us (90%)
  local copies, waits for them, and re-layouts  25.4 us (9%)
    pallas_call x1, Pallas kernels, backward(): pl.pallas_call(functools.partial(backward_kernel, fast), out_shape=[sd((3...  165 us
    pallas_call x1, Pallas kernels, forward(): pl.pallas_call(functools.partial(forward_kernel, fast), out_shape=out_sha...  95.2 us
    unnamed x23, local copies, waits for them, and re-layouts  15 us

profile of v4, /device:TPU:0, one launch (start us, length us, event | category | flops | bytes accessed | tf_op | source)
XLA Modules:
  0.0 287.5 jit_solution(10968493558557820510)
XLA Ops:
  0.6 0.1 pad.18.clone
  0.7 0.7 stack.28.gain
  1.4 0.0 copy-start.3
  1.4 0.7 stack.27
  2.1 0.7 stack.29
  2.8 0.7 stack.30
  3.5 0.7 stack.31
  4.2 0.7 stack.32
  4.9 0.8 fusion
  5.6 0.8 broadcast_add_fusion
  6.4 0.0 copy-done.3
  6.4 0.6 stack.34.rows_in
  7.0 0.7 reshape.68
  7.7 0.1 select_maximum_fusion
  7.8 0.6 pad.14.small
  8.4 0.1 reshape.78
  8.5 0.6 pad.12.slot_rows
  9.1 95.2 %forward.1 = (bf16[1184,768]{1,0:T(8,128)(2,1)}, bf16[2304,384]{1,0:T(8,128)(2,1)}, bf16[384,768]{1,0:T(8,128)(2,1)}, bf16[768,1536]{1,0:T(8,128)(2,1)}, bf16[15...) custom-call(s32[8]{0:T(128)} %parent.3, ...), custom_call_target="tpu_custom_call" | custom-call | tf_op jit(solution)/shard_map/forward/pallas_call | solution.py:941
  104.3 164.9 %backward.1 = (f32[2304,384]{1,0:T(8,128)}, f32[384,768]{1,0:T(8,128)}, f32[768,1536]{1,0:T(8,128)}, f32[1536,768]{1,0:T(8,128)}, f32[384,128]{1,0:T(8,128)}, /*index=5*/bf16[1184,768]{1,0:T(8,128)(2,1)}) custom-call(s32[8]{0:T(128)} %parent.3, s32[96,1]{1,0:T(8,128)} %pad.12.slot_rows, f32[1184,1]{1,0:T(8,128)} %get-tuple-element.37.inverse, ...), custom_call_target="tpu_custom_call" | custom-call | tf_op jit(solution)/shard_map/backward/pallas_call | solution.py:1334
  269.2 0.0 copy-start.1
  269.2 0.8 slice_bitcast_fusion.8
  270.1 0.6 pad_maximum_fusion
  270.6 1.3 slice_bitcast_fusion
  271.9 1.4 slice_bitcast_fusion.1
  273.3 0.0 copy-start
  273.3 3.0 %copy.41 = bf16[1184,768]{1,0:T(8,128)(2,1)} copy(bf16[1184,768]{1,0:T(8,128)(2,1)} %get-tuple-element.84) | data formatting | bytes 3637248
  276.3 0.0 copy-done.1
  276.3 0.0 slice-start.2
  276.3 1.2 copy.42
  277.6 0.0 copy-done
  277.6 0.0 copy-start.2
  277.6 0.0 slice-start.3
  277.6 1.8 copy.43
  279.4 1.4 copy-done.2
  280.8 0.0 slice-start
  280.8 1.0 copy.44
  281.8 0.0 slice-done.2
  281.8 0.0 slice-done.3
  281.8 0.0 slice-start.1
  281.8 2.4 copy.45
  284.2 0.8 slice-done
  285.1 0.3 slice-done.1
  285.4 2.2 copy.46
  (5 shorter events, 0.0 us)
Async XLA Ops:
  1.4 5.0 %copy-start.3 = (f32[1,768]{1,0:T(1,128)}, f32[1,768]{1,0:T(1,128)S(1)}, u32[]{:S(2)}) copy-start(f32[1,768]{1,0:T(1,128)S(1)} %stack.28.gain) | copy-start | bytes 9220
  269.2 7.1 %copy-start.1 = (bf16[1184,768]{1,0:T(8,128)(2,1)S(1)}, bf16[1184,768]{1,0:T(8,128)(2,1)}, u32[]{:S(2)}) copy-start(bf16[1184,768]{1,0:T(8,128)(2,1)} %get-tuple-element.85) | copy-start | bytes 5455876
  273.3 4.2 %copy-start = (f32[2304,384]{1,0:T(8,128)S(1)}, f32[2304,384]{1,0:T(8,128)}, u32[]{:S(2)}) copy-start(f32[2304,384]{1,0:T(8,128)} %get-tuple-element.53) | copy-start | bytes 10616836
  276.3 5.5 %slice-start.2 = ((s8[4718592]{0:T(1024)(128)(4,1)}), s8[4194304]{0:T(1024)(128)(4,1)S(1)}, s32[]{:S(2)}) async-start(s8[4718592]{0:T(1024)(128)(4,1)} %bitcast.31), calls=%async_computation.2 | async-start | bytes 8388608
  277.6 3.2 %copy-start.2 = (f32[384,768]{1,0:T(8,128)S(1)}, f32[384,768]{1,0:T(8,128)}, u32[]{:S(2)}) copy-start(f32[384,768]{1,0:T(8,128)} %get-tuple-element.88) | copy-start | bytes 3538948
  277.6 4.3 %slice-start.3 = ((s8[4718592]{0:T(1024)(128)(4,1)}), s8[524288]{0:T(1024)(128)(4,1)S(1)}, s32[]{:S(2)}) async-start(s8[4718592]{0:T(1024)(128)(4,1)} %bitcast.31), calls=%async_computation.3 | async-start | bytes 1048576
  280.8 4.3 %slice-start = ((s8[4718592]{0:T(1024)(128)(4,1)}), s8[4194304]{0:T(1024)(128)(4,1)S(1)}, s32[]{:S(2)}) async-start(s8[4718592]{0:T(1024)(128)(4,1)} %bitcast.29), calls=%async_computation | async-start | bytes 8388608
  281.8 3.5 %slice-start.1 = ((s8[4718592]{0:T(1024)(128)(4,1)}), s8[524288]{0:T(1024)(128)(4,1)S(1)}, s32[]{:S(2)}) async-start(s8[4718592]{0:T(1024)(128)(4,1)} %bitcast.29), calls=%async_computation.1 | async-start | bytes 1048576

commit v5 on v4

--- a/solution.py
+++ b/solution.py
@@ -128,130 +128,129 @@
     def core_six_in(block):
         return copy(6, block, rows(block, (1 - pos.core) * half, half), rows(block, (1 - pos.core) * half, half), pos.sib)
 
-    def stage_zero(block):
+    def start_core(block):
         core_out(block).start()
 
-    def stage_one(block):
+    def take_core(block):
         core_out(block).wait()
         free(2, pos.sib)
         add(block, mine, half, from_core.at[lax.rem(block, SLOTS)])
 
-        @pl.when(x_first)
-        def _():
-            x_one(block).start()
-
-        @pl.when(z_first & pos.end)
-        def _():
-            z_one(block).start()
-
-    def stage_two(block):
-        @pl.when(x_first)
-        def _():
-            x_one(block).wait()
-            free(1, pos.xn)
-            add(block, xrow, quarter, from_one.at[lax.rem(block, SLOTS), pl.ds(0, quarter)])
-
-            @pl.when(pos.end)
-            def _():
-                x_two(block).start()
-
-        @pl.when(z_first & pos.end)
-        def _():
-            z_one(block).wait_send()
-            free(1, pos.zp)
-
-        @pl.when(z_first & pos.mid)
-        def _():
-            z_one(block).wait_recv()
-            add(block, half, half, from_one.at[lax.rem(block, SLOTS)])
-            z_two(block).start()
-
-    def stage_three(block):
-        @pl.when(x_first & pos.end)
-        def _():
-            x_two(block).wait_send()
-            free(0, pos.zp)
-
-        @pl.when(x_first & pos.mid)
-        def _():
-            x_two(block).wait_recv()
-            add(block, xrow, quarter, from_two.at[lax.rem(block, SLOTS)])
-            x_three(block).start()
-
-        @pl.when(z_first & pos.mid)
-        def _():
-            z_two(block).wait()
-            free(0, pos.zm)
-            add(block, keep, quarter, from_two.at[lax.rem(block, SLOTS)])
-            z_three(block).start()
-
-    def stage_four(block):
-        @pl.when(x_first & pos.mid)
-        def _():
-            x_three(block).wait()
-            add(block, xrow, quarter, from_three.at[lax.rem(block, SLOTS)])
-            claim(0)
-            x_four(block).start()
-
-        @pl.when(z_first & pos.mid)
-        def _():
-            z_three(block).wait()
-            add(block, keep, quarter, from_three.at[lax.rem(block, SLOTS)])
-            claim(0)
-            z_four(block).start()
-
-    def stage_five(block):
-        @pl.when(x_first)
-        def _():
-            @pl.when(pos.end)
-            def _():
-                x_four(block).wait_recv()
-
-            @pl.when(pos.mid)
-            def _():
-                x_four(block).wait_send()
-
-            claim(1)
-            x_five(block).start()
-
-        @pl.when(z_first & pos.mid)
-        def _():
-            z_four(block).wait_send()
-            z_four_in(block).wait_recv()
-            claim(1)
-            z_five(block).start()
-
-    def stage_six(block):
-        @pl.when(x_first)
-        def _():
-            x_five(block).wait_send()
-            x_five_in(block).wait_recv()
-
-        @pl.when(z_first & pos.end)
-        def _():
-            z_five(block).wait_recv()
-
-        @pl.when(z_first & pos.mid)
-        def _():
-            z_five(block).wait_send()
-
+    def take_x(block):
+        x_one(block).wait()
+        free(1, pos.xn)
+        add(block, xrow, quarter, from_one.at[lax.rem(block, SLOTS), pl.ds(0, quarter)])
+
+    def send_x(block):
+        take_core(block)
+        x_one(block).start()
+
+    def send_z(block):
+        take_core(block)
+        z_one(block).start()
+
+    def x_end_two(block):
+        take_x(block)
+        x_two(block).start()
+
+    def x_end_three(block):
+        x_two(block).wait_send()
+        free(0, pos.zp)
+
+    def x_mid_three(block):
+        x_two(block).wait_recv()
+        add(block, xrow, quarter, from_two.at[lax.rem(block, SLOTS)])
+        x_three(block).start()
+
+    def x_mid_four(block):
+        x_three(block).wait()
+        add(block, xrow, quarter, from_three.at[lax.rem(block, SLOTS)])
+        claim(0)
+        x_four(block).start()
+
+    def x_end_five(block):
+        x_four(block).wait_recv()
+        claim(1)
+        x_five(block).start()
+
+    def x_mid_five(block):
+        x_four(block).wait_send()
+        claim(1)
+        x_five(block).start()
+
+    def x_six(block):
+        x_five(block).wait_send()
+        x_five_in(block).wait_recv()
         claim(2)
         core_six(block).start()
 
-    def stage_seven(block):
+    def z_end_two(block):
+        z_one(block).wait_send()
+        free(1, pos.zp)
+
+    def z_end_six(block):
+        z_five(block).wait_recv()
+        claim(2)
+        core_six(block).start()
+
+    def z_mid_two(block):
+        z_one(block).wait_recv()
+        add(block, half, half, from_one.at[lax.rem(block, SLOTS)])
+        z_two(block).start()
+
+    def z_mid_three(block):
+        z_two(block).wait()
+        free(0, pos.zm)
+        add(block, keep, quarter, from_two.at[lax.rem(block, SLOTS)])
+        z_three(block).start()
+
+    def z_mid_four(block):
+        z_three(block).wait()
+        add(block, keep, quarter, from_three.at[lax.rem(block, SLOTS)])
+        claim(0)
+        z_four(block).start()
+
+    def z_mid_five(block):
+        z_four(block).wait_send()
+        z_four_in(block).wait_recv()
+        claim(1)
+        z_five(block).start()
+
+    def z_mid_six(block):
+        z_five(block).wait_send()
+        claim(2)
+        core_six(block).start()
+
+    def last(block):
         core_six(block).wait_send()
         core_six_in(block).wait_recv()
-        finish(block)
-
-    stages = (stage_zero, stage_one, stage_two, stage_three, stage_four, stage_five, stage_six, stage_seven)
+
+    roles = (
+        (x_first & pos.end, (start_core, send_x, x_end_two, x_end_three, None, x_end_five, x_six, last)),
+        (x_first & pos.mid, (start_core, send_x, take_x, x_mid_three, x_mid_four, x_mid_five, x_six, last)),
+        (z_first & pos.end, (start_core, send_z, z_end_two, None, None, None, z_end_six, last)),
+        (z_first & pos.mid, (start_core, take_core, z_mid_two, z_mid_three, z_mid_four, z_mid_five, z_mid_six, last)),
+    )
+    depth = len(roles[0][1])
 
     def tick(step):
-        for index in reversed(range(8)):
-            block = step - SPREAD * index
-
-            @pl.when((block >= 0) & (block < count))
-            def _(index=index, block=block):
-                stages[index](block)
+        for here, stages in roles:
+
+            @pl.when(here)
+            def _(stages=stages):
+                for index in reversed(range(depth)):
+                    block = step - SPREAD * index
+                    if stages[index] is not None:
+
+                        @pl.when((block >= 0) & (block < count))
+                        def _(index=index, block=block, stages=stages):
+                            stages[index](block)
+
+        over = step - SPREAD * (depth - 1)
+
+        @pl.when((over >= 0) & (over < count))
+        def _():
+            finish(over)
 
     return tick
 
@@ -476,9 +475,14 @@
         colbias[s : s + 1, :] = jnp.where(jnp.maximum(inside, reach[s]) > 0.0, 0.0, MASKED)
 
 
-def build_select(slot_rows, select):
+def build_select(slots, select):
+    row = lax.broadcasted_iota(jnp.int32, (select.shape[0], 1), 0)
+    where = jnp.full((select.shape[0], 1), -1, jnp.int32)
+    for t in range(SEGS):
+        for m in range(MEMW):
+            where = jnp.where(row == MEMW * t + m, slots[t, m] + SEG * t, where)
     place = lax.broadcasted_iota(jnp.int32, select.shape, 1)
-    select[...] = (slot_rows[...] == place).astype(F32).astype(BF)
+    select[...] = (where == place).astype(F32).astype(BF)
 
 
 def window(s):
@@ -503,7 +507,7 @@
     return raised, 1.0 / jnp.sum(raised, axis=-1, keepdims=True)
 
 
-def attend_pair(q, k, v, kmem, vmem, colbias, mixed, s, columns):
+def attend_pair(q, k, v, kmem, vmem, colbias, mixed, probs, s, columns):
     left, right, is_left = lane_halves()
     at, off = window(s)
     rows = pl.ds(at, WIN)
@@ -512,14 +516,17 @@
     kk = jnp.concatenate([k[rows, columns], kmem[:, columns]], axis=0)
     vv = jnp.concatenate([v[rows, columns], vmem[:, columns]], axis=0)
     raised, scale = softmax_parts(qs, kk, colbias[pl.ds(s, 1), :])
-    both = mm((raised * scale).astype(BF), vv)
+    row, valid = valid_rows(off)
+    keep = jnp.where(valid, 1.0, 0.0)
+    chances = (raised * (scale * jnp.concatenate([keep, keep], axis=0))).astype(BF)
+    probs[...] = chances
+    both = mm(chances, vv)
     out = jnp.where(is_left, both[:WIN], both[WIN:])
-    row, valid = valid_rows(off)
     old = mixed[rows, columns].astype(F32)
     mixed[rows, columns] = jnp.where(row >= off, out, old).astype(BF)
 
 
-def attend_back_pair(q, k, v, kmem, vmem, colbias, dmix, dq, dk, dv, dkmem, dvmem, s, columns, acc):
+def attend_back_pair(q, k, v, kmem, vmem, probs, dmix, dq, dk, dv, dkmem, dvmem, s, columns):
     left, right, is_left = lane_halves()
     at, off = window(s)
     rows = pl.ds(at, WIN)
@@ -529,102 +536,28 @@
     vv = jnp.concatenate([v[rows, columns], vmem[:, columns]], axis=0)
     dw = dmix[rows, columns]
     ds_in = jnp.concatenate([dw * left, dw * right], axis=0)
-    raised, scale = softmax_parts(qs, kk, colbias[pl.ds(s, 1), :])
-    row, valid = valid_rows(off)
-    keep = jnp.where(valid, 1.0, 0.0)
-    chances = raised * (scale * jnp.concatenate([keep, keep], axis=0))
+    low = probs[...]
+    chances = low.astype(F32)
     dp = mm_t(ds_in, vv)
     inner = jnp.sum(chances * dp, axis=-1, keepdims=True)
     ds = (chances * (dp - inner)).astype(BF)
-    pb = chances.astype(BF)
     dqs = mm(ds, kk)
+    row, valid = valid_rows(off)
     new = jnp.where(is_left, dqs[:WIN], dqs[WIN:]) * HD ** (-0.5)
     old = dq[rows, columns].astype(F32)
     dq[rows, columns] = jnp.where(row >= off, new, old).astype(BF)
     dks = t_mm(ds, qs)
-    dvs = t_mm(pb, ds_in)
-    dk[rows, acc] = dk[rows, acc] + dks[:WIN]
-    dv[rows, acc] = dv[rows, acc] + dvs[:WIN]
-    dkmem[:, acc] = dkmem[:, acc] + dks[WIN:]
-    dvmem[:, acc] = dvmem[:, acc] + dvs[WIN:]
+    dvs = t_mm(low, ds_in)
+    dk[rows, columns] = dk[rows, columns] + dks[:WIN]
+    dv[rows, columns] = dv[rows, columns] + dvs[:WIN]
+    dkmem[:, columns] = dkmem[:, columns] + dks[WIN:]
+    dvmem[:, columns] = dvmem[:, columns] + dvs[WIN:]
 
 
 def spread(select, part):
     high = part.astype(BF)
     low = (part - high.astype(F32)).astype(BF)
     return t_mm(select, high) + t_mm(select, low)
-
-
-def forward_attention_kernel(parent, slot_rows, q, k, v, mixed, colbias, select, kmem, vmem):
-    base = lax.axis_index("dp") * SEGS
-    build_masks(parent, base, colbias)
-    build_select(slot_rows, select)
-    kmem[...] = mm(select[...], k[...]).astype(BF)
-    vmem[...] = mm(select[...], v[...]).astype(BF)
-    pairs = q.shape[1] // PAIR
-
-    @pl.loop(0, SEGS)
-    def _(s):
-        for pair in range(pairs):
-            attend_pair(q, k, v, kmem, vmem, colbias, mixed, s, pl.ds(pair * PAIR, PAIR))
-
-
-def backward_attention_kernel(
-    parent, slot_rows, q, k, v, dmix, dq, dk, dv, colbias, select, kmem, vmem, dka, dva, dkm, dvm
-):
-    base = lax.axis_index("dp") * SEGS
-    build_masks(parent, base, colbias)
-    build_select(slot_rows, select)
-    kmem[...] = mm(select[...], k[...]).astype(BF)
-    vmem[...] = mm(select[...], v[...]).astype(BF)
-    pairs = q.shape[1] // PAIR
-    for ref in (dka, dva, dkm, dvm):
-        ref[...] = jnp.zeros(ref.shape, F32)
-
-    @pl.loop(0, SEGS)
-    def _(s):
-        for pair in range(pairs):
-            columns = pl.ds(pair * PAIR, PAIR)
-            attend_back_pair(
-                q, k, v, kmem, vmem, colbias, dmix, dq, dka, dva, dkm, dvm, s, columns, columns
-            )
-
-    for pair in range(pairs):
-        columns = pl.ds(pair * PAIR, PAIR)
-        dk[:, columns] = ((dka[:, columns] + spread(select[...], dkm[:, columns])) * HD ** (-0.5)).astype(BF)
-        dv[:, columns] = (dva[:, columns] + spread(select[...], dvm[:, columns])).astype(BF)
-
-
-def attention_call(kernel, outs, parent, slot_rows, arrays, scratch, name):
-    rows, width = arrays[0].shape
-    vm = pl.BlockSpec(memory_space=pltpu.VMEM)
-    return pl.pallas_call(
-        kernel,
-        out_shape=[jax.ShapeDtypeStruct((rows, width), BF)] * outs,
-        in_specs=[pl.BlockSpec(memory_space=pltpu.SMEM), vm] + [vm] * len(arrays),
-        out_specs=[vm] * outs,
-        scratch_shapes=[
-            pltpu.VMEM((SEGS, WIN + MEMP), F32),
-            pltpu.VMEM((MEMP, rows), BF),
-            pltpu.VMEM((MEMP, width), BF),
-            pltpu.VMEM((MEMP, width), BF),
-        ]
-        + scratch,
-        compiler_params=pltpu.CompilerParams(vmem_limit_bytes=60 * 2**20),
-        name=name,
-    )(parent, slot_rows, *arrays)
-
-
-def forward_attention(parent, slot_rows, q, k, v):
-    return attention_call(forward_attention_kernel, 1, parent, slot_rows, (q, k, v), [], "attend")[0]
-
-
-def backward_attention(parent, slot_rows, q, k, v, dmix):
-    rows, width = q.shape
-    scratch = [pltpu.VMEM((rows, width), F32)] * 2 + [pltpu.VMEM((MEMP, width), F32)] * 2
-    return attention_call(
-        backward_attention_kernel, 3, parent, slot_rows, (q, k, v, dmix), scratch, "attend_back"
-    )
 
 
 def norm_stats(values):
@@ -648,6 +581,10 @@
     return (inner * phi).astype(BF), (phi + inner * density).astype(BF)
 
 
+def flat_row(ref, start, size):
+    return ref[pl.ds(start, size)].reshape(1, size)
+
+
 TILE = 128
 
 
@@ -665,9 +602,15 @@
 def forward_kernel(
     fast,
     parent,
-    slot_rows,
-    small,
-    rows_in,
+    slots,
+    bias_qv,
+    bias_out,
+    gain_one,
+    shift_one,
+    bias_up,
+    bias_down,
+    gain_two,
+    shift_two,
     tokens_h,
     grad_h,
     own_qkv,
@@ -677,7 +620,7 @@
     *rest,
 ):
     count = 0 if fast else 5
-    given, outs, rest = rest[:count], rest[count : count + 16], rest[count + 16 :]
+    given, outs, rest = rest[:count], rest[count : count + 18], rest[count + 18 :]
     (
         output_h,
         their_qkv_h,
@@ -695,6 +638,8 @@
         d_two_h,
         d_ffn_h,
         vec,
+        probs_h,
+        select,
     ) = outs
     (
         tokens,
@@ -702,6 +647,7 @@
         their_out,
         their_up,
         their_down,
+        small,
         small_their,
         qkv,
         mixed,
@@ -712,16 +658,18 @@
         acted,
         slopes,
         colbias,
-        select,
         kmem,
         vmem,
         sums,
+        probs,
         io_sem,
         slope_sem,
+        probs_sem,
         *wires,
     ) = rest
     rows, depth = tokens.shape
     width = mixed.shape[2]
+    units = acted.shape[1]
     theirs = (their_qkv, their_out, their_up, their_down)
     own = (own_qkv, own_out, own_up, own_down)
 
@@ -744,6 +692,11 @@
     ]
     load_tokens.start()
     done = [0]
+    small[...] = jnp.zeros(small.shape, F32)
+    small[0:1, :] = bias_qv[0:1, :]
+    small[2:3, :] = bias_qv[1:2, :]
+    for c in range(units // CHUNK):
+        small[3 + c : 4 + c, 0:CHUNK] = flat_row(bias_up, c * CHUNK, CHUNK)
     if fast:
         pos = Place()
         small_sem, *wires = wires
@@ -777,7 +730,7 @@
             done[0] = count
 
     build_masks(parent, lax.axis_index("dp") * SEGS, colbias)
-    build_select(slot_rows, select)
+    build_select(slots, select)
     load_tokens.wait()
     pairs = width // PAIR
     for half in range(2):
@@ -799,14 +752,27 @@
         kmem[...] = mm(select[...], k[...]).astype(BF)
         vmem[...] = mm(select[...], v[...]).astype(BF)
 
+        def put_probs(s, half=half):
+            slot = lax.rem(s, 2)
+            return pltpu.make_async_copy(probs.at[slot], probs_h.at[half, s], probs_sem.at[slot])
+
         @pl.loop(0, SEGS)
-        def _(s, half=half, q=q, k=k, v=v):
+        def _(s, half=half, q=q, k=k, v=v, put_probs=put_probs):
+            @pl.when(s >= 2)
+            def _():
+                put_probs(s - 2).wait()
+
             for pair in range(pairs):
-                attend_pair(q, k, v, kmem, vmem, colbias, mixed.at[half], s, pl.ds(pair * PAIR, PAIR))
+                attend_pair(
+                    q, k, v, kmem, vmem, colbias, mixed.at[half], probs.at[lax.rem(s, 2), pair], s, pl.ds(pair * PAIR, PAIR)
+                )
                 if pair < GATHER[2 * half + 1]:
                     tick(done[0] + s * GATHER[2 * half + 1] + pair)
+            put_probs(s).start()
 
         done[0] += SEGS * GATHER[2 * half + 1]
+        put_probs(SEGS - 2).wait()
+        put_probs(SEGS - 1).wait()
     put_qkv.start()
     put_mixed.start()
     until(BOUNDS[1][1] + 3 * RELAY)
@@ -820,11 +786,11 @@
     done[0] += 3 * GATHER[4]
 
     def norm_one(span):
-        resid = tokens[span, :].astype(F32) + (acc_own[span, :] + rows_in[0:1, :])
+        resid = tokens[span, :].astype(F32) + (acc_own[span, :] + flat_row(bias_out, 0, depth))
         unit, scale = norm_stats(resid)
         normed[span, :] = unit
         inverse[span, :] = scale
-        hidden[span, :] = (unit * rows_in[1:2, :] + rows_in[2:3, :]).astype(BF)
+        hidden[span, :] = (unit * flat_row(gain_one, 0, depth) + flat_row(shift_one, 0, depth)).astype(BF)
 
     row_tiles(rows, norm_one)
     load_grad.start()
@@ -886,12 +852,12 @@
     sums[...] = jnp.zeros(sums.shape, F32)
 
     def norm_two(span):
-        first = normed[span, :] * rows_in[1:2, :] + rows_in[2:3, :]
-        resid = first + ((acc_own[span, :] + acc_their[span, :]) + rows_in[3:4, :])
+        first = normed[span, :] * flat_row(gain_one, 0, depth) + flat_row(shift_one, 0, depth)
+        resid = first + ((acc_own[span, :] + acc_their[span, :]) + flat_row(bias_down, 0, depth))
         unit, scale = norm_stats(resid)
         grad = tokens[span, :].astype(F32)
-        tokens[span, :] = (unit * rows_in[4:5, :] + rows_in[5:6, :]).astype(BF)
-        back = norm_back(grad, unit, scale, rows_in[4:5, :])
+        tokens[span, :] = (unit * flat_row(gain_two, 0, depth) + flat_row(shift_two, 0, depth)).astype(BF)
+        back = norm_back(grad, unit, scale, flat_row(gain_two, 0, depth))
         acc_own[span, :] = back
         low = back.astype(BF)
         hidden[span, :] = low
@@ -916,12 +882,13 @@
 GATHER = (0, 1, 1, 1, 0, 1, 0, 0, 0)
 
 
-def forward(fast, parent, slot_rows, small, rows_in, tokens, grad_out, own, given):
+def forward(fast, parent, slots, vectors, tokens, grad_out, own, given):
     rows, depth = tokens.shape
     width = own[0].shape[1]
     units = own[2].shape[1]
     vm = pl.BlockSpec(memory_space=pltpu.VMEM)
     hbm = pl.BlockSpec(memory_space=pl.ANY)
+    sm = pl.BlockSpec(memory_space=pltpu.SMEM)
     sd = jax.ShapeDtypeStruct
     out_shape = [
         sd((rows, depth), BF),
@@ -937,16 +904,19 @@
         sd((rows, depth), F32),
         sd((rows, depth), BF),
         sd((18, BC), F32),
+        sd((2, SEGS, width // PAIR, 2 * WIN, WIN + MEMP), BF),
+        sd((MEMP, rows), BF),
     ]
     return pl.pallas_call(
         functools.partial(forward_kernel, fast),
         out_shape=out_shape,
-        in_specs=[pl.BlockSpec(memory_space=pltpu.SMEM), vm, vm, vm, hbm, hbm] + [vm] * 4 + [hbm] * len(given),
-        out_specs=[hbm] * 8 + [vm] + [hbm] * 6 + [vm],
+        in_specs=[sm, sm] + [vm] * len(vectors) + [hbm, hbm] + [vm] * 4 + [hbm] * len(given),
+        out_specs=[hbm] * 8 + [vm] + [hbm] * 6 + [vm, hbm, vm],
         scratch_shapes=[
             pltpu.VMEM((rows, depth), BF),
             *[pltpu.VMEM(w.shape, BF) for w in own],
-            pltpu.VMEM(small.shape, F32),
+            pltpu.VMEM((16, width), F32),
+            pltpu.VMEM((16, width), F32),
             pltpu.VMEM((2, 3, rows, width), BF),
             pltpu.VMEM((2, rows, width), BF),
             pltpu.VMEM((rows, depth), F32),
@@ -956,11 +926,12 @@
             pltpu.VMEM((rows, units), BF),
             pltpu.VMEM((2, rows, CHUNK), BF),
             pltpu.VMEM((SEGS, WIN + MEMP), F32),
-            pltpu.VMEM((MEMP, rows), BF),
             pltpu.VMEM((MEMP, width), BF),
             pltpu.VMEM((MEMP, width), BF),
             pltpu.VMEM((3, 8, depth), F32),
+            pltpu.VMEM((2, width // PAIR, 2 * WIN, WIN + MEMP), BF),
             pltpu.SemaphoreType.DMA((15,)),
+            pltpu.SemaphoreType.DMA((2,)),
             pltpu.SemaphoreType.DMA((2,)),
         ]
         + ([pltpu.SemaphoreType.DMA((2,))] + gather_scratch() if fast else []),
@@ -968,7 +939,7 @@
             collective_id=0 if fast else None, has_side_effects=fast, vmem_limit_bytes=67043328
         ),
         name="forward",
-    )(parent, slot_rows, small, rows_in, tokens, grad_out, *own, *given)
+    )(parent, slots, *vectors, tokens, grad_out, *own, *given)
 
 
 DOWN, UP, OUT, QKV, VEC = 0, 24, 48, 54, 72
@@ -979,8 +950,7 @@
 
 def backward_kernel(
     fast,
-    parent,
-    slot_rows,
+    select,
     inverse,
     gain,
     vec_in,
@@ -994,6 +964,7 @@
     slope_their_h,
     qkv_h,
     mixed_h,
+    probs_h,
     w_up_own,
     w_up_their,
     w_down_own,
@@ -1028,8 +999,7 @@
     qkv,
     d_qkv,
     d_mixed,
-    colbias,
-    select,
+    probs,
     kmem,
     vmem,
     dkm,
@@ -1037,6 +1007,7 @@
     load_sem,
     chunk_sem,
     put_sem,
+    probs_sem,
     *wires,
 ):
     rows, depth = tokens.shape
@@ -1068,6 +1039,10 @@
             pltpu.make_async_copy(up_h.at[:, span], up_buf.at[slot], chunk_sem.at[2, slot]),
             pltpu.make_async_copy(down_h.at[span, :], down_buf.at[slot], chunk_sem.at[3, slot]),
         )
+
+    def load_probs(half, s):
+        slot = lax.rem(s, 2)
+        return pltpu.make_async_copy(probs_h.at[half, s], probs.at[slot], probs_sem.at[slot])
 
     def start(copies):
         for copy in copies:
@@ -1088,6 +1063,7 @@
     start(load_w)
     load_tokens.start()
     load_qkv[0].start()
+    load_probs(0, 0).start()
 
     def put(block, target):
         return pltpu.make_async_copy(grads.at[block], target, put_sem.at[lax.rem(block, 8)])
@@ -1132,7 +1108,9 @@
     else:
 
         def tick(step):
-            finish(step)
+            @pl.when(step < COUNT)
+            def _():
+                finish(step)
 
         last = COUNT
     done = [0]
@@ -1187,7 +1165,10 @@
                 def _():
                     start(load_chunk(1, 0))
 
+            each = TICKS[1 + half]
             d_inner[...] = (mm_t(d_low[...], down_buf[slot]) * slope_buf[slot].astype(F32)).astype(BF)
+            if each > 1:
+                tick(done[0] + c * each)
             if half == 0:
                 piece = t_mm(hidden[...], d_inner[...])
                 for r in range(2):
@@ -1196,10 +1177,12 @@
                 total = jnp.sum(d_inner[...].astype(F32), axis=0, keepdims=True)
                 for j in range(2):
                     grads[VEC, pl.ds(6 + 2 * c + j, 1), :] = total[:, BC * j : BC * (j + 1)]
-            ticks(c, TICKS[1 + half], 6)
+                if each > 2:
+                    tick(done[0] + c * each + 1)
             for part in range(3):
                 columns = slice(CHUNK * part, CHUNK * (part + 1))
                 acc[:, columns] = acc[:, columns] + mm_t(d_inner[...], up_buf[slot, columns, :])
+            tick(done[0] + c * each + each - 1)
 
         done[0] += 6 * TICKS[1 + half]
 
@@ -1213,7 +1196,7 @@
         span = pl.ds(pl.multiple_of(i * tile, tile), tile)
         total = d_res[span, :] + (acc_own[span, :] + acc_their[span, :])
         unit = normed[span, :]
-        one = norm_back(total, unit, inverse[span, :], gain[...])
+        one = norm_back(total, unit, inverse[span, :], flat_row(gain, 0, depth))
         d_res[span, :] = one
         low = one.astype(BF)
         d_low[span, :] = low
@@ -1243,8 +1226,6 @@
 
     done[0] += 2 * TICKS[3]
 
-    build_masks(parent, lax.axis_index("dp") * SEGS, colbias)
-    build_select(slot_rows, select)
     wait(load_w)
     load_tokens.wait()
     pairs = width // PAIR
@@ -1258,17 +1239,35 @@
         dkm[...] = jnp.zeros(dkm.shape, F32)
         dvm[...] = jnp.zeros(dvm.shape, F32)
 
-        @pl.loop(0, SEGS)
-        def _(s, half=half):
-            for pair in range(pairs):
-                columns = pl.ds(pair * PAIR, PAIR)
-                attend_back_pair(
-                    q, k, v, kmem, vmem, colbias, d_mixed.at[half], d_qkv.at[0], dka, dva, dkm, dvm, s, columns, columns
-                )
-                if pair < TICKS[4 + half]:
-                    tick(done[0] + s * TICKS[4 + half] + pair)
-
-        done[0] += SEGS * TICKS[4 + half]
+        @pl.loop(0, SEGS * pairs)
+        def _(spot, half=half):
+            s, pair = spot // pairs, lax.rem(spot, pairs)
+
+            @pl.when(pair == 0)
+            def _():
+                load_probs(half, s).wait()
+
+                @pl.when(s < SEGS - 1)
+                def _():
+                    load_probs(half, s + 1).start()
+
+                if half == 0:
+
+                    @pl.when(s == SEGS - 1)
+                    def _():
+                        load_probs(1, 0).start()
+
+            columns = pl.ds(pl.multiple_of(pair * PAIR, PAIR), PAIR)
+            part = probs.at[lax.rem(s, 2), pair]
+            attend_back_pair(q, k, v, kmem, vmem, part, d_mixed.at[half], d_qkv.at[0], dka, dva, dkm, dvm, s, columns)
+
+            @pl.when(lax.rem(spot, TICKS[4 + half]) == 0)
+            def _():
+                tick(done[0] + spot // TICKS[4 + half])
+
+        done[0] += -(-SEGS * pairs // TICKS[4 + half])
+        if half == 0:
+            assert done[0] <= QKV
         if half == 0:
             load_qkv[1].start()
         for pair in range(pairs):
@@ -1308,9 +1307,7 @@
 
             done[0] += 3 * TICKS[7]
             put_tokens.start()
-    assert done[0] <= COUNT
-
-    @pl.loop(done[0], last)
+    @pl.loop(min(done[0], last), last)
     def _(step):
         tick(step)
 
@@ -1319,11 +1316,11 @@
     put_tokens.wait()
 
 
-TICKS = (1, 2, 1, 1, 2, 2, 2, 1)
+TICKS = (1, 3, 2, 1, 2, 1, 3, 1)
 TICK_TILES = 8
 
 
-def backward(fast, parent, slot_rows, inverse, gain, vec_in, arrays):
+def backward(fast, select, inverse, gain, vec_in, arrays):
     tokens, acted, mixed = arrays[0], arrays[5], arrays[9]
     rows, depth = tokens.shape
     units = acted.shape[1]
@@ -1341,7 +1338,7 @@
             sd((BR, BC), F32),
             sd((rows, depth), BF),
         ],
-        in_specs=[pl.BlockSpec(memory_space=pltpu.SMEM), vm, vm, vm, vm] + [hbm] * len(arrays),
+        in_specs=[vm, vm, vm, vm] + [hbm] * len(arrays),
         out_specs=[hbm] * 6,
         scratch_shapes=[
             pltpu.VMEM((COUNT, BR, BC), F32),
@@ -1364,8 +1361,7 @@
             pltpu.VMEM((3, rows, width), BF),
             pltpu.VMEM((3, rows, width), BF),
             pltpu.VMEM((2, rows, width), BF),
-            pltpu.VMEM((SEGS, WIN + MEMP), F32),
-            pltpu.VMEM((MEMP, rows), BF),
+            pltpu.VMEM((2, width // PAIR, 2 * WIN, WIN + MEMP), BF),
             pltpu.VMEM((MEMP, width), BF),
             pltpu.VMEM((MEMP, width), BF),
             pltpu.VMEM((MEMP, width), F32),
@@ -1373,13 +1369,14 @@
             pltpu.SemaphoreType.DMA((13,)),
             pltpu.SemaphoreType.DMA((4, 2)),
             pltpu.SemaphoreType.DMA((8,)),
+            pltpu.SemaphoreType.DMA((2,)),
         ]
         + (sum_scratch() if fast else []),
         compiler_params=pltpu.CompilerParams(
             collective_id=1 if fast else None, has_side_effects=fast, vmem_limit_bytes=67043328
         ),
         name="backward",
-    )(parent, slot_rows, inverse, gain, vec_in, *arrays)
+    )(select, inverse, gain, vec_in, *arrays)
 
 
 def halves_swap(own, small):
@@ -1414,15 +1411,13 @@
     depth, width = w_qkv.shape[1:]
     hidden_units = w_up.shape[1]
     own = (w_qkv.reshape(3 * depth, width), w_out, w_up, w_down)
-    table = jnp.pad(bias_up.reshape(-1, CHUNK), ((0, 0), (0, width - CHUNK)))
-    small = jnp.concatenate([bias_qv[:1], jnp.zeros((1, width), F32), bias_qv[1:], table])
-    small = jnp.pad(small, ((0, 16 - small.shape[0]), (0, 0)))
-    given = () if fast else halves_swap(own, small)
-    slot_rows = mem_slots + jnp.arange(SEGS, dtype=jnp.int32)[:, None] * SEG
-    slot_rows = jnp.pad(slot_rows.reshape(-1, 1), ((0, MEMP - MEMW * SEGS), (0, 0)), constant_values=-1)
-    rows_in = jnp.stack(
-        [bias_out, gain_one, shift_one, bias_down, gain_two, shift_two, jnp.zeros_like(gain_one), jnp.zeros_like(gain_one)]
-    )
+    if fast:
+        given = ()
+    else:
+        table = jnp.pad(bias_up.reshape(-1, CHUNK), ((0, 0), (0, width - CHUNK)))
+        small = jnp.concatenate([bias_qv[:1], jnp.zeros((1, width), F32), bias_qv[1:], table])
+        given = halves_swap(own, jnp.pad(small, ((0, 16 - small.shape[0]), (0, 0))))
+    vectors = (bias_qv, bias_out, gain_one, shift_one, bias_up, bias_down, gain_two, shift_two)
     (
         output,
         *theirs,
@@ -1437,13 +1432,15 @@
         d_two,
         d_ffn,
         vec,
-    ) = forward(fast, parent, slot_rows, small, rows_in, tokens, grad_out, own, given)
+        probs,
+        select,
+    ) = forward(fast, parent, mem_slots, vectors, tokens, grad_out, own, given)
     if not fast:
         theirs = given[:4]
-    arrays = (tokens, hidden_low, d_ffn, d_two, normed, acted, slope_own, slope_their, qkv, mixed)
+    arrays = (tokens, hidden_low, d_ffn, d_two, normed, acted, slope_own, slope_their, qkv, mixed, probs)
     weights = tuple(w[i] for i in (2, 3, 1, 0) for w in (own, theirs))
     g_w_qkv, g_w_out, g_w_up, g_w_down, flat, grad_tokens = backward(
-        fast, parent, slot_rows, inverse, gain_one.reshape(1, -1), vec, arrays + weights
+        fast, select, inverse, gain_one, vec, arrays + weights
     )
     if not fast:
         g_w_qkv, g_w_out, g_w_up, g_w_down, flat = lax.psum((g_w_qkv, g_w_out, g_w_up, g_w_down, flat), "dp")

time: 289 us -> 270 us (0.934)
  Pallas kernels: 260 us -> 249 us
  local copies, waits for them, and re-layouts: 25.4 us -> 17.7 us
    pallas_call x1, Pallas kernels: 165 us -> 153 us  [backward(): pl.pallas_call(functools.partial(backward_kernel, fast), out_shape=[sd((3...]
    another operation x8 -> x0, local copies, waits for them, and re-layouts: 4.78 us -> none  [shards(): jnp.stack([bias_out, gain_one, shift_one, bias_down, gain_two, shift_two,...]
    unnamed x23 -> x21, local copies, waits for them, and re-layouts: 15 us -> 15 us
where the time goes in v5:
time: 270 us; the launch traced here: 268 us
  Pallas kernels  249 us (92%)
  local copies, waits for them, and re-layouts  17.7 us (7%)
    pallas_call x1, Pallas kernels, backward(): pl.pallas_call(functools.partial(backward_kernel, fast), out_shape=[sd((3...  153 us
    pallas_call x1, Pallas kernels, forward(): pl.pallas_call(functools.partial(forward_kernel, fast), out_shape=out_sha...  96.2 us
    unnamed x21, local copies, waits for them, and re-layouts  15 us

profile of v5, /device:TPU:0, one launch (start us, length us, event | category | flops | bytes accessed | tf_op | source)
XLA Modules:
  0.0 268.0 jit_solution(5421338541814668934)
XLA Ops:
  0.6 96.2 %forward.1 = (bf16[1184,768]{1,0:T(8,128)(2,1)}, bf16[2304,384]{1,0:T(8,128)(2,1)}, bf16[384,768]{1,0:T(8,128)(2,1)}, bf16[768,1536]{1,0:T(8,128)(2,1)}, bf16[15...) custom-call(s32[8]{0:T(128)} %parent.1, ...), custom_call_target="tpu_custom_call" | custom-call | tf_op jit(solution)/shard_map/forward/pallas_call | solution.py:910
  96.8 152.9 %backward.1 = (f32[2304,384]{1,0:T(8,128)}, f32[384,768]{1,0:T(8,128)}, f32[768,1536]{1,0:T(8,128)}, f32[1536,768]{1,0:T(8,128)}, f32[384,128]{1,0:T(8,128)}, /*index=5*/bf16[1184,768]{1,0:T(8,128)(2,1)}) custom-call(bf16[96,1184]{1,0:T(8,128)(2,1)} %get-tuple-element.39.select, f32[1184,1]{1,0:T(8,128)} %get-tuple-element.40.inverse, f32[768]{0:T(1024)} %gain.1, ...), custom_call_target="tpu_custom_call" | custom-call | tf_op jit(solution)/shard_map/backward/pallas_call | solution.py:1331
  249.7 0.0 copy-start.1
  249.7 0.8 slice_bitcast_fusion.8
  250.5 0.6 pad_maximum_fusion
  251.1 1.3 slice_bitcast_fusion
  252.4 1.4 slice_bitcast_fusion.1
  253.8 0.0 copy-start
  253.8 3.0 %copy.40 = bf16[1184,768]{1,0:T(8,128)(2,1)} copy(bf16[1184,768]{1,0:T(8,128)(2,1)} %get-tuple-element.86) | data formatting | bytes 3637248
  256.8 0.0 copy-done.1
  256.8 0.0 slice-start.2
  256.8 1.2 copy.41
  258.0 0.0 copy-done
  258.0 0.0 copy-start.2
  258.0 0.0 slice-start.3
  258.0 1.8 copy.42
  259.8 1.4 copy-done.2
  261.3 0.0 slice-start
  261.3 1.0 copy.43
  262.3 0.0 slice-done.2
  262.3 0.0 slice-done.3
  262.3 0.0 slice-start.1
  262.3 2.4 copy.44
  264.7 0.8 slice-done
  265.5 0.3 slice-done.1
  265.8 2.2 copy.45
  (3 shorter events, 0.0 us)
Async XLA Ops:
  249.7 7.1 %copy-start.1 = (bf16[1184,768]{1,0:T(8,128)(2,1)S(1)}, bf16[1184,768]{1,0:T(8,128)(2,1)}, u32[]{:S(2)}) copy-start(bf16[1184,768]{1,0:T(8,128)(2,1)} %get-tuple-element.87) | copy-start | bytes 5455876
  253.8 4.2 %copy-start = (f32[2304,384]{1,0:T(8,128)S(1)}, f32[2304,384]{1,0:T(8,128)}, u32[]{:S(2)}) copy-start(f32[2304,384]{1,0:T(8,128)} %get-tuple-element.57) | copy-start | bytes 10616836
  256.8 5.5 %slice-start.2 = ((s8[4718592]{0:T(1024)(128)(4,1)}), s8[4194304]{0:T(1024)(128)(4,1)S(1)}, s32[]{:S(2)}) async-start(s8[4718592]{0:T(1024)(128)(4,1)} %bitcast.30), calls=%async_computation.2 | async-start | bytes 8388608
  258.0 3.2 %copy-start.2 = (f32[384,768]{1,0:T(8,128)S(1)}, f32[384,768]{1,0:T(8,128)}, u32[]{:S(2)}) copy-start(f32[384,768]{1,0:T(8,128)} %get-tuple-element.90) | copy-start | bytes 3538948
  258.0 4.3 %slice-start.3 = ((s8[4718592]{0:T(1024)(128)(4,1)}), s8[524288]{0:T(1024)(128)(4,1)S(1)}, s32[]{:S(2)}) async-start(s8[4718592]{0:T(1024)(128)(4,1)} %bitcast.30), calls=%async_computation.3 | async-start | bytes 1048576
  261.3 4.3 %slice-start = ((s8[4718592]{0:T(1024)(128)(4,1)}), s8[4194304]{0:T(1024)(128)(4,1)S(1)}, s32[]{:S(2)}) async-start(s8[4718592]{0:T(1024)(128)(4,1)} %bitcast.28), calls=%async_computation | async-start | bytes 8388608
  262.3 3.5 %slice-start.1 = ((s8[4718592]{0:T(1024)(128)(4,1)}), s8[524288]{0:T(1024)(128)(4,1)S(1)}, s32[]{:S(2)}) async-start(s8[4718592]{0:T(1024)(128)(4,1)} %bitcast.28), calls=%async_computation.1 | async-start | bytes 1048576

commit v6 on v5

--- a/solution.py
+++ b/solution.py
@@ -29,7 +29,7 @@
         self.mid = (self.z == 1) | (self.z == 2)
 
 
-def sum_barrier(pos):
+def sum_greet(pos):
     barrier = pltpu.get_barrier_semaphore()
 
     def greet(dev):
@@ -43,7 +43,9 @@
     def _():
         greet(pos.zm)
 
-    pl.semaphore_wait(barrier, jnp.where(pos.mid, 4, 3))
+
+def sum_met(pos):
+    pl.semaphore_wait(pltpu.get_barrier_semaphore(), jnp.where(pos.mid, 4, 3))
 
 
 def make_tick(pos, grads, from_core, from_one, from_two, from_three, sent, got, credit, count, finish):
@@ -269,15 +271,18 @@
 
 CR, CC = 64, 384
 CHUNKS = 24
-RELAY = 2
+RELAY = 3
 BF = jnp.bfloat16
 
 
-def gather_barrier(pos, other):
+def gather_greet(pos, other):
     barrier = pltpu.get_barrier_semaphore()
     for where in ({"tensor": other}, {"dp": pos.xn}, {"dp": pos.zp}, {"dp": pos.sib}):
         pl.semaphore_signal(barrier, inc=1, device_id=where, device_id_type=MESH)
-    pl.semaphore_wait(barrier, 4)
+
+
+def gather_met():
+    pl.semaphore_wait(pltpu.get_barrier_semaphore(), 4)
 
 
 def chunk_parts(piece, chunk, kind):
@@ -287,7 +292,7 @@
         return [(piece * 64 + (chunk - 6) * 32, 32, 384 * q, 32 * q) for q in range(2)]
     if kind == 2:
         return [(piece * 128 + (chunk - 8) * 16, 16, 384 * q, 16 * q) for q in range(4)]
-    return [(piece * 256 + (chunk - 16) * 32, 32, 384 * q, 32 * q) for q in range(2)]
+    return [((chunk - 16) * 192 + piece * 32, 32, 384 * q, 32 * q) for q in range(2)]
 
 
 BOUNDS = ((0, 6), (6, 8), (8, 16), (16, 24))
@@ -329,19 +334,20 @@
     def over_core(lane, chunk, piece):
         return copy(lane, chunk, landed.at[piece, chunk], piece, {"dp": pos.sib})
 
-    def stage_own():
-        for kind in range(4):
-            lo, hi = BOUNDS[kind]
-
-            @pl.loop(lo, hi)
-            def _(chunk, kind=kind):
-                for row, rows, column, at in chunk_parts(piece_y, chunk, kind):
-                    staged[chunk, pl.ds(at, rows)] = own[kind][
-                        pl.ds(pl.multiple_of(row, UNIT[kind]), rows), pl.ds(column, CC)
-                    ].astype(jnp.float32)
-
-    def send_own():
-        @pl.loop(0, CHUNKS)
+    def stage_own(kind):
+        lo, hi = BOUNDS[kind]
+
+        @pl.loop(lo, hi)
+        def _(chunk):
+            for row, rows, column, at in chunk_parts(piece_y, chunk, kind):
+                staged[chunk, pl.ds(at, rows)] = own[kind][
+                    pl.ds(pl.multiple_of(row, UNIT[kind]), rows), pl.ds(column, CC)
+                ].astype(jnp.float32)
+
+    def send_own(kind):
+        lo, hi = BOUNDS[kind]
+
+        @pl.loop(lo, hi)
         def _(chunk):
             over_y(chunk).start()
 
@@ -588,15 +594,18 @@
 TILE = 128
 
 
-def row_tiles(rows, body):
-    full = rows // TILE
+SPLIT = 6 * TILE
+
+
+def row_tiles(first, last, body):
+    full = (last - first) // TILE
 
     @pl.loop(0, full)
     def _(i):
-        body(pl.ds(pl.multiple_of(i * TILE, TILE), TILE))
-
-    if rows % TILE:
-        body(pl.ds(full * TILE, rows % TILE))
+        body(pl.ds(pl.multiple_of(first + i * TILE, TILE), TILE))
+
+    if (last - first) % TILE:
+        body(pl.ds(first + full * TILE, (last - first) % TILE))
 
 
 def forward_kernel(
@@ -613,10 +622,10 @@
     shift_two,
     tokens_h,
     grad_h,
-    own_qkv,
-    own_out,
-    own_up,
-    own_down,
+    qkv_in,
+    out_in,
+    up_in,
+    down_in,
     *rest,
 ):
     count = 0 if fast else 5
@@ -643,6 +652,10 @@
     ) = outs
     (
         tokens,
+        own_qkv,
+        own_out,
+        own_up,
+        own_down,
         their_qkv,
         their_out,
         their_up,
@@ -683,14 +696,23 @@
     put_normed = move(4, normed, normed_h)
     put_hidden = move(5, hidden, hidden_h)
     put_acted = move(6, acted, acted_h)
-    put_two = move(7, acc_own, d_two_h)
-    put_ffn = move(8, hidden, d_ffn_h)
-    put_output = move(9, tokens, output_h)
+    late = ((acc_own, d_two_h), (hidden, d_ffn_h), (tokens, output_h))
+    put_late = [
+        [move(7 + 3 * part + i, ref.at[rows_of], target.at[rows_of]) for i, (ref, target) in enumerate(late)]
+        for part, rows_of in enumerate((pl.ds(0, SPLIT), pl.ds(SPLIT, rows - SPLIT)))
+    ]
     put_theirs = [
-        move(10 + i, ref, target)
+        move(13 + i, ref, target)
         for i, (ref, target) in enumerate(zip(theirs, (their_qkv_h, their_out_h, their_up_h, their_down_h)))
     ]
+    load_own = [move(17 + i, a, b) for i, (a, b) in enumerate(zip((qkv_in, out_in, up_in, down_in), own))]
+    if fast:
+        pos = Place()
+        gather_greet(pos, 1 - lax.axis_index("tensor"))
+    load_own[0].start()
     load_tokens.start()
+    for copy in load_own[1:]:
+        copy.start()
     done = [0]
     small[...] = jnp.zeros(small.shape, F32)
     small[0:1, :] = bias_qv[0:1, :]
@@ -698,16 +720,22 @@
     for c in range(units // CHUNK):
         small[3 + c : 4 + c, 0:CHUNK] = flat_row(bias_up, c * CHUNK, CHUNK)
     if fast:
-        pos = Place()
         small_sem, *wires = wires
         stage_own, send_own, tick = make_gather(pos, own, theirs, *wires)
-        stage_own()
-        gather_barrier(pos, 1 - lax.axis_index("tensor"))
+        load_own[0].wait()
+        stage_own(0)
+        gather_met()
+        send_own(0)
         swap = swap_small(small, small_their, small_sem)
         swap.start()
-        send_own()
+        for kind in range(1, 4):
+            load_own[kind].wait()
+            stage_own(kind)
+            send_own(kind)
     else:
-        copies = [move(10 + i, a, b) for i, (a, b) in enumerate(zip(given, theirs + (small_their,)))]
+        for copy in load_own:
+            copy.wait()
+        copies = [move(13 + i, a, b) for i, (a, b) in enumerate(zip(given, theirs + (small_their,)))]
         for copy in copies:
             copy.start()
         for copy in copies:
@@ -719,6 +747,13 @@
     def ticks(index, each, trips):
         for i in range(each):
             tick(done[0] + index * each + i)
+
+    def tick_every(index, every, trips):
+        @pl.when(lax.rem(index, every) == 0)
+        def _():
+            tick(done[0] + index // every)
+
+        return -(-trips // every)
 
     def until(count):
         if done[0] < count:
@@ -745,9 +780,7 @@
         def _(c, half=half, weights=weights, table=table):
             part = mm(tokens[...], weights[pl.ds(pl.multiple_of(c * depth, depth), depth), :])
             qkv[half, c] = (part + table[pl.ds(c, 1), :]).astype(BF)
-            ticks(c, GATHER[2 * half], 3)
-
-        done[0] += 3 * GATHER[2 * half]
+
         q, k, v = (qkv.at[half, i] for i in range(3))
         kmem[...] = mm(select[...], k[...]).astype(BF)
         vmem[...] = mm(select[...], v[...]).astype(BF)
@@ -766,24 +799,30 @@
                 attend_pair(
                     q, k, v, kmem, vmem, colbias, mixed.at[half], probs.at[lax.rem(s, 2), pair], s, pl.ds(pair * PAIR, PAIR)
                 )
-                if pair < GATHER[2 * half + 1]:
-                    tick(done[0] + s * GATHER[2 * half + 1] + pair)
+                if pair == 0 and half == 0:
+                    tick(done[0] + s)
+                if pair == 2 and half == 1:
+                    tick_every(s, GATHER[0], SEGS)
             put_probs(s).start()
 
-        done[0] += SEGS * GATHER[2 * half + 1]
+        done[0] += SEGS if half == 0 else -(-SEGS // GATHER[0])
         put_probs(SEGS - 2).wait()
         put_probs(SEGS - 1).wait()
+
+        if half == 1:
+            until(BOUNDS[1][1] + 3 * RELAY)
+        out = (own_out, their_out)[half]
+
+        @pl.loop(0, 3)
+        def _(n, half=half, out=out):
+            columns = pl.ds(pl.multiple_of(n * CHUNK, CHUNK), CHUNK)
+            part = mm(mixed[half], out[:, columns])
+            acc_own[:, columns] = part if half == 0 else acc_own[:, columns] + part
+            ticks(n, GATHER[1 + half], 3)
+
+        done[0] += 3 * GATHER[1 + half]
     put_qkv.start()
     put_mixed.start()
-    until(BOUNDS[1][1] + 3 * RELAY)
-
-    @pl.loop(0, 3)
-    def _(n):
-        columns = pl.ds(pl.multiple_of(n * CHUNK, CHUNK), CHUNK)
-        acc_own[:, columns] = mm(mixed[0], own_out[:, columns]) + mm(mixed[1], their_out[:, columns])
-        ticks(n, GATHER[4], 3)
-
-    done[0] += 3 * GATHER[4]
 
     def norm_one(span):
         resid = tokens[span, :].astype(F32) + (acc_own[span, :] + flat_row(bias_out, 0, depth))
@@ -792,7 +831,7 @@
         inverse[span, :] = scale
         hidden[span, :] = (unit * flat_row(gain_one, 0, depth) + flat_row(shift_one, 0, depth)).astype(BF)
 
-    row_tiles(rows, norm_one)
+    row_tiles(0, rows, norm_one)
     load_grad.start()
     put_normed.start()
     put_hidden.start()
@@ -826,24 +865,40 @@
             acted[:, span] = act
             slopes[lax.rem(c, 2)] = steep
             put_slope(c).start()
-            ticks(c, GATHER[5 + 2 * half], 6)
-
-        done[0] += 6 * GATHER[5 + 2 * half]
+            tick_every(c, GATHER[3 + 2 * half], 6)
+
+        done[0] += -(-6 // GATHER[3 + 2 * half])
+        low, high = slice(0, units // 2), slice(units // 2, units)
         if half == 0:
             put_acted.start()
+
+            @pl.loop(0, 3)
+            def _(n, down=down, acc=acc):
+                columns = pl.ds(pl.multiple_of(n * CHUNK, CHUNK), CHUNK)
+                acc[:, columns] = mm(acted[:, low], down[low, columns]) + mm(acted[:, high], down[high, columns])
+                ticks(n, GATHER[4], 3)
+
         else:
+            until((BOUNDS[3][0] + BOUNDS[3][1]) // 2 + 3 * RELAY)
+
+            @pl.loop(0, 3)
+            def _(n, down=down, acc=acc):
+                columns = pl.ds(pl.multiple_of(n * CHUNK, CHUNK), CHUNK)
+                acc[:, columns] = mm(acted[:, low], down[low, columns])
+                ticks(n, 1, 3)
+
+            done[0] += 3
             until(BOUNDS[3][1] + 3 * RELAY)
             if fast:
                 for copy in put_theirs:
                     copy.start()
 
-        @pl.loop(0, 3)
-        def _(n, half=half, down=down, acc=acc):
-            columns = pl.ds(pl.multiple_of(n * CHUNK, CHUNK), CHUNK)
-            acc[:, columns] = mm(acted[...], down[:, columns])
-            ticks(n, GATHER[6 + 2 * half], 3)
-
-        done[0] += 3 * GATHER[6 + 2 * half]
+            @pl.loop(0, 3)
+            def _(n, down=down, acc=acc):
+                columns = pl.ds(pl.multiple_of(n * CHUNK, CHUNK), CHUNK)
+                acc[:, columns] = acc[:, columns] + mm(acted[:, high], down[high, columns])
+
+        done[0] += 3 * GATHER[4] if half == 0 else 0
     put_slope(4).wait()
     put_slope(5).wait()
 
@@ -864,22 +919,24 @@
         for index, value in enumerate((low.astype(F32), grad * unit, grad)):
             sums[index] = sums[index] + value.reshape(-1, 8, depth).sum(axis=0)
 
-    row_tiles(rows, norm_two)
-    put_two.start()
-    put_ffn.start()
-    put_output.start()
+    row_tiles(0, SPLIT, norm_two)
+    for copy in put_late[0]:
+        copy.start()
+    row_tiles(SPLIT, rows, norm_two)
+    for copy in put_late[1]:
+        copy.start()
     for index in range(3):
         total = jnp.sum(sums[index], axis=0, keepdims=True)
         for j in range(6):
             vec[6 * index + j : 6 * index + j + 1, :] = total[:, BC * j : BC * (j + 1)]
-    for copy in (put_qkv, put_mixed, put_normed, put_two, put_ffn, put_output):
+    for copy in (put_qkv, put_mixed, put_normed, *put_late[0], *put_late[1]):
         copy.wait()
     if fast:
         for copy in put_theirs:
             copy.wait()
 
 
-GATHER = (0, 1, 1, 1, 0, 1, 0, 0, 0)
+GATHER = (2, 1, 1, 2, 1, 2)
 
 
 def forward(fast, parent, slots, vectors, tokens, grad_out, own, given):
@@ -910,10 +967,11 @@
     return pl.pallas_call(
         functools.partial(forward_kernel, fast),
         out_shape=out_shape,
-        in_specs=[sm, sm] + [vm] * len(vectors) + [hbm, hbm] + [vm] * 4 + [hbm] * len(given),
+        in_specs=[sm, sm] + [vm] * len(vectors) + [hbm, hbm] + [hbm] * (4 + len(given)),
         out_specs=[hbm] * 8 + [vm] + [hbm] * 6 + [vm, hbm, vm],
         scratch_shapes=[
             pltpu.VMEM((rows, depth), BF),
+            *[pltpu.VMEM(w.shape, BF) for w in own],
             *[pltpu.VMEM(w.shape, BF) for w in own],
             pltpu.VMEM((16, width), F32),
             pltpu.VMEM((16, width), F32),
@@ -930,7 +988,7 @@
             pltpu.VMEM((MEMP, width), BF),
             pltpu.VMEM((3, 8, depth), F32),
             pltpu.VMEM((2, width // PAIR, 2 * WIN, WIN + MEMP), BF),
-            pltpu.SemaphoreType.DMA((15,)),
+            pltpu.SemaphoreType.DMA((21,)),
             pltpu.SemaphoreType.DMA((2,)),
             pltpu.SemaphoreType.DMA((2,)),
         ]
@@ -1052,6 +1110,9 @@
         for copy in copies:
             copy.wait()
 
+    if fast:
+        pos = Place()
+        sum_greet(pos)
     load_d.start()
     load_acted(0).start()
     start(load_chunk(0, 0))
@@ -1102,7 +1163,6 @@
             put(block, g_vec).start()
 
     if fast:
-        pos = Place()
         tick = make_tick(pos, grads, *wires, COUNT, finish)
         last = COUNT + 7 * SPREAD
     else:
@@ -1126,7 +1186,7 @@
     acc_their[...] = jnp.zeros(acc_their.shape, F32)
     sums[...] = jnp.zeros(sums.shape, F32)
     if fast:
-        sum_barrier(pos)
+        sum_met(pos)
 
     load_d.wait()
 
@@ -1379,6 +1439,57 @@
     )(select, inverse, gain, vec_in, *arrays)
 
 
+def results_kernel(count, vec, *refs):
+    sources, rest = refs[:count], refs[count:]
+    targets, rest = rest[:count], rest[count:]
+    vectors, rest = rest[:8], rest[8:]
+    buffers, (in_sem, out_sem) = rest[:count], rest[count:]
+    pieces = []
+    for i, source in enumerate(sources):
+        rows = source.shape[0]
+        parts = max(1, rows * source.shape[1] * source.dtype.itemsize // 2**20)
+        while rows % parts or (rows // parts) % 16:
+            parts -= 1
+        size = rows // parts
+        for part in range(parts):
+            at = pl.ds(part * size, size)
+            pieces.append((source.at[at], buffers[i].at[at], targets[i].at[at]))
+    loads = [pltpu.make_async_copy(a, b, in_sem.at[i]) for i, (a, b, c) in enumerate(pieces)]
+    stores = [pltpu.make_async_copy(b, c, out_sem.at[i]) for i, (a, b, c) in enumerate(pieces)]
+    for load in loads:
+        load.start()
+    bias_qv, *flat = vectors
+    for j in range(6):
+        bias_qv[j // 3 : j // 3 + 1, BC * (j % 3) : BC * (j % 3 + 1)] = vec[j : j + 1, :]
+    row = 6
+    for ref in flat:
+        for j in range(ref.shape[0] // BC):
+            ref[pl.ds(BC * j, BC)] = vec[row, :]
+            row += 1
+    for load, store in zip(loads, stores):
+        load.wait()
+        store.start()
+    for store in stores:
+        store.wait()
+
+
+def results(vec, large, width, units, depth):
+    vm = pl.BlockSpec(memory_space=pltpu.VMEM)
+    hbm = pl.BlockSpec(memory_space=pl.ANY)
+    sd = jax.ShapeDtypeStruct
+    small = [sd((2, width), F32), sd((units,), F32)] + [sd((depth,), F32)] * 6
+    count = len(large)
+    return pl.pallas_call(
+        functools.partial(results_kernel, count),
+        out_shape=[sd(a.shape, a.dtype) for a in large] + small,
+        in_specs=[vm] + [hbm] * count,
+        out_specs=[hbm] * count + [vm] * len(small),
+        scratch_shapes=[pltpu.VMEM(a.shape, a.dtype) for a in large] + [pltpu.SemaphoreType.DMA((32,))] * 2,
+        compiler_params=pltpu.CompilerParams(vmem_limit_bytes=60 * 2**20),
+        name="results",
+    )(vec, *large)
+
+
 def halves_swap(own, small):
     unit = (lax.axis_index("dp") >= 0).astype(F32)
 
@@ -1444,17 +1555,27 @@
     )
     if not fast:
         g_w_qkv, g_w_out, g_w_up, g_w_down, flat = lax.psum((g_w_qkv, g_w_out, g_w_up, g_w_down, flat), "dp")
-    g_w_qkv = g_w_qkv.reshape(w_qkv.shape)
-    sums, row = [], 0
-    for size in (width, width, hidden_units) + (depth,) * 6:
-        sums.append(flat[row : row + size // BC].reshape(-1))
-        row += size // BC
-    g_bias_q, g_bias_v, g_bias_up, g_bias_out, g_gain_one, g_shift_one, g_bias_down, g_gain_two, g_shift_two = sums
+    (
+        g_w_qkv,
+        g_w_out,
+        g_w_up,
+        g_w_down,
+        grad_tokens,
+        output,
+        g_bias_qv,
+        g_bias_up,
+        g_bias_out,
+        g_gain_one,
+        g_shift_one,
+        g_bias_down,
+        g_gain_two,
+        g_shift_two,
+    ) = results(flat, (g_w_qkv, g_w_out, g_w_up, g_w_down, grad_tokens, output), width, hidden_units, depth)
     return (
         output,
         grad_tokens,
-        g_w_qkv,
-        jnp.stack([g_bias_q, g_bias_v]),
+        g_w_qkv.reshape(w_qkv.shape),
+        g_bias_qv,
         g_w_out,
         g_bias_out,
         g_gain_one,

time: 270 us -> 257 us (0.952)
  local copies, waits for them, and re-layouts: 17.7 us -> 0 us
  Pallas kernels: 249 us -> 256 us
    unnamed x21 -> x0, local copies, waits for them, and re-layouts: 15 us -> none
    pallas_call x0 -> x1, Pallas kernels: none -> 14.5 us  [results(): pl.pallas_call(functools.partial(results_kernel, count), out_shape=[sd(a....]
    pallas_call x1, Pallas kernels: 96.2 us -> 90 us  [forward(): pl.pallas_call(functools.partial(forward_kernel, fast), out_shape=out_sha...]
    reshape x2 -> x0, local copies, waits for them, and re-layouts: 2.7 us -> none  [shards(): sums.append(flat[row:row + size // BC].reshape(-1))]
where the time goes in v6:
time: 257 us
  Pallas kernels  256 us (100%)
    pallas_call x1, Pallas kernels, backward(): pl.pallas_call(functools.partial(backward_kernel, fast), out_shape=[sd((3...  152 us
    pallas_call x1, Pallas kernels, forward(): pl.pallas_call(functools.partial(forward_kernel, fast), out_shape=out_sha...  90 us
    pallas_call x1, Pallas kernels, results(): pl.pallas_call(functools.partial(results_kernel, count), out_shape=[sd(a....  14.5 us

profile of v6, /device:TPU:0, one launch (start us, length us, event | category | flops | bytes accessed | tf_op | source)
XLA Modules:
  0.0 257.0 jit_solution(14184176949285634254)
XLA Ops:
  0.6 90.0 %forward.1 = (bf16[1184,768]{1,0:T(8,128)(2,1)}, bf16[2304,384]{1,0:T(8,128)(2,1)}, bf16[384,768]{1,0:T(8,128)(2,1)}, bf16[768,1536]{1,0:T(8,128)(2,1)}, bf16[15...) custom-call(s32[8]{0:T(128)} %parent.1, ...), custom_call_target="tpu_custom_call" | custom-call | tf_op jit(solution)/shard_map/forward/pallas_call | solution.py:967
  90.7 151.7 %backward.1 = (f32[2304,384]{1,0:T(8,128)}, f32[384,768]{1,0:T(8,128)}, f32[768,1536]{1,0:T(8,128)}, f32[1536,768]{1,0:T(8,128)}, f32[384,128]{1,0:T(8,128)}, /*index=5*/bf16[1184,768]{1,0:T(8,128)(2,1)}) custom-call(bf16[96,1184]{1,0:T(8,128)(2,1)} %get-tuple-element.52.select, f32[1184,1]{1,0:T(8,128)} %get-tuple-element.53.inverse, f32[768]{0:T(1024)} %gain.1, ...), custom_call_target="tpu_custom_call" | custom-call | tf_op jit(solution)/shard_map/backward/pallas_call | solution.py:1391
  242.4 14.5 %results.1 = (f32[2304,384]{1,0:T(8,128)}, f32[384,768]{1,0:T(8,128)}, f32[768,1536]{1,0:T(8,128)}, f32[1536,768]{1,0:T(8,128)}, bf16[1184,768]{1,0:T(8,128)(2,1...) custom-call(f32[384,128]{1,0:T(8,128)} %get-tuple-element.69.vec, ...), custom_call_target="tpu_custom_call" | custom-call | tf_op jit(solution)/shard_map/results/pallas_call | solution.py:1482

commit v7 on v6

--- a/solution.py
+++ b/solution.py
@@ -481,14 +481,16 @@
         colbias[s : s + 1, :] = jnp.where(jnp.maximum(inside, reach[s]) > 0.0, 0.0, MASKED)
 
 
-def build_select(slots, select):
-    row = lax.broadcasted_iota(jnp.int32, (select.shape[0], 1), 0)
-    where = jnp.full((select.shape[0], 1), -1, jnp.int32)
-    for t in range(SEGS):
-        for m in range(MEMW):
-            where = jnp.where(row == MEMW * t + m, slots[t, m] + SEG * t, where)
-    place = lax.broadcasted_iota(jnp.int32, select.shape, 1)
-    select[...] = (where == place).astype(F32).astype(BF)
+def build_select(slots, select, select_t):
+    for ref, axis in ((select, 0), (select_t, 1)):
+        shape = (ref.shape[0], 1) if axis == 0 else (1, ref.shape[1])
+        entry = lax.broadcasted_iota(jnp.int32, shape, axis)
+        where = jnp.full(shape, -1, jnp.int32)
+        for t in range(SEGS):
+            for m in range(MEMW):
+                where = jnp.where(entry == MEMW * t + m, slots[t, m] + SEG * t, where)
+        place = lax.broadcasted_iota(jnp.int32, ref.shape, 1 - axis)
+        ref[...] = (where == place).astype(F32).astype(BF)
 
 
 def window(s):
@@ -560,10 +562,10 @@
     dvmem[:, columns] = dvmem[:, columns] + dvs[WIN:]
 
 
-def spread(select, part):
+def spread(select_t, part):
     high = part.astype(BF)
     low = (part - high.astype(F32)).astype(BF)
-    return t_mm(select, high) + t_mm(select, low)
+    return mm(select_t, high) + mm(select_t, low)
 
 
 def norm_stats(values):
@@ -629,7 +631,7 @@
     *rest,
 ):
     count = 0 if fast else 5
-    given, outs, rest = rest[:count], rest[count : count + 18], rest[count + 18 :]
+    given, outs, rest = rest[:count], rest[count : count + 19], rest[count + 19 :]
     (
         output_h,
         their_qkv_h,
@@ -648,7 +650,8 @@
         d_ffn_h,
         vec,
         probs_h,
-        select,
+        select_t,
+        memory,
     ) = outs
     (
         tokens,
@@ -671,8 +674,7 @@
         acted,
         slopes,
         colbias,
-        kmem,
-        vmem,
+        select,
         sums,
         probs,
         io_sem,
@@ -765,7 +767,7 @@
             done[0] = count
 
     build_masks(parent, lax.axis_index("dp") * SEGS, colbias)
-    build_select(slots, select)
+    build_select(slots, select, select_t)
     load_tokens.wait()
     pairs = width // PAIR
     for half in range(2):
@@ -782,6 +784,7 @@
             qkv[half, c] = (part + table[pl.ds(c, 1), :]).astype(BF)
 
         q, k, v = (qkv.at[half, i] for i in range(3))
+        kmem, vmem = memory.at[half, 0], memory.at[half, 1]
         kmem[...] = mm(select[...], k[...]).astype(BF)
         vmem[...] = mm(select[...], v[...]).astype(BF)
 
@@ -790,7 +793,7 @@
             return pltpu.make_async_copy(probs.at[slot], probs_h.at[half, s], probs_sem.at[slot])
 
         @pl.loop(0, SEGS)
-        def _(s, half=half, q=q, k=k, v=v, put_probs=put_probs):
+        def _(s, half=half, q=q, k=k, v=v, kmem=kmem, vmem=vmem, put_probs=put_probs):
             @pl.when(s >= 2)
             def _():
                 put_probs(s - 2).wait()
@@ -962,13 +965,14 @@
         sd((rows, depth), BF),
         sd((18, BC), F32),
         sd((2, SEGS, width // PAIR, 2 * WIN, WIN + MEMP), BF),
-        sd((MEMP, rows), BF),
+        sd((rows, MEMP), BF),
+        sd((2, 2, MEMP, width), BF),
     ]
     return pl.pallas_call(
         functools.partial(forward_kernel, fast),
         out_shape=out_shape,
         in_specs=[sm, sm] + [vm] * len(vectors) + [hbm, hbm] + [hbm] * (4 + len(given)),
-        out_specs=[hbm] * 8 + [vm] + [hbm] * 6 + [vm, hbm, vm],
+        out_specs=[hbm] * 8 + [vm] + [hbm] * 6 + [vm, hbm, vm, vm],
         scratch_shapes=[
             pltpu.VMEM((rows, depth), BF),
             *[pltpu.VMEM(w.shape, BF) for w in own],
@@ -984,8 +988,7 @@
             pltpu.VMEM((rows, units), BF),
             pltpu.VMEM((2, rows, CHUNK), BF),
             pltpu.VMEM((SEGS, WIN + MEMP), F32),
-            pltpu.VMEM((MEMP, width), BF),
-            pltpu.VMEM((MEMP, width), BF),
+            pltpu.VMEM((MEMP, rows), BF),
             pltpu.VMEM((3, 8, depth), F32),
             pltpu.VMEM((2, width // PAIR, 2 * WIN, WIN + MEMP), BF),
             pltpu.SemaphoreType.DMA((21,)),
@@ -1008,7 +1011,8 @@
 
 def backward_kernel(
     fast,
-    select,
+    select_t,
+    memory,
     inverse,
     gain,
     vec_in,
@@ -1031,12 +1035,6 @@
     w_out_their,
     w_qkv_own,
     w_qkv_their,
-    g_qkv,
-    g_out,
-    g_up,
-    g_down,
-    g_vec,
-    g_tokens,
     grads,
     d_low,
     hidden,
@@ -1058,13 +1056,10 @@
     d_qkv,
     d_mixed,
     probs,
-    kmem,
-    vmem,
     dkm,
     dvm,
     load_sem,
     chunk_sem,
-    put_sem,
     probs_sem,
     *wires,
 ):
@@ -1083,7 +1078,6 @@
     load_w = [fetch(7 + i, w, w_qkv.at[i]) for i, w in enumerate((w_qkv_own, w_qkv_their))]
     load_tokens = fetch(9, tokens_h, tokens)
     load_qkv = [fetch(10 + half, qkv_h.at[half], qkv) for half in range(2)]
-    put_tokens = fetch(12, d_low, g_tokens)
 
     def load_acted(c):
         return pltpu.make_async_copy(acted_h.at[:, pl.ds(pl.multiple_of(c * BR, BR), BR)], a_buf.at[lax.rem(c, 2)], chunk_sem.at[0, lax.rem(c, 2)])
@@ -1126,41 +1120,8 @@
     load_qkv[0].start()
     load_probs(0, 0).start()
 
-    def put(block, target):
-        return pltpu.make_async_copy(grads.at[block], target, put_sem.at[lax.rem(block, 8)])
-
-    def wait_put(block):
-        put(block, g_vec).wait()
-
     def finish(block):
-        @pl.when(block >= 8)
-        def _():
-            wait_put(block - 8)
-
-        def at(row, column):
-            return pl.ds(pl.multiple_of(row, BR), BR), pl.ds(pl.multiple_of(column, BC), BC)
-
-        @pl.when(block < UP)
-        def _():
-            put(block, g_down.at[at(BR * (block // 6), BC * lax.rem(block, 6))]).start()
-
-        @pl.when((block >= UP) & (block < OUT))
-        def _():
-            i = block - UP
-            put(block, g_up.at[at(BR * lax.rem(i // 2, 2), CHUNK * (i // 4) + BC * lax.rem(i, 2))]).start()
-
-        @pl.when((block >= OUT) & (block < QKV))
-        def _():
-            put(block, g_out.at[at(0, BC * (block - OUT))]).start()
-
-        @pl.when((block >= QKV) & (block < VEC))
-        def _():
-            i = block - QKV
-            put(block, g_qkv.at[at(BR * (i // 3), BC * lax.rem(i, 3))]).start()
-
-        @pl.when(block == VEC)
-        def _():
-            put(block, g_vec).start()
+        pass
 
     if fast:
         tick = make_tick(pos, grads, *wires, COUNT, finish)
@@ -1168,9 +1129,7 @@
     else:
 
         def tick(step):
-            @pl.when(step < COUNT)
-            def _():
-                finish(step)
+            pass
 
         last = COUNT
     done = [0]
@@ -1248,12 +1207,7 @@
 
     load_two.wait()
     load_normed.wait()
-    tile = 32
-    trips = rows // tile
-
-    @pl.loop(0, trips)
-    def _(i):
-        span = pl.ds(pl.multiple_of(i * tile, tile), tile)
+    def norm_one(span):
         total = d_res[span, :] + (acc_own[span, :] + acc_their[span, :])
         unit = normed[span, :]
         one = norm_back(total, unit, inverse[span, :], flat_row(gain, 0, depth))
@@ -1261,12 +1215,20 @@
         low = one.astype(BF)
         d_low[span, :] = low
         for index, value in enumerate((low.astype(F32), total * unit, total)):
-            sums[index] = sums[index] + value.reshape(tile // 8, 8, depth).sum(axis=0)
+            sums[index] = sums[index] + value.reshape(-1, 8, depth).sum(axis=0)
+
+    trips = rows // NORM_TILE
+
+    @pl.loop(0, trips)
+    def _(i):
+        norm_one(pl.ds(pl.multiple_of(i * NORM_TILE, NORM_TILE), NORM_TILE))
 
         @pl.when(lax.rem(i, TICK_TILES) == 0)
         def _():
             tick(done[0] + i // TICK_TILES)
 
+    if rows % NORM_TILE:
+        norm_one(pl.ds(trips * NORM_TILE, rows % NORM_TILE))
     done[0] += -(-trips // TICK_TILES)
     for index in range(3):
         total = jnp.sum(sums[index], axis=0, keepdims=True)
@@ -1293,17 +1255,18 @@
     for half in range(2):
         load_qkv[half].wait()
         q, k, v = (qkv.at[i] for i in range(3))
-        kmem[...] = mm(select[...], k[...]).astype(BF)
-        vmem[...] = mm(select[...], v[...]).astype(BF)
+        kmem, vmem = memory.at[half, 0], memory.at[half, 1]
         acc_their[...] = jnp.zeros(acc_their.shape, F32)
         dkm[...] = jnp.zeros(dkm.shape, F32)
         dvm[...] = jnp.zeros(dvm.shape, F32)
 
-        @pl.loop(0, SEGS * pairs)
-        def _(spot, half=half):
-            s, pair = spot // pairs, lax.rem(spot, pairs)
-
-            @pl.when(pair == 0)
+        group = UNROLL[half]
+
+        @pl.loop(0, SEGS * pairs // group)
+        def _(trip, half=half, group=group, kmem=kmem, vmem=vmem):
+            s, first = trip * group // pairs, lax.rem(trip * group, pairs)
+
+            @pl.when(first == 0)
             def _():
                 load_probs(half, s).wait()
 
@@ -1317,23 +1280,24 @@
                     def _():
                         load_probs(1, 0).start()
 
-            columns = pl.ds(pl.multiple_of(pair * PAIR, PAIR), PAIR)
-            part = probs.at[lax.rem(s, 2), pair]
-            attend_back_pair(q, k, v, kmem, vmem, part, d_mixed.at[half], d_qkv.at[0], dka, dva, dkm, dvm, s, columns)
-
-            @pl.when(lax.rem(spot, TICKS[4 + half]) == 0)
-            def _():
-                tick(done[0] + spot // TICKS[4 + half])
+            for i in range(group):
+                pair = i if group == pairs else first
+                columns = pl.ds(pl.multiple_of(pair * PAIR, PAIR), PAIR)
+                part = probs.at[lax.rem(s, 2), pair]
+                attend_back_pair(q, k, v, kmem, vmem, part, d_mixed.at[half], d_qkv.at[0], dka, dva, dkm, dvm, s, columns)
+                spot = trip * group + i
+
+                @pl.when(lax.rem(spot, TICKS[4 + half]) == 0)
+                def _(spot=spot):
+                    tick(done[0] + spot // TICKS[4 + half])
 
         done[0] += -(-SEGS * pairs // TICKS[4 + half])
         if half == 0:
             assert done[0] <= QKV
         if half == 0:
             load_qkv[1].start()
-        for pair in range(pairs):
-            columns = pl.ds(pair * PAIR, PAIR)
-            d_qkv[1, :, columns] = ((dka[:, columns] + spread(select[...], dkm[:, columns])) * HD ** (-0.5)).astype(BF)
-            d_qkv[2, :, columns] = (dva[:, columns] + spread(select[...], dvm[:, columns])).astype(BF)
+        d_qkv[1] = ((dka[...] + spread(select_t[...], dkm[...])) * HD ** (-0.5)).astype(BF)
+        d_qkv[2] = (dva[...] + spread(select_t[...], dvm[...])).astype(BF)
         if half == 0:
 
             @pl.loop(0, 3)
@@ -1366,43 +1330,31 @@
                 ticks(c, TICKS[7], 3)
 
             done[0] += 3 * TICKS[7]
-            put_tokens.start()
     @pl.loop(min(done[0], last), last)
     def _(step):
         tick(step)
 
-    for block in range(COUNT - 8, COUNT):
-        wait_put(block)
-    put_tokens.wait()
-
 
 TICKS = (1, 3, 2, 1, 2, 1, 3, 1)
-TICK_TILES = 8
-
-
-def backward(fast, select, inverse, gain, vec_in, arrays):
+TICK_TILES = 2
+NORM_TILE = 128
+UNROLL = (3, 1)
+
+
+def backward(fast, select_t, memory, inverse, gain, vec_in, arrays):
     tokens, acted, mixed = arrays[0], arrays[5], arrays[9]
     rows, depth = tokens.shape
     units = acted.shape[1]
     width = mixed.shape[1]
     vm = pl.BlockSpec(memory_space=pltpu.VMEM)
     hbm = pl.BlockSpec(memory_space=pl.ANY)
-    sd = jax.ShapeDtypeStruct
+    kept = pltpu.VMEM if fast else jax.ShapeDtypeStruct
     return pl.pallas_call(
         functools.partial(backward_kernel, fast),
-        out_shape=[
-            sd((3 * depth, width), F32),
-            sd((width, depth), F32),
-            sd((depth, units), F32),
-            sd((units, depth), F32),
-            sd((BR, BC), F32),
-            sd((rows, depth), BF),
-        ],
-        in_specs=[vm, vm, vm, vm] + [hbm] * len(arrays),
-        out_specs=[hbm] * 6,
+        out_shape=[kept((COUNT, BR, BC), F32), kept((rows, depth), BF)],
+        in_specs=[vm, vm, vm, vm, vm] + [hbm] * len(arrays),
+        out_specs=[vm, vm],
         scratch_shapes=[
-            pltpu.VMEM((COUNT, BR, BC), F32),
-            pltpu.VMEM((rows, depth), BF),
             pltpu.VMEM((rows, depth), BF),
             pltpu.VMEM((rows, depth), F32),
             pltpu.VMEM((rows, depth), F32),
@@ -1422,72 +1374,70 @@
             pltpu.VMEM((3, rows, width), BF),
             pltpu.VMEM((2, rows, width), BF),
             pltpu.VMEM((2, width // PAIR, 2 * WIN, WIN + MEMP), BF),
-            pltpu.VMEM((MEMP, width), BF),
-            pltpu.VMEM((MEMP, width), BF),
             pltpu.VMEM((MEMP, width), F32),
             pltpu.VMEM((MEMP, width), F32),
-            pltpu.SemaphoreType.DMA((13,)),
+            pltpu.SemaphoreType.DMA((12,)),
             pltpu.SemaphoreType.DMA((4, 2)),
-            pltpu.SemaphoreType.DMA((8,)),
             pltpu.SemaphoreType.DMA((2,)),
         ]
         + (sum_scratch() if fast else []),
         compiler_params=pltpu.CompilerParams(
-            collective_id=1 if fast else None, has_side_effects=fast, vmem_limit_bytes=67043328
+            collective_id=1 if fast else None, has_side_effects=fast, vmem_limit_bytes=47 * 2**20 if fast else 67043328
         ),
         name="backward",
-    )(select, inverse, gain, vec_in, *arrays)
-
-
-def results_kernel(count, vec, *refs):
-    sources, rest = refs[:count], refs[count:]
-    targets, rest = rest[:count], rest[count:]
-    vectors, rest = rest[:8], rest[8:]
-    buffers, (in_sem, out_sem) = rest[:count], rest[count:]
-    pieces = []
-    for i, source in enumerate(sources):
-        rows = source.shape[0]
-        parts = max(1, rows * source.shape[1] * source.dtype.itemsize // 2**20)
-        while rows % parts or (rows // parts) % 16:
-            parts -= 1
-        size = rows // parts
-        for part in range(parts):
-            at = pl.ds(part * size, size)
-            pieces.append((source.at[at], buffers[i].at[at], targets[i].at[at]))
-    loads = [pltpu.make_async_copy(a, b, in_sem.at[i]) for i, (a, b, c) in enumerate(pieces)]
-    stores = [pltpu.make_async_copy(b, c, out_sem.at[i]) for i, (a, b, c) in enumerate(pieces)]
-    for load in loads:
-        load.start()
+    )(select_t, memory, inverse, gain, vec_in, *arrays)
+
+
+def results_kernel(blocks, grad_tokens, output, g_qkv, g_out, g_up, g_down, tokens_h, output_out, *rest):
+    vectors, (sems, out_sem) = rest[:8], rest[8:]
+    places = [(g_down, BR * (i // 6), BC * (i % 6)) for i in range(24)]
+    places += [(g_up, BR * (i // 2 % 2), CHUNK * (i // 4) + BC * (i % 2)) for i in range(24)]
+    places += [(g_out, 0, BC * i) for i in range(6)]
+    places += [(g_qkv, BR * (i // 3), BC * (i % 3)) for i in range(18)]
+    copies = [
+        pltpu.make_async_copy(blocks.at[i], target.at[pl.ds(row, BR), pl.ds(column, BC)], sems.at[i])
+        for i, (target, row, column) in enumerate(places)
+    ]
+    copies.append(pltpu.make_async_copy(grad_tokens, tokens_h, out_sem.at[0]))
+    copies.append(pltpu.make_async_copy(output, output_out, out_sem.at[1]))
+    for copy in copies:
+        copy.start()
     bias_qv, *flat = vectors
     for j in range(6):
-        bias_qv[j // 3 : j // 3 + 1, BC * (j % 3) : BC * (j % 3 + 1)] = vec[j : j + 1, :]
+        bias_qv[j // 3 : j // 3 + 1, BC * (j % 3) : BC * (j % 3 + 1)] = blocks[VEC, j : j + 1, :]
     row = 6
     for ref in flat:
         for j in range(ref.shape[0] // BC):
-            ref[pl.ds(BC * j, BC)] = vec[row, :]
+            ref[pl.ds(BC * j, BC)] = blocks[VEC, row, :]
             row += 1
-    for load, store in zip(loads, stores):
-        load.wait()
-        store.start()
-    for store in stores:
-        store.wait()
-
-
-def results(vec, large, width, units, depth):
+    for copy in copies:
+        copy.wait()
+
+
+def results(fast, blocks, grad_tokens, output, width, units):
     vm = pl.BlockSpec(memory_space=pltpu.VMEM)
     hbm = pl.BlockSpec(memory_space=pl.ANY)
     sd = jax.ShapeDtypeStruct
+    rows, depth = output.shape
+    if fast:
+        blocks, grad_tokens, output = (
+            pltpu.with_memory_space_constraint(a, pltpu.VMEM) for a in (blocks, grad_tokens, output)
+        )
+    large = [sd((3 * depth, width), F32), sd((width, depth), F32), sd((depth, units), F32), sd((units, depth), F32)]
+    large += [sd((rows, depth), BF)] * 2
     small = [sd((2, width), F32), sd((units,), F32)] + [sd((depth,), F32)] * 6
-    count = len(large)
     return pl.pallas_call(
-        functools.partial(results_kernel, count),
-        out_shape=[sd(a.shape, a.dtype) for a in large] + small,
-        in_specs=[vm] + [hbm] * count,
-        out_specs=[hbm] * count + [vm] * len(small),
-        scratch_shapes=[pltpu.VMEM(a.shape, a.dtype) for a in large] + [pltpu.SemaphoreType.DMA((32,))] * 2,
-        compiler_params=pltpu.CompilerParams(vmem_limit_bytes=60 * 2**20),
+        results_kernel,
+        out_shape=large + small,
+        in_specs=[vm, vm, vm],
+        out_specs=[hbm] * 6 + [vm] * len(small),
+        scratch_shapes=[
+            pltpu.SemaphoreType.DMA((VEC,)),
+            pltpu.SemaphoreType.DMA((2,)),
+        ],
+        compiler_params=pltpu.CompilerParams(vmem_limit_bytes=(8 if fast else 40) * 2**20),
         name="results",
-    )(vec, *large)
+    )(blocks, grad_tokens, output)
 
 
 def halves_swap(own, small):
@@ -1544,17 +1494,16 @@
         d_ffn,
         vec,
         probs,
-        select,
+        select_t,
+        memory,
     ) = forward(fast, parent, mem_slots, vectors, tokens, grad_out, own, given)
     if not fast:
         theirs = given[:4]
     arrays = (tokens, hidden_low, d_ffn, d_two, normed, acted, slope_own, slope_their, qkv, mixed, probs)
     weights = tuple(w[i] for i in (2, 3, 1, 0) for w in (own, theirs))
-    g_w_qkv, g_w_out, g_w_up, g_w_down, flat, grad_tokens = backward(
-        fast, select, inverse, gain_one, vec, arrays + weights
-    )
+    blocks, grad_tokens = backward(fast, select_t, memory, inverse, gain_one, vec, arrays + weights)
     if not fast:
-        g_w_qkv, g_w_out, g_w_up, g_w_down, flat = lax.psum((g_w_qkv, g_w_out, g_w_up, g_w_down, flat), "dp")
+        blocks = lax.psum(blocks, "dp")
     (
         g_w_qkv,
         g_w_out,
@@ -1570,7 +1519,7 @@
         g_bias_down,
         g_gain_two,
         g_shift_two,
-    ) = results(flat, (g_w_qkv, g_w_out, g_w_up, g_w_down, grad_tokens, output), width, hidden_units, depth)
+    ) = results(fast, blocks, grad_tokens, output, width, hidden_units)
     return (
         output,
         grad_tokens,

time: 257 us -> 250 us (0.973)
  Pallas kernels: 256 us -> 248 us
    pallas_call x2, Pallas kernels: 166 us -> 158 us  [the longest x1 150 us: backward(): pl.pallas_call(functools.partial(backward_kernel, fast), out_shape=[kept(...]
where the time goes in v7:
time: 250 us
  Pallas kernels  248 us (99%)
    pallas_call x1, Pallas kernels, backward(): pl.pallas_call(functools.partial(backward_kernel, fast), out_shape=[kept(...  150 us
    pallas_call x1, Pallas kernels, forward(): pl.pallas_call(functools.partial(forward_kernel, fast), out_shape=out_sha...  90.1 us
    pallas_call x1, Pallas kernels, results(): pl.pallas_call(results_kernel, out_shape=large + small, in_specs=[vm, vm,...  7.4 us

profile of v7, /device:TPU:0, one launch (start us, length us, event | category | flops | bytes accessed | tf_op | source)
XLA Modules:
  0.0 250.0 jit_solution(2920276751883792759)
XLA Ops:
  0.6 90.1 %forward.1 = (bf16[1184,768]{1,0:T(8,128)(2,1)}, bf16[2304,384]{1,0:T(8,128)(2,1)}, bf16[384,768]{1,0:T(8,128)(2,1)}, bf16[768,1536]{1,0:T(8,128)(2,1)}, bf16[15...) custom-call(s32[8]{0:T(128)} %parent.1, ...), custom_call_target="tpu_custom_call" | custom-call | tf_op jit(solution)/shard_map/forward/pallas_call | solution.py:971
  90.8 150.1 %backward.1 = (f32[73,384,128]{2,1,0:T(8,128)S(1)}, bf16[1184,768]{1,0:T(8,128)(2,1)S(1)}) custom-call(bf16[1184,96]{1,0:T(8,128)(2,1)} %get-tuple-element.49.select_t, bf16[2,2,96,384]{3,2,1,0:T(8,128)(2,1)} %get-tuple-element.50.memory, f32[1184,1]{1,0:T(8,128)} %get-tuple-element.51.inverse, f32[768]{0:T(1024)} %gain.1, ...), custom_call_target="tpu_custom_call" | custom-call | tf_op jit(solution)/shard_map/backward/pallas_call | solution.py:1352
  240.9 0.0 copy-start
  240.9 1.5 copy-done
  242.4 7.4 %results.1 = (f32[2304,384]{1,0:T(8,128)}, f32[384,768]{1,0:T(8,128)}, f32[768,1536]{1,0:T(8,128)}, f32[1536,768]{1,0:T(8,128)}, bf16[1184,768]{1,0:T(8,128)(2,1...) custom-call(f32[73,384,128]{2,1,0:T(8,128)S(1)} %get-tuple-element.6, ...), custom_call_target="tpu_custom_call" | custom-call | tf_op jit(solution)/shard_map/results/pallas_call | solution.py:1429
Async XLA Ops:
  240.9 1.5 copy-start

commit v8 on v7

--- a/solution.py
+++ b/solution.py
@@ -11,7 +11,7 @@
 
 MESH = pl.DeviceIdType.MESH
 BR, BC = 384, 128
-SPREAD = 3
+AFTER = (0, 3, 6, 9, 12, 15, 18, 21)
 SLOTS = 16
 
 
@@ -241,14 +241,14 @@
             @pl.when(here)
             def _(stages=stages):
                 for index in reversed(range(depth)):
-                    block = step - SPREAD * index
+                    block = step - AFTER[index]
                     if stages[index] is not None:
 
                         @pl.when((block >= 0) & (block < count))
                         def _(index=index, block=block, stages=stages):
                             stages[index](block)
 
-        over = step - SPREAD * (depth - 1)
+        over = step - AFTER[depth - 1]
 
         @pl.when((over >= 0) & (over < count))
         def _():
@@ -271,7 +271,7 @@
 
 CR, CC = 64, 384
 CHUNKS = 24
-RELAY = 3
+HOPS = (3, 6, 7)
 BF = jnp.bfloat16
 
 
@@ -405,15 +405,12 @@
         unpack(chunk)
 
     def tick(step):
-        guarded(step - 3 * RELAY, fourth)
-        guarded(step - 2 * RELAY, third)
-        guarded(step - RELAY, second)
+        guarded(step - HOPS[2], fourth)
+        guarded(step - HOPS[1], third)
+        guarded(step - HOPS[0], second)
         guarded(step, first)
 
     return stage_own, send_own, tick
-
-
-GATHER_TICKS = CHUNKS + 3 * RELAY
 
 
 def gather_scratch():
@@ -774,7 +771,7 @@
         weights = (own_qkv, their_qkv)[half]
         table = (small, small_their)[half]
         if half == 1:
-            until(BOUNDS[0][1] + 3 * RELAY)
+            until(BOUNDS[0][1] + HOPS[2])
             if fast:
                 swap.wait()
 
@@ -813,7 +810,7 @@
         put_probs(SEGS - 1).wait()
 
         if half == 1:
-            until(BOUNDS[1][1] + 3 * RELAY)
+            until(BOUNDS[1][1] + HOPS[2])
         out = (own_out, their_out)[half]
 
         @pl.loop(0, 3)
@@ -850,7 +847,7 @@
             return pltpu.make_async_copy(slopes.at[lax.rem(c, 2)], slope_h.at[:, span], slope_sem.at[lax.rem(c, 2)])
 
         if half == 1:
-            until(BOUNDS[2][1] + 3 * RELAY)
+            until(BOUNDS[2][1] + HOPS[2])
             put_acted.wait()
             put_slope(4).wait()
             put_slope(5).wait()
@@ -882,7 +879,7 @@
                 ticks(n, GATHER[4], 3)
 
         else:
-            until((BOUNDS[3][0] + BOUNDS[3][1]) // 2 + 3 * RELAY)
+            until((BOUNDS[3][0] + BOUNDS[3][1]) // 2 + HOPS[2])
 
             @pl.loop(0, 3)
             def _(n, down=down, acc=acc):
@@ -891,7 +888,7 @@
                 ticks(n, 1, 3)
 
             done[0] += 3
-            until(BOUNDS[3][1] + 3 * RELAY)
+            until(BOUNDS[3][1] + HOPS[2])
             if fast:
                 for copy in put_theirs:
                     copy.start()
@@ -1111,21 +1108,13 @@
     load_acted(0).start()
     start(load_chunk(0, 0))
     load_hidden.start()
-    load_two.start()
-    load_normed.start()
-    load_mixed.start()
-    start(load_out)
-    start(load_w)
-    load_tokens.start()
-    load_qkv[0].start()
-    load_probs(0, 0).start()
 
     def finish(block):
         pass
 
     if fast:
         tick = make_tick(pos, grads, *wires, COUNT, finish)
-        last = COUNT + 7 * SPREAD
+        last = COUNT + AFTER[7]
     else:
 
         def tick(step):
@@ -1157,6 +1146,11 @@
         def _():
             load_acted(c + 1).start()
 
+        @pl.when(c == 3)
+        def _():
+            load_two.start()
+            load_normed.start()
+
         for part in range(2):
             piece = t_mm(a_buf[lax.rem(c, 2)], d_low[:, part * width : (part + 1) * width])
             for j in range(3):
@@ -1183,6 +1177,10 @@
                 @pl.when(c == 5)
                 def _():
                     start(load_chunk(1, 0))
+                    load_mixed.start()
+                    start(load_out)
+                    load_qkv[0].start()
+                    load_probs(0, 0).start()
 
             each = TICKS[1 + half]
             d_inner[...] = (mm_t(d_low[...], down_buf[slot]) * slope_buf[slot].astype(F32)).astype(BF)
@@ -1205,6 +1203,9 @@
 
         done[0] += 6 * TICKS[1 + half]
 
+    start(load_w)
+    load_tokens.start()
+
     load_two.wait()
     load_normed.wait()
     def norm_one(span):
@@ -1248,8 +1249,6 @@
 
     done[0] += 2 * TICKS[3]
 
-    wait(load_w)
-    load_tokens.wait()
     pairs = width // PAIR
     dka, dva = acc_their.at[:, pl.ds(0, width)], acc_their.at[:, pl.ds(width, width)]
     for half in range(2):
@@ -1299,6 +1298,8 @@
         d_qkv[1] = ((dka[...] + spread(select_t[...], dkm[...])) * HD ** (-0.5)).astype(BF)
         d_qkv[2] = (dva[...] + spread(select_t[...], dvm[...])).astype(BF)
         if half == 0:
+            wait(load_w)
+            load_tokens.wait()
 
             @pl.loop(0, 3)
             def _(c):
@@ -1388,8 +1389,10 @@
     )(select_t, memory, inverse, gain, vec_in, *arrays)
 
 
-def results_kernel(blocks, grad_tokens, output, g_qkv, g_out, g_up, g_down, tokens_h, output_out, *rest):
-    vectors, (sems, out_sem) = rest[:8], rest[8:]
+def results_kernel(blocks, grad_tokens, output_h, g_qkv, g_out, g_up, g_down, tokens_h, output_out, *rest):
+    vectors, (output, sems, out_sem) = rest[:8], rest[8:]
+    load = pltpu.make_async_copy(output_h, output, out_sem.at[2])
+    load.start()
     places = [(g_down, BR * (i // 6), BC * (i % 6)) for i in range(24)]
     places += [(g_up, BR * (i // 2 % 2), CHUNK * (i // 4) + BC * (i % 2)) for i in range(24)]
     places += [(g_out, 0, BC * i) for i in range(6)]
@@ -1399,8 +1402,11 @@
         for i, (target, row, column) in enumerate(places)
     ]
     copies.append(pltpu.make_async_copy(grad_tokens, tokens_h, out_sem.at[0]))
+    for copy in copies[:24]:
+        copy.start()
+    load.wait()
     copies.append(pltpu.make_async_copy(output, output_out, out_sem.at[1]))
-    for copy in copies:
+    for copy in copies[24:]:
         copy.start()
     bias_qv, *flat = vectors
     for j in range(6):
@@ -1420,20 +1426,20 @@
     sd = jax.ShapeDtypeStruct
     rows, depth = output.shape
     if fast:
-        blocks, grad_tokens, output = (
-            pltpu.with_memory_space_constraint(a, pltpu.VMEM) for a in (blocks, grad_tokens, output)
-        )
+        blocks, grad_tokens = (pltpu.with_memory_space_constraint(a, pltpu.VMEM) for a in (blocks, grad_tokens))
+        output = pltpu.with_memory_space_constraint(output, pltpu.HBM)
     large = [sd((3 * depth, width), F32), sd((width, depth), F32), sd((depth, units), F32), sd((units, depth), F32)]
     large += [sd((rows, depth), BF)] * 2
     small = [sd((2, width), F32), sd((units,), F32)] + [sd((depth,), F32)] * 6
     return pl.pallas_call(
         results_kernel,
         out_shape=large + small,
-        in_specs=[vm, vm, vm],
+        in_specs=[vm, vm, hbm],
         out_specs=[hbm] * 6 + [vm] * len(small),
         scratch_shapes=[
+            pltpu.VMEM((rows, depth), BF),
             pltpu.SemaphoreType.DMA((VEC,)),
-            pltpu.SemaphoreType.DMA((2,)),
+            pltpu.SemaphoreType.DMA((3,)),
         ],
         compiler_params=pltpu.CompilerParams(vmem_limit_bytes=(8 if fast else 40) * 2**20),
         name="results",

time: 250 us -> 245 us (0.980)
  Pallas kernels: 248 us -> 244 us
    pallas_call x1, Pallas kernels: 90.1 us -> 87.2 us  [forward(): pl.pallas_call(functools.partial(forward_kernel, fast), out_shape=out_sha...]
    pallas_call x1, Pallas kernels: 150 us -> 148 us  [backward(): pl.pallas_call(functools.partial(backward_kernel, fast), out_shape=[kept(...]
where the time goes in v8:
time: 245 us
  Pallas kernels  244 us (100%)
    pallas_call x1, Pallas kernels, backward(): pl.pallas_call(functools.partial(backward_kernel, fast), out_shape=[kept(...  148 us
    pallas_call x1, Pallas kernels, forward(): pl.pallas_call(functools.partial(forward_kernel, fast), out_shape=out_sha...  87.2 us
    pallas_call x1, Pallas kernels, results(): pl.pallas_call(results_kernel, out_shape=large + small, in_specs=[vm, vm,...  8.89 us

profile of v8, /device:TPU:0, one launch (start us, length us, event | category | flops | bytes accessed | tf_op | source)
XLA Modules:
  0.0 244.6 jit_solution(16753076015832918368)
XLA Ops:
  0.6 87.2 %forward.1 = (bf16[1184,768]{1,0:T(8,128)(2,1)}, bf16[2304,384]{1,0:T(8,128)(2,1)}, bf16[384,768]{1,0:T(8,128)(2,1)}, bf16[768,1536]{1,0:T(8,128)(2,1)}, bf16[15...) custom-call(s32[8]{0:T(128)} %parent.1, ...), custom_call_target="tpu_custom_call" | custom-call | tf_op jit(solution)/shard_map/forward/pallas_call | solution.py:968
  87.9 147.6 %backward.1 = (f32[73,384,128]{2,1,0:T(8,128)S(1)}, bf16[1184,768]{1,0:T(8,128)(2,1)S(1)}) custom-call(bf16[1184,96]{1,0:T(8,128)(2,1)} %get-tuple-element.49.select_t, bf16[2,2,96,384]{3,2,1,0:T(8,128)(2,1)} %get-tuple-element.50.memory, f32[1184,1]{1,0:T(8,128)} %get-tuple-element.51.inverse, f32[768]{0:T(1024)} %gain.1, ...), custom_call_target="tpu_custom_call" | custom-call | tf_op jit(solution)/shard_map/backward/pallas_call | solution.py:1353
  235.5 8.9 %results.1 = (f32[2304,384]{1,0:T(8,128)}, f32[384,768]{1,0:T(8,128)}, f32[768,1536]{1,0:T(8,128)}, f32[1536,768]{1,0:T(8,128)}, bf16[1184,768]{1,0:T(8,128)(2,1...) custom-call(f32[73,384,128]{2,1,0:T(8,128)S(1)} %get-tuple-element.6, ...), custom_call_target="tpu_custom_call" | custom-call | tf_op jit(solution)/shard_map/results/pallas_call | solution.py:1434

commit v9 on v8

--- a/solution.py
+++ b/solution.py
@@ -644,7 +644,7 @@
         slope_own_h,
         slope_their_h,
         d_two_h,
-        d_ffn_h,
+        d_ffn,
         vec,
         probs_h,
         select_t,
@@ -695,7 +695,7 @@
     put_normed = move(4, normed, normed_h)
     put_hidden = move(5, hidden, hidden_h)
     put_acted = move(6, acted, acted_h)
-    late = ((acc_own, d_two_h), (hidden, d_ffn_h), (tokens, output_h))
+    late = ((acc_own, d_two_h), (tokens, output_h))
     put_late = [
         [move(7 + 3 * part + i, ref.at[rows_of], target.at[rows_of]) for i, (ref, target) in enumerate(late)]
         for part, rows_of in enumerate((pl.ds(0, SPLIT), pl.ds(SPLIT, rows - SPLIT)))
@@ -848,6 +848,9 @@
 
         if half == 1:
             until(BOUNDS[2][1] + HOPS[2])
+            if fast:
+                for copy in put_theirs[:3]:
+                    copy.start()
             put_acted.wait()
             put_slope(4).wait()
             put_slope(5).wait()
@@ -890,8 +893,7 @@
             done[0] += 3
             until(BOUNDS[3][1] + HOPS[2])
             if fast:
-                for copy in put_theirs:
-                    copy.start()
+                put_theirs[3].start()
 
             @pl.loop(0, 3)
             def _(n, down=down, acc=acc):
@@ -903,7 +905,6 @@
     put_slope(5).wait()
 
     load_grad.wait()
-    put_hidden.wait()
     sums[...] = jnp.zeros(sums.shape, F32)
 
     def norm_two(span):
@@ -915,7 +916,7 @@
         back = norm_back(grad, unit, scale, flat_row(gain_two, 0, depth))
         acc_own[span, :] = back
         low = back.astype(BF)
-        hidden[span, :] = low
+        d_ffn[span, :] = low
         for index, value in enumerate((low.astype(F32), grad * unit, grad)):
             sums[index] = sums[index] + value.reshape(-1, 8, depth).sum(axis=0)
 
@@ -929,7 +930,7 @@
         total = jnp.sum(sums[index], axis=0, keepdims=True)
         for j in range(6):
             vec[6 * index + j : 6 * index + j + 1, :] = total[:, BC * j : BC * (j + 1)]
-    for copy in (put_qkv, put_mixed, put_normed, *put_late[0], *put_late[1]):
+    for copy in (put_qkv, put_mixed, put_normed, put_hidden, *put_late[0], *put_late[1]):
         copy.wait()
     if fast:
         for copy in put_theirs:
@@ -947,6 +948,7 @@
     hbm = pl.BlockSpec(memory_space=pl.ANY)
     sm = pl.BlockSpec(memory_space=pltpu.SMEM)
     sd = jax.ShapeDtypeStruct
+    kept = pltpu.VMEM if fast else sd
     out_shape = [
         sd((rows, depth), BF),
         *[sd(w.shape, BF) for w in own],
@@ -959,7 +961,7 @@
         sd((rows, units), BF),
         sd((rows, units), BF),
         sd((rows, depth), F32),
-        sd((rows, depth), BF),
+        kept((rows, depth), BF),
         sd((18, BC), F32),
         sd((2, SEGS, width // PAIR, 2 * WIN, WIN + MEMP), BF),
         sd((rows, MEMP), BF),
@@ -969,7 +971,7 @@
         functools.partial(forward_kernel, fast),
         out_shape=out_shape,
         in_specs=[sm, sm] + [vm] * len(vectors) + [hbm, hbm] + [hbm] * (4 + len(given)),
-        out_specs=[hbm] * 8 + [vm] + [hbm] * 6 + [vm, hbm, vm, vm],
+        out_specs=[hbm] * 8 + [vm] + [hbm] * 5 + [vm, vm, hbm, vm, vm],
         scratch_shapes=[
             pltpu.VMEM((rows, depth), BF),
             *[pltpu.VMEM(w.shape, BF) for w in own],
@@ -994,7 +996,7 @@
         ]
         + ([pltpu.SemaphoreType.DMA((2,))] + gather_scratch() if fast else []),
         compiler_params=pltpu.CompilerParams(
-            collective_id=0 if fast else None, has_side_effects=fast, vmem_limit_bytes=67043328
+            collective_id=0 if fast else None, has_side_effects=fast, vmem_limit_bytes=62000000 if fast else 67043328
         ),
         name="forward",
     )(parent, slots, *vectors, tokens, grad_out, *own, *given)
@@ -1015,7 +1017,7 @@
     vec_in,
     tokens_h,
     hidden_h,
-    d_ffn_h,
+    d_ffn,
     d_two_h,
     normed_h,
     acted_h,
@@ -1045,7 +1047,6 @@
     down_buf,
     d_inner,
     sums,
-    tokens,
     mixed,
     w_out,
     w_qkv,
@@ -1060,13 +1061,13 @@
     probs_sem,
     *wires,
 ):
-    rows, depth = tokens.shape
+    rows, depth = hidden.shape
     width = mixed.shape[1]
+    tokens = hidden
 
     def fetch(index, source, target):
         return pltpu.make_async_copy(source, target, load_sem.at[index])
 
-    load_d = fetch(0, d_ffn_h, d_low)
     load_hidden = fetch(1, hidden_h, hidden)
     load_two = fetch(2, d_two_h, d_res)
     load_normed = fetch(3, normed_h, normed)
@@ -1104,7 +1105,6 @@
     if fast:
         pos = Place()
         sum_greet(pos)
-    load_d.start()
     load_acted(0).start()
     start(load_chunk(0, 0))
     load_hidden.start()
@@ -1136,7 +1136,6 @@
     if fast:
         sum_met(pos)
 
-    load_d.wait()
 
     @pl.loop(0, 4)
     def _(c):
@@ -1152,10 +1151,11 @@
             load_normed.start()
 
         for part in range(2):
-            piece = t_mm(a_buf[lax.rem(c, 2)], d_low[:, part * width : (part + 1) * width])
+            piece = t_mm(a_buf[lax.rem(c, 2)], d_ffn[:, part * width : (part + 1) * width])
             for j in range(3):
                 grads[DOWN + 6 * c + 3 * part + j] = piece[:, BC * j : BC * (j + 1)]
-        ticks(c, TICKS[0], 4)
+            if part >= 2 - TICKS[0]:
+                tick(done[0] + c * TICKS[0] + part - 2 + TICKS[0])
 
     done[0] += 4 * TICKS[0]
 
@@ -1183,7 +1183,7 @@
                     load_probs(0, 0).start()
 
             each = TICKS[1 + half]
-            d_inner[...] = (mm_t(d_low[...], down_buf[slot]) * slope_buf[slot].astype(F32)).astype(BF)
+            d_inner[...] = (mm_t(d_ffn[...], down_buf[slot]) * slope_buf[slot].astype(F32)).astype(BF)
             if each > 1:
                 tick(done[0] + c * each)
             if half == 0:
@@ -1349,11 +1349,14 @@
     width = mixed.shape[1]
     vm = pl.BlockSpec(memory_space=pltpu.VMEM)
     hbm = pl.BlockSpec(memory_space=pl.ANY)
+    if fast:
+        kept_in = pltpu.with_memory_space_constraint(arrays[2], pltpu.VMEM)
+        arrays = (*arrays[:2], kept_in, *arrays[3:])
     kept = pltpu.VMEM if fast else jax.ShapeDtypeStruct
     return pl.pallas_call(
         functools.partial(backward_kernel, fast),
         out_shape=[kept((COUNT, BR, BC), F32), kept((rows, depth), BF)],
-        in_specs=[vm, vm, vm, vm, vm] + [hbm] * len(arrays),
+        in_specs=[vm, vm, vm, vm, vm, hbm, hbm, vm] + [hbm] * (len(arrays) - 3),
         out_specs=[vm, vm],
         scratch_shapes=[
             pltpu.VMEM((rows, depth), BF),
@@ -1367,7 +1370,6 @@
             pltpu.VMEM((2, CHUNK, depth), BF),
             pltpu.VMEM((rows, CHUNK), BF),
             pltpu.VMEM((3, 8, depth), F32),
-            pltpu.VMEM((rows, depth), BF),
             pltpu.VMEM((rows, width), BF),
             pltpu.VMEM((2, width, depth), BF),
             pltpu.VMEM((2, 3 * depth, width), BF),
@@ -1383,16 +1385,14 @@
         ]
         + (sum_scratch() if fast else []),
         compiler_params=pltpu.CompilerParams(
-            collective_id=1 if fast else None, has_side_effects=fast, vmem_limit_bytes=47 * 2**20 if fast else 67043328
+            collective_id=1 if fast else None, has_side_effects=fast, vmem_limit_bytes=45100000 if fast else 67043328
         ),
         name="backward",
     )(select_t, memory, inverse, gain, vec_in, *arrays)
 
 
-def results_kernel(blocks, grad_tokens, output_h, g_qkv, g_out, g_up, g_down, tokens_h, output_out, *rest):
-    vectors, (output, sems, out_sem) = rest[:8], rest[8:]
-    load = pltpu.make_async_copy(output_h, output, out_sem.at[2])
-    load.start()
+def results_kernel(blocks, grad_tokens, output, g_qkv, g_out, g_up, g_down, tokens_h, output_out, *rest):
+    vectors, (sems, out_sem) = rest[:8], rest[8:]
     places = [(g_down, BR * (i // 6), BC * (i % 6)) for i in range(24)]
     places += [(g_up, BR * (i // 2 % 2), CHUNK * (i // 4) + BC * (i % 2)) for i in range(24)]
     places += [(g_out, 0, BC * i) for i in range(6)]
@@ -1402,11 +1402,8 @@
         for i, (target, row, column) in enumerate(places)
     ]
     copies.append(pltpu.make_async_copy(grad_tokens, tokens_h, out_sem.at[0]))
-    for copy in copies[:24]:
-        copy.start()
-    load.wait()
     copies.append(pltpu.make_async_copy(output, output_out, out_sem.at[1]))
-    for copy in copies[24:]:
+    for copy in copies:
         copy.start()
     bias_qv, *flat = vectors
     for j in range(6):
@@ -1426,20 +1423,20 @@
     sd = jax.ShapeDtypeStruct
     rows, depth = output.shape
     if fast:
-        blocks, grad_tokens = (pltpu.with_memory_space_constraint(a, pltpu.VMEM) for a in (blocks, grad_tokens))
-        output = pltpu.with_memory_space_constraint(output, pltpu.HBM)
+        blocks, grad_tokens, output = (
+            pltpu.with_memory_space_constraint(a, pltpu.VMEM) for a in (blocks, grad_tokens, output)
+        )
     large = [sd((3 * depth, width), F32), sd((width, depth), F32), sd((depth, units), F32), sd((units, depth), F32)]
     large += [sd((rows, depth), BF)] * 2
     small = [sd((2, width), F32), sd((units,), F32)] + [sd((depth,), F32)] * 6
     return pl.pallas_call(
         results_kernel,
         out_shape=large + small,
-        in_specs=[vm, vm, hbm],
+        in_specs=[vm, vm, vm],
         out_specs=[hbm] * 6 + [vm] * len(small),
         scratch_shapes=[
-            pltpu.VMEM((rows, depth), BF),
             pltpu.SemaphoreType.DMA((VEC,)),
-            pltpu.SemaphoreType.DMA((3,)),
+            pltpu.SemaphoreType.DMA((2,)),
         ],
         compiler_params=pltpu.CompilerParams(vmem_limit_bytes=(8 if fast else 40) * 2**20),
         name="results",

time: 245 us -> 242 us (0.988)
  Pallas kernels: 244 us -> 241 us
where the time goes in v9:
time: 242 us
  Pallas kernels  241 us (100%)
    pallas_call x1, Pallas kernels, backward(): pl.pallas_call(functools.partial(backward_kernel, fast), out_shape=[kept(...  147 us
    pallas_call x1, Pallas kernels, forward(): pl.pallas_call(functools.partial(forward_kernel, fast), out_shape=out_sha...  87.1 us
    pallas_call x1, Pallas kernels, results(): pl.pallas_call(results_kernel, out_shape=large + small, in_specs=[vm, vm,...  7.41 us

profile of v9, /device:TPU:0, one launch (start us, length us, event | category | flops | bytes accessed | tf_op | source)
XLA Modules:
  0.0 242.2 jit_solution(8719849754234784689)
XLA Ops:
  0.6 87.1 %forward.1 = (bf16[1184,768]{1,0:T(8,128)(2,1)}, bf16[2304,384]{1,0:T(8,128)(2,1)}, bf16[384,768]{1,0:T(8,128)(2,1)}, bf16[768,1536]{1,0:T(8,128)(2,1)}, bf16[15...) custom-call(s32[8]{0:T(128)} %parent.1, ...), custom_call_target="tpu_custom_call" | custom-call | tf_op jit(solution)/shard_map/forward/pallas_call | solution.py:970
  87.7 0.0 copy-start
  87.7 146.9 %backward.1 = (f32[73,384,128]{2,1,0:T(8,128)S(1)}, bf16[1184,768]{1,0:T(8,128)(2,1)S(1)}) custom-call(bf16[1184,96]{1,0:T(8,128)(2,1)} %get-tuple-element.49.select_t, bf16[2,2,96,384]{3,2,1,0:T(8,128)(2,1)} %get-tuple-element.50.memory, f32[1184,1]{1,0:T(8,128)} %get-tuple-element.51.inverse, f32[768]{0:T(1024)} %gain.1, ...), custom_call_target="tpu_custom_call" | custom-call | tf_op jit(solution)/shard_map/backward/pallas_call | solution.py:1356
  234.6 0.0 copy-done
  234.6 7.4 %results.1 = (f32[2304,384]{1,0:T(8,128)}, f32[384,768]{1,0:T(8,128)}, f32[768,1536]{1,0:T(8,128)}, f32[1536,768]{1,0:T(8,128)}, bf16[1184,768]{1,0:T(8,128)(2,1...) custom-call(f32[73,384,128]{2,1,0:T(8,128)S(1)} %get-tuple-element.6, ...), custom_call_target="tpu_custom_call" | custom-call | tf_op jit(solution)/shard_map/results/pallas_call | solution.py:1432
Async XLA Ops:
  87.7 146.9 %copy-start = (bf16[1184,768]{1,0:T(8,128)(2,1)S(1)}, bf16[1184,768]{1,0:T(8,128)(2,1)}, u32[]{:S(2)}) copy-start(bf16[1184,768]{1,0:T(8,128)(2,1)} %get-tuple-element.69.output) | copy-start | bytes 5455876

commit v10 on v9

--- a/solution.py
+++ b/solution.py
@@ -1336,7 +1336,7 @@
         tick(step)
 
 
-TICKS = (1, 3, 2, 1, 2, 1, 3, 1)
+TICKS = (2, 3, 1, 1, 2, 1, 2, 2)
 TICK_TILES = 2
 NORM_TILE = 128
 UNROLL = (3, 1)

time: 242 us -> 242 us (level)
  no operation moved by 1% of the time
where the time goes in v10:
time: 242 us
  Pallas kernels  241 us (100%)
    pallas_call x1, Pallas kernels, backward(): pl.pallas_call(functools.partial(backward_kernel, fast), out_shape=[kept(...  146 us
    pallas_call x1, Pallas kernels, forward(): pl.pallas_call(functools.partial(forward_kernel, fast), out_shape=out_sha...  87.1 us
    pallas_call x1, Pallas kernels, results(): pl.pallas_call(results_kernel, out_shape=large + small, in_specs=[vm, vm,...  7.41 us

profile of v10, /device:TPU:0, one launch (start us, length us, event | category | flops | bytes accessed | tf_op | source)
XLA Modules:
  0.0 241.7 jit_solution(4898573925815158238)
XLA Ops:
  0.6 87.1 %forward.1 = (bf16[1184,768]{1,0:T(8,128)(2,1)}, bf16[2304,384]{1,0:T(8,128)(2,1)}, bf16[384,768]{1,0:T(8,128)(2,1)}, bf16[768,1536]{1,0:T(8,128)(2,1)}, bf16[15...) custom-call(s32[8]{0:T(128)} %parent.1, ...), custom_call_target="tpu_custom_call" | custom-call | tf_op jit(solution)/shard_map/forward/pallas_call | solution.py:970
  87.7 0.0 copy-start
  87.7 146.4 %backward.1 = (f32[73,384,128]{2,1,0:T(8,128)S(1)}, bf16[1184,768]{1,0:T(8,128)(2,1)S(1)}) custom-call(bf16[1184,96]{1,0:T(8,128)(2,1)} %get-tuple-element.49.select_t, bf16[2,2,96,384]{3,2,1,0:T(8,128)(2,1)} %get-tuple-element.50.memory, f32[1184,1]{1,0:T(8,128)} %get-tuple-element.51.inverse, f32[768]{0:T(1024)} %gain.1, ...), custom_call_target="tpu_custom_call" | custom-call | tf_op jit(solution)/shard_map/backward/pallas_call | solution.py:1356
  234.1 0.0 copy-done
  234.1 7.4 %results.1 = (f32[2304,384]{1,0:T(8,128)}, f32[384,768]{1,0:T(8,128)}, f32[768,1536]{1,0:T(8,128)}, f32[1536,768]{1,0:T(8,128)}, bf16[1184,768]{1,0:T(8,128)(2,1...) custom-call(f32[73,384,128]{2,1,0:T(8,128)S(1)} %get-tuple-element.6, ...), custom_call_target="tpu_custom_call" | custom-call | tf_op jit(solution)/shard_map/results/pallas_call | solution.py:1432
Async XLA Ops:
  87.7 146.4 %copy-start = (bf16[1184,768]{1,0:T(8,128)(2,1)S(1)}, bf16[1184,768]{1,0:T(8,128)(2,1)}, u32[]{:S(2)}) copy-start(bf16[1184,768]{1,0:T(8,128)(2,1)} %get-tuple-element.69.output) | copy-start | bytes 5455876
